TPU v7x, 32 devices: a whole 2x2x4 slice. The times are simulated.
32 devices in a mesh: dp: 8 (over y, x, core), seq: 4 (over z).
Axes of the slice: x: 2, y: 2, z: 4, core: 2. Of those that a mesh axis runs over, the one named last changes fastest.
Arguments:
- tokens: bfloat16 [16, 512, 2048], P('dp', 'seq'), may hold values from -6 to 6
- cotangent: bfloat16 [16, 512, 2048], P('dp', 'seq'), may hold values from -6 to 6
- attention_base: bfloat16 [4, 2048, 2048], P(None, ('dp', 'seq')), may hold values from -0.125 to 0.125
- expand_base: bfloat16 [2, 2048, 5632], P(None, ('dp', 'seq')), may hold values from -0.125 to 0.125
- contract_base: bfloat16 [5632, 2048], P(None, ('dp', 'seq')), may hold values from -0.078125 to 0.078125
- attention_down: float32 [4, 2048, 16], replicated, may hold values from -0.125 to 0.125
- attention_up: float32 [4, 16, 2048], replicated, may hold values from -0.15 to 0.15
- attention_magnitude: float32 [4, 2048], replicated, may hold values from 0.5 to 24
- expand_down: float32 [2, 2048, 16], replicated, may hold values from -0.125 to 0.125
- expand_up: float32 [2, 16, 5632], replicated, may hold values from -0.15 to 0.15
- expand_magnitude: float32 [2, 5632], replicated, may hold values from 0.5 to 1.5
- contract_down: float32 [5632, 16], replicated, may hold values from -0.078125 to 0.078125
- contract_up: float32 [16, 2048], replicated, may hold values from -0.15 to 0.15
- contract_magnitude: float32 [2048], replicated, may hold values from 0.5 to 1.5
- prompt_length: int32 [16], P('dp'), may hold values from 64 to 256, as said below
- response_length: int32 [16], P('dp'), may hold values from 128 to 256
Outputs:
- layer_output: bfloat16 [16, 512, 2048], P('dp', 'seq')
- tokens_grad: float32 [16, 512, 2048], P('dp', 'seq')
- attention_down_grad: float32 [4, 2048, 16], replicated
- attention_up_grad: float32 [4, 16, 2048], replicated
- attention_magnitude_grad: float32 [4, 2048], replicated
- expand_down_grad: float32 [2, 2048, 16], replicated
- expand_up_grad: float32 [2, 16, 5632], replicated
- expand_magnitude_grad: float32 [2, 5632], replicated
- contract_down_grad: float32 [5632, 16], replicated
- contract_up_grad: float32 [16, 2048], replicated
- contract_magnitude_grad: float32 [2048], replicated
Inputs may be any that keep to these rules, and one draw needn't show every extreme that they name: `prompt_length`: rows 2i and 2i+1 form a pair with the same prompt length.
All inputs are finite; a program needn't handle non-finite values.
Results may differ from a plain program's by a relative error of at most 0.025.
Values may be sent and summed in bfloat16 or wider, within the bound.
No kernel may reach another device: no remote copies, remote signals or barrier semaphores. Data moves between devices by JAX's collectives and lax.ppermute only.
A program may use at most 320 MiB of HBM per device.

v0:
```python
import jax
import jax.numpy as jnp
from jax import lax
from jax.sharding import PartitionSpec as P

HEADS = 16
HEAD_DIM = 128


adapter_scale = 2.0
highest_precision = lax.Precision.HIGHEST


def rms_norm(values):
    return values * lax.rsqrt(jnp.mean(values * values, axis=-1, keepdims=True) + 1e-05)


def rotary(values, positions):
    head_half = HEAD_DIM // 2
    frequency = 10000.0 ** (-jnp.arange(head_half).astype(jnp.float32) / head_half)
    angles = positions[:, None] * frequency[None, :]
    cosine = jnp.cos(angles)[None, :, None, :]
    sine = jnp.sin(angles)[None, :, None, :]
    shaped = values.reshape(values.shape[0], values.shape[1], HEADS, 2, head_half)
    former = shaped[:, :, :, 0]
    latter = shaped[:, :, :, 1]
    turned = jnp.stack([former * cosine - latter * sine, latter * cosine + former * sine], axis=3)
    return turned.reshape(values.shape)


def silu_product(gate_value, up_value):
    return gate_value / (1.0 + jnp.exp(-gate_value)) * up_value


def prepare_weights(frozen_weight, adapter_down_weight, adapter_up_weight):
    squares = jnp.einsum(
        "io,io->o", frozen_weight, frozen_weight, preferred_element_type=jnp.float32
    )
    cross_product_term = jnp.dot(
        adapter_down_weight.T,
        frozen_weight,
        precision=highest_precision,
        preferred_element_type=jnp.float32,
    )
    gram_product = jnp.dot(adapter_down_weight.T, adapter_down_weight, precision=highest_precision)
    raised_to_float = jnp.dot(gram_product, adapter_up_weight, precision=highest_precision)
    per_column_norm = jnp.sqrt(
        squares
        + 2.0 * adapter_scale * jnp.sum(adapter_up_weight * cross_product_term, axis=0)
        + adapter_scale * adapter_scale * jnp.sum(adapter_up_weight * raised_to_float, axis=0)
    )
    return (per_column_norm, cross_product_term, gram_product)


def apply_projection(
    input_rows,
    frozen_weight,
    adapter_down_weight,
    adapter_up_weight,
    magnitude_vector,
    per_column_norm,
):
    frozen_product = jnp.dot(input_rows, frozen_weight, preferred_element_type=jnp.float32)
    cast_to_bfloat = jnp.dot(
        input_rows,
        adapter_down_weight,
        precision=highest_precision,
        preferred_element_type=jnp.float32,
    )
    direction_matrix = frozen_product + adapter_scale * jnp.dot(
        cast_to_bfloat, adapter_up_weight, precision=highest_precision
    )
    return (
        direction_matrix * (magnitude_vector / per_column_norm),
        direction_matrix,
        cast_to_bfloat,
    )


def project_back(
    output_gradient,
    input_rows,
    saved_residual_triple,
    frozen_weight,
    adapter_down_weight,
    adapter_up_weight,
    magnitude_vector,
    prepared_weight_triple,
):
    direction_matrix = saved_residual_triple[1]
    cast_to_bfloat = saved_residual_triple[2]
    per_column_norm, cross_product_term, gram_product = prepared_weight_triple
    scaling = magnitude_vector / per_column_norm
    grad_magnitude = jnp.sum(output_gradient * direction_matrix, axis=0) / per_column_norm
    direction_gradient = output_gradient * scaling
    normalizer_weight = -magnitude_vector * grad_magnitude / (per_column_norm * per_column_norm)
    restored_from_low = jnp.dot(
        direction_gradient, adapter_up_weight.T, precision=highest_precision
    )
    grad_inputs = jnp.einsum(
        "to,io->ti",
        direction_gradient.astype(jnp.bfloat16),
        frozen_weight,
        preferred_element_type=jnp.float32,
    ) + adapter_scale * jnp.dot(
        restored_from_low, adapter_down_weight.T, precision=highest_precision
    )
    scaled_up_weight = adapter_up_weight * normalizer_weight[None, :]
    grad_down = (
        adapter_scale
        * jnp.dot(
            input_rows.T,
            restored_from_low,
            precision=highest_precision,
            preferred_element_type=jnp.float32,
        )
        + adapter_scale
        * jnp.dot(
            frozen_weight,
            scaled_up_weight.T,
            precision=highest_precision,
            preferred_element_type=jnp.float32,
        )
        + adapter_scale
        * adapter_scale
        * jnp.dot(
            adapter_down_weight,
            jnp.dot(adapter_up_weight, scaled_up_weight.T, precision=highest_precision),
            precision=highest_precision,
        )
    )
    grad_up = (
        adapter_scale * jnp.dot(cast_to_bfloat.T, direction_gradient, precision=highest_precision)
        + adapter_scale * cross_product_term * normalizer_weight[None, :]
        + adapter_scale
        * adapter_scale
        * jnp.dot(gram_product, scaled_up_weight, precision=highest_precision)
    )
    return (grad_inputs, grad_down, grad_up, grad_magnitude)


def masked_scores(query_heads, key_heads, allowed):
    raw_scores = jnp.einsum(
        "qhd,khd->hqk", query_heads, key_heads, preferred_element_type=jnp.float32
    )
    return jnp.where(allowed[None], raw_scores * HEAD_DIM ** (-0.5), -1e30)


def attend_forward(row_data):
    query_heads, key_heads, value_heads, allowed = row_data
    scores = masked_scores(query_heads, key_heads, allowed)
    row_peak = jnp.max(scores, axis=-1, keepdims=True)
    unnormed = jnp.exp(scores - row_peak)
    total_weight = jnp.sum(unnormed, axis=-1, keepdims=True)
    shares = (unnormed / total_weight).astype(jnp.bfloat16)
    log_total = (row_peak + jnp.log(total_weight))[..., 0]
    attended = jnp.einsum("hqk,khd->qhd", shares, value_heads, preferred_element_type=jnp.float32)
    return (attended, log_total)


def attend_local_back(row_data):
    query_heads, key_heads, value_heads, grad_heads, allowed, log_total = row_data
    scores = masked_scores(query_heads, key_heads, allowed)
    share_float = jnp.exp(scores - log_total[..., None])
    grad_shares = jnp.einsum(
        "qhd,khd->hqk", grad_heads, value_heads, preferred_element_type=jnp.float32
    )
    row_stat = jnp.sum(share_float * grad_shares, axis=-1)
    grad_raw = (share_float * (grad_shares - row_stat[..., None]) * HEAD_DIM ** (-0.5)).astype(
        jnp.bfloat16
    )
    grad_queries = jnp.einsum(
        "hqk,khd->qhd", grad_raw, key_heads, preferred_element_type=jnp.float32
    )
    return (grad_queries, grad_raw, share_float.astype(jnp.bfloat16), row_stat)


def attend_owner_back(row_data):
    query_all, grad_all, log_all, stat_all, key_own, value_own, allowed_own = row_data
    scores = masked_scores(query_all, key_own, allowed_own)
    share_float = jnp.exp(scores - log_all[..., None])
    grad_values = jnp.einsum(
        "hqk,qhd->khd",
        share_float.astype(jnp.bfloat16),
        grad_all,
        preferred_element_type=jnp.float32,
    )
    grad_shares = jnp.einsum(
        "qhd,khd->hqk", grad_all, value_own, preferred_element_type=jnp.float32
    )
    grad_raw = (share_float * (grad_shares - stat_all[..., None]) * HEAD_DIM ** (-0.5)).astype(
        jnp.bfloat16
    )
    grad_keys = jnp.einsum("hqk,qhd->khd", grad_raw, query_all, preferred_element_type=jnp.float32)
    return (grad_keys, grad_values)


def body(
    tokens,
    cotangent,
    attention_base,
    expand_base,
    contract_base,
    attention_down,
    attention_up,
    attention_magnitude,
    expand_down,
    expand_up,
    expand_magnitude,
    contract_down,
    contract_up,
    contract_magnitude,
    prompt_length,
    response_length,
):
    row_count, group_rows, width = tokens.shape
    token_count = row_count * group_rows
    seq_place = lax.axis_index("seq")
    full_length = group_rows * lax.axis_size("seq")
    query_place = seq_place * group_rows + jnp.arange(group_rows, dtype=jnp.int32)
    positions = query_place.astype(jnp.float32)
    key_place = jnp.arange(full_length, dtype=jnp.int32)
    totals = prompt_length + response_length
    allowed = (key_place[None, None, :] <= query_place[None, :, None]) & (
        key_place[None, None, :] < totals[:, None, None]
    )
    attention_full = lax.all_gather(attention_base, ("dp", "seq"), axis=1, tiled=True)
    expand_full, contract_full = (
        lax.all_gather(expand_base, ("dp", "seq"), axis=1, tiled=True),
        lax.all_gather(contract_base, ("dp", "seq"), axis=1, tiled=True),
    )
    prepared = [
        prepare_weights(attention_full[member], attention_down[member], attention_up[member])
        for member in range(4)
    ]
    flat_tokens = tokens.reshape(token_count, width).astype(jnp.float32)
    first_normed = rms_norm(flat_tokens).astype(jnp.bfloat16)
    projected = [
        apply_projection(
            first_normed,
            attention_full[member],
            attention_down[member],
            attention_up[member],
            attention_magnitude[member],
            prepared[member][0],
        )
        for member in range(3)
    ]
    queries = rotary(projected[0][0].reshape(row_count, group_rows, width), positions).astype(
        jnp.bfloat16
    )
    keys_local = rotary(projected[1][0].reshape(row_count, group_rows, width), positions).astype(
        jnp.bfloat16
    )
    values_local = projected[2][0].reshape(row_count, group_rows, width).astype(jnp.bfloat16)
    keys_all, values_all = (
        lax.all_gather(keys_local, "seq", axis=1, tiled=True),
        lax.all_gather(values_local, "seq", axis=1, tiled=True),
    )
    query_heads = queries.reshape(row_count, group_rows, HEADS, HEAD_DIM)
    key_heads = keys_all.reshape(row_count, full_length, HEADS, HEAD_DIM)
    value_heads = values_all.reshape(row_count, full_length, HEADS, HEAD_DIM)
    attended, log_total = lax.map(attend_forward, (query_heads, key_heads, value_heads, allowed))
    mixed_heads = attended.reshape(token_count, width).astype(jnp.bfloat16)
    output_kept = apply_projection(
        mixed_heads,
        attention_full[3],
        attention_down[3],
        attention_up[3],
        attention_magnitude[3],
        prepared[3][0],
    )
    middle = flat_tokens + output_kept[0]
    second_normed = rms_norm(middle).astype(jnp.bfloat16)
    feed_prepared = [
        prepare_weights(expand_full[member], expand_down[member], expand_up[member])
        for member in range(2)
    ]
    contract_prepared = prepare_weights(contract_full, contract_down, contract_up)
    gate_kept = apply_projection(
        second_normed,
        expand_full[0],
        expand_down[0],
        expand_up[0],
        expand_magnitude[0],
        feed_prepared[0][0],
    )
    up_kept = apply_projection(
        second_normed,
        expand_full[1],
        expand_down[1],
        expand_up[1],
        expand_magnitude[1],
        feed_prepared[1][0],
    )
    hidden = silu_product(gate_kept[0], up_kept[0]).astype(jnp.bfloat16)
    down_kept = apply_projection(
        hidden, contract_full, contract_down, contract_up, contract_magnitude, contract_prepared[0]
    )
    layer_output = (
        (middle + down_kept[0]).reshape(row_count, group_rows, width).astype(jnp.bfloat16)
    )
    expand_full, contract_full = (
        lax.all_gather(expand_base, ("dp", "seq"), axis=1, tiled=True),
        lax.all_gather(contract_base, ("dp", "seq"), axis=1, tiled=True),
    )
    grad_middle = cotangent.reshape(token_count, width).astype(jnp.float32)
    contract_back = project_back(
        grad_middle,
        hidden,
        down_kept,
        contract_full,
        contract_down,
        contract_up,
        contract_magnitude,
        contract_prepared,
    )
    silu_pullback = jax.vjp(silu_product, gate_kept[0], up_kept[0])[1]
    grad_gate, grad_up_value = silu_pullback(contract_back[0])
    gate_back = project_back(
        grad_gate,
        second_normed,
        gate_kept,
        expand_full[0],
        expand_down[0],
        expand_up[0],
        expand_magnitude[0],
        feed_prepared[0],
    )
    up_back = project_back(
        grad_up_value,
        second_normed,
        up_kept,
        expand_full[1],
        expand_down[1],
        expand_up[1],
        expand_magnitude[1],
        feed_prepared[1],
    )
    grad_second = gate_back[0] + up_back[0]
    grad_middle = grad_middle + jax.vjp(rms_norm, middle)[1](grad_second)[0]
    expand_down_grad = jnp.stack([gate_back[1], up_back[1]])
    expand_up_grad = jnp.stack([gate_back[2], up_back[2]])
    expand_magnitude_grad = jnp.stack([gate_back[3], up_back[3]])
    contract_down_grad = contract_back[1]
    contract_up_grad = contract_back[2]
    contract_magnitude_grad = contract_back[3]
    attention_full = lax.all_gather(attention_base, ("dp", "seq"), axis=1, tiled=True)
    output_back = project_back(
        grad_middle,
        mixed_heads,
        output_kept,
        attention_full[3],
        attention_down[3],
        attention_up[3],
        attention_magnitude[3],
        prepared[3],
    )
    grad_heads = output_back[0].astype(jnp.bfloat16).reshape(row_count, group_rows, HEADS, HEAD_DIM)
    grad_queries, grad_raw, share_low, row_stat = lax.map(
        attend_local_back, (query_heads, key_heads, value_heads, grad_heads, allowed, log_total)
    )
    query_all, grad_all, log_all, stat_all = (
        lax.all_gather(query_heads, "seq", axis=1, tiled=True),
        lax.all_gather(grad_heads, "seq", axis=1, tiled=True),
        lax.all_gather(log_total.astype(jnp.bfloat16), "seq", axis=2, tiled=True).astype(
            log_total.dtype
        ),
        lax.all_gather(row_stat.astype(jnp.bfloat16), "seq", axis=2, tiled=True).astype(
            row_stat.dtype
        ),
    )
    own_keys = key_heads_own = keys_local.reshape(row_count, group_rows, HEADS, HEAD_DIM)
    value_own = values_local.reshape(row_count, group_rows, HEADS, HEAD_DIM)
    allowed_own = (query_place[None, None, :] <= key_place[None, :, None]) & (
        query_place[None, None, :] < totals[:, None, None]
    )
    grad_keys_own, grad_values_own = lax.map(
        attend_owner_back,
        (query_all, grad_all, log_all, stat_all, key_heads_own, value_own, allowed_own),
    )
    grad_keys = grad_keys_own.reshape(row_count, group_rows, width)
    grad_values = grad_values_own.reshape(row_count, group_rows, width)
    grad_query_plain = rotary(
        grad_queries.reshape(row_count, group_rows, width), -positions
    ).reshape(token_count, width)
    grad_key_plain = rotary(grad_keys, -positions).reshape(token_count, width)
    grad_value_plain = grad_values.reshape(token_count, width)
    sources = [grad_query_plain, grad_key_plain, grad_value_plain]
    attention_back = [
        project_back(
            sources[member],
            first_normed,
            projected[member],
            attention_full[member],
            attention_down[member],
            attention_up[member],
            attention_magnitude[member],
            prepared[member],
        )
        for member in range(3)
    ]
    grad_first = attention_back[0][0] + attention_back[1][0] + attention_back[2][0]
    tokens_grad = grad_middle + jax.vjp(rms_norm, flat_tokens)[1](grad_first)[0]
    attention_down_grad = jnp.stack(
        [attention_back[0][1], attention_back[1][1], attention_back[2][1], output_back[1]]
    )
    attention_up_grad = jnp.stack(
        [attention_back[0][2], attention_back[1][2], attention_back[2][2], output_back[2]]
    )
    attention_magnitude_grad = jnp.stack(
        [attention_back[0][3], attention_back[1][3], attention_back[2][3], output_back[3]]
    )
    (
        attention_down_grad,
        attention_up_grad,
        attention_magnitude_grad,
        expand_down_grad,
        expand_up_grad,
        expand_magnitude_grad,
        contract_down_grad,
        contract_up_grad,
        contract_magnitude_grad,
    ) = lax.psum(
        (
            attention_down_grad,
            attention_up_grad,
            attention_magnitude_grad,
            expand_down_grad,
            expand_up_grad,
            expand_magnitude_grad,
            contract_down_grad,
            contract_up_grad,
            contract_magnitude_grad,
        ),
        ("dp", "seq"),
    )
    return (
        layer_output,
        tokens_grad.reshape(row_count, group_rows, width),
        attention_down_grad,
        attention_up_grad,
        attention_magnitude_grad,
        expand_down_grad,
        expand_up_grad,
        expand_magnitude_grad,
        contract_down_grad,
        contract_up_grad,
        contract_magnitude_grad,
    )


def solution(mesh):
    placed = (
        P("dp", "seq", None),
        P("dp", "seq", None),
        P(None, ("dp", "seq"), None),
        P(None, ("dp", "seq"), None),
        P(None, ("dp", "seq")),
        P(),
        P(),
        P(),
        P(),
        P(),
        P(),
        P(),
        P(),
        P(),
        P("dp"),
        P("dp"),
    )
    return jax.shard_map(
        body,
        mesh=mesh,
        in_specs=placed,
        out_specs=(
            P("dp", "seq", None),
            P("dp", "seq", None),
            P(),
            P(),
            P(),
            P(),
            P(),
            P(),
            P(),
            P(),
            P(),
        ),
        check_vma=False,
    )
```

profile of v0, /device:TPU:0, one launch (start us, length us, event | category | flops | bytes accessed | tf_op | source)
XLA Modules:
  0.0 1548.6 jit_solution(5965567785800622505)
XLA Ops:
  18.5 190.0 %all-gather.8.cloned.1.call-done = bf16[4,2048,2048]{2,1,0:T(8,128)(2,1)} async-done(((bf16[4,64,2048]{2,1,0:T(8,128)(2,1)}), bf16[4,2048,2048]{2,1,0:T(8,128)(2,1)}) %all-gather.8.cloned.1.call-update) | async-done | bytes 33554448 | tf_op jit(solution)/shard_map/all_gather | solution.py:227
  208.5 6.0 fusion.135
  214.5 6.6 fusion.143
  221.1 6.5 fusion.151
  228.2 6.5 fusion.399
  234.7 8.1 fusion.113
  243.5 5.0 fusion.139
  248.4 5.6 broadcast_multiply_fusion.3
  270.2 5.7 fusion.155
  276.0 3.8 multiply_convert_fusion.13
  293.6 60.5 %all-gather.16.cloned.1.call-done = bf16[5632,2048]{0,1:T(8,128)(2,1)} async-done(((bf16[5632,64]{0,1:T(8,128)(2,1)}), bf16[5632,2048]{0,1:T(8,128)(2,1)}) %all-gather.16.cloned.1.call-update) | async-done | bytes 23068688 | tf_op jit(solution)/shard_map/all_gather | solution.py:230
  354.1 24.0 %multiply_reduce_fusion.8 = (f32[2048]{0:T(1024)}, f32[16,2048]{1,0:T(8,128)}) fusion(f32[16,2048]{1,0:T(8,128)S(1)} %copy-done.42, f32[5632,16]{0,1:T(8,128)S(1)} %copy-done, bf16[5632,2048]{0,1:T(8,128)(2,1)} %all-gather.16.cloned.1.call-done), kind=kOutput, calls=%fused_computation.548 | convolution fusion | flops 2214656000 | bytes 23699456 | tf_op jit(solution)/shard_map/dot_general | solution.py:39
  378.2 10.2 fusion.94
  389.7 5.8 fusion.147
  395.5 4.0 broadcast_multiply_fusion.4
  412.6 3.7 copy.58
  418.9 15.6 %all-gather.12.cloned.1.call-done = bf16[2,512,2048]{1,2,0:T(8,128)(2,1)} async-done(((bf16[2,128,2048]{1,2,0:T(8,128)(2,1)}), bf16[2,512,2048]{1,2,0:T(8,128)(2,1)}) %all-gather.12.cloned.1.call-update) | async-done | bytes 4194320 | tf_op jit(solution)/shard_map/all_gather | solution.py:257
  434.5 6.4 copy.47
  440.9 73.8 %all-gather.10.cloned.1.call-done = bf16[2,512,2048]{1,2,0:T(8,128)(2,1)} async-done(((bf16[2,128,2048]{1,2,0:T(8,128)(2,1)}), bf16[2,512,2048]{1,2,0:T(8,128)(2,1)}) %all-gather.10.cloned.1.call-update) | async-done | bytes 4194320 | tf_op jit(solution)/shard_map/all_gather | solution.py:258
  514.7 12.9 while.39
  532.8 6.2 fusion.131
  546.1 12.1 all_gather.36
  558.9 212.7 %all-gather.14.cloned.1.call-done = bf16[2,2048,5632]{2,1,0:T(8,128)(2,1)} async-done(((bf16[2,64,5632]{2,1,0:T(8,128)(2,1)}), bf16[2,2048,5632]{2,1,0:T(8,128)(2,1)}) %all-gather.14.cloned.1.call-update) | async-done | bytes 46137360 | tf_op jit(solution)/shard_map/all_gather | solution.py:229
  771.5 13.2 fusion.111
  784.7 6.9 fusion.157
  791.6 14.5 fusion.99
  806.1 19.6 %fusion.96 = (f32[5632]{0:T(1024)S(1)}, f32[5632]{0:T(1024)S(1)}) fusion(bf16[2,2048,5632]{2,1,0:T(8,128)(2,1)} %all-gather.14.cloned.1.call-done), kind=kLoop, calls=%fused_computation.93 | loop fusion | flops 69194752 | bytes 46182400 | tf_op jit(solution)/shard_map/io,io->o/dot_general | solution.py:36
  825.8 13.3 fusion.342
  839.8 12.7 fusion.103
  852.5 9.9 multiply_convert_fusion.7
  866.3 11.7 fusion.535
  884.0 13.3 fusion.302
  897.4 12.6 multiply_reduce_fusion.2
  912.4 4.6 fusion.170
  917.0 4.6 fusion.173
  921.6 12.5 fusion.97
  937.3 13.7 fusion.105
  951.0 4.6 multiply_reduce_fusion.6
  958.6 6.5 fusion.125
  982.8 20.2 %while.40 = (s32[]{:T(128)}, f32[2,128,16,128]{1,3,2,0:T(8,128)}, bf16[2,16,128]{2,1,0:T(8,128)(2,1)}, bf16[2,512,16,128]{3,1,2,0:T(8,128)(2,1)}, pred[2,128,512...) while((s32[]{:T(128)}, f32[2,128,16,128]{1,3,2,0:T(8,128)}, ...), condition=%wide.region_23.24_spmd.clone, body=%wide.region_21.23_spmd.sunk.clone | while | flops 817887232 | bytes 85854552 | solution.py:360
  1003.1 21.4 %fusion.230 = f32[2048,16]{0,1:T(8,128)S(1)} fusion(bf16[2,2048,5632]{2,1,0:T(8,128)(2,1)} %all-gather.14.cloned.1.call-done, f32[2,16,5632]{2,1,0:T(8,128)S(1)} %copy-done.3, f32[5632]{0:T(1024)S(1)} %get-tuple-element.278), kind=kOutput, calls=%fused_computation.264 | convolution fusion | flops 2214682624 | bytes 23584768 | tf_op jit(solution)/shard_map/dot_general | solution.py:118
  1025.1 21.0 %fusion.233 = f32[2048,16]{0,1:T(8,128)S(1)} fusion(bf16[2,2048,5632]{2,1,0:T(8,128)(2,1)} %all-gather.14.cloned.1.call-done, f32[2,16,5632]{2,1,0:T(8,128)S(1)} %copy-done.3, f32[5632]{0:T(1024)S(1)} %get-tuple-element.281), kind=kOutput, calls=%fused_computation.265 | convolution fusion | flops 2214682624 | bytes 23584768 | tf_op jit(solution)/shard_map/dot_general | solution.py:118
  1046.3 9.1 fusion.227
  1056.1 15.2 all_gather.38
  1080.8 12.8 convolution_bitcast_fusion
  1106.5 32.8 %while.41 = (s32[]{:T(128)}, f32[2,128,16,128]{1,3,2,0:T(8,128)}, f32[2,128,16,128]{1,3,2,0:T(8,128)}, bf16[2,512,16,128]{1,3,2,0:T(8,128)(2,1)}, pred[2,512,128...) while((s32[]{:T(128)}, f32[2,128,16,128]{1,3,2,0:T(8,128)}, ...), condition=%wide.region_25.26_spmd.clone, body=%wide.region_24.25_spmd.sunk.clone | while | flops 1085276160 | bytes 29855372 | solution.py:378
  1107.0 4.5 fusion.673
  1111.6 6.4 fusion.674
  1118.0 5.2 fusion.675
  1123.2 4.5 fusion.673
  1127.8 6.4 fusion.674
  1134.2 5.2 fusion.675
  1141.5 5.4 multiply_subtract_fusion.1
  1147.0 3.8 fusion.523
  1158.4 3.7 fusion.524
  1189.2 3.7 fusion.275
  1192.9 6.1 fusion.133
  1201.0 5.7 fusion.149
  1208.7 5.9 fusion.141
  1225.3 8.9 fusion.221
  1234.8 8.9 fusion.224
  1244.3 9.2 fusion.218
  1256.4 126.2 %all-reduce.5.cloned.1.call-done = (f32[4,2048]{1,0:T(4,128)}, f32[2,5632]{1,0:T(2,128)}, f32[2048]{0:T(1024)}) async-done(((f32[4,2048]{1,0:T(4,128)}, f32[2,5632]{1,0:T(2,128)}, f32[2048]{0:T(1024)}), (f32[4,2048]{1,0:T(4,128)}, f32[2,5632]{1,0:T(2,128)}, f32[2048]{0:T(1024)})) %all-reduce.5.cloned.1.call-update) | async-done | bytes 86032 | tf_op jit(solution)/shard_map/psum | solution.py:424
  1382.7 146.9 %all-reduce.7.cloned.1.call-done = (f32[4,2048,16]{1,2,0:T(8,128)}, f32[4,16,2048]{2,1,0:T(8,128)}, f32[2,2048,16]{1,2,0:T(8,128)}, f32[2,16,5632]{2,1,0:T(8,128...) async-done(((f32[4,2048,16]{1,2,0:T(8,128)}, f32[4,16,2048]{2,1,0:T(8,128)}, f32[2,2048,16]{1,2,0:T(8,128)}, f32[2,16,5632]{2,1,0:T(8,128)}, f32[5632,16]{0,1:T(8,128)}, ...) | async-done | bytes 2523152 | tf_op jit(solution)/shard_map/psum | solution.py:424
  (610 shorter events, 232.5 us)
Async XLA Ops:
  7.2 276.3 %copy-start = (f32[5632,16]{0,1:T(8,128)S(1)}, f32[5632,16]{0,1:T(8,128)}, u32[]{:S(2)}) copy-start(f32[5632,16]{0,1:T(8,128)} %param.33) | copy-start | bytes 1081348
  7.2 201.2 %all-gather.8.cloned.1.call-start = ((), (), s32[]{:S(2)}) async-start(), calls=%async_computation | async-start | bytes 34603008 | tf_op jit(solution)/shard_map/all_gather | solution.py:227
  8.0 346.2 %all-gather.16.cloned.1.call-start = ((), (), s32[]{:S(2)}) async-start(), calls=%async_computation.4 | async-start | bytes 23789568 | tf_op jit(solution)/shard_map/all_gather | solution.py:230
  8.7 425.8 %all-gather.12.cloned.1.call-start = ((), (), s32[]{:S(2)}) async-start(), calls=%async_computation.2 | async-start | bytes 5242880 | tf_op jit(solution)/shard_map/all_gather | solution.py:257
  15.3 199.2 %copy-start.177 = (f32[2,128]{1,0:T(2,128)}, f32[2,128]{1,0:T(2,128)S(1)}, u32[]{:S(2)}) copy-start(f32[2,128]{1,0:T(2,128)S(1)} %fusion.284) | copy-start | bytes 3076
  17.4 210.8 %copy-start.10 = (f32[4,16,2048]{2,1,0:T(8,128)S(1)}, f32[4,16,2048]{2,1,0:T(8,128)}, u32[]{:S(2)}) copy-start(f32[4,16,2048]{2,1,0:T(8,128)} %param.28) | copy-start | bytes 1572868
  18.4 230.1 %copy-start.90 = (f32[256,16]{0,1:T(8,128)}, f32[256,16]{0,1:T(8,128)S(1)}, u32[]{:S(2)}) copy-start(f32[256,16]{0,1:T(8,128)S(1)} %fusion.416) | copy-start | bytes 49156
  18.4 224.4 %copy-start.148 = (f32[1,2048]{1,0:T(1,128)}, f32[1,2048]{1,0:T(1,128)S(1)}, u32[]{:S(2)}) copy-start(f32[1,2048]{1,0:T(1,128)S(1)} %get-tuple-element.351) | copy-start | bytes 24580
  18.4 224.4 %copy-start.152 = (f32[1,2048]{1,0:T(1,128)}, f32[1,2048]{1,0:T(1,128)S(1)}, u32[]{:S(2)}) copy-start(f32[1,2048]{1,0:T(1,128)S(1)} %get-tuple-element.348) | copy-start | bytes 24580
  18.4 251.1 %copy-start.146 = (f32[1,2048]{1,0:T(1,128)}, f32[1,2048]{1,0:T(1,128)S(1)}, u32[]{:S(2)}) copy-start(f32[1,2048]{1,0:T(1,128)S(1)} %get-tuple-element.350) | copy-start | bytes 24580
  18.5 251.1 %copy-start.150 = (f32[1,2048]{1,0:T(1,128)}, f32[1,2048]{1,0:T(1,128)S(1)}, u32[]{:S(2)}) copy-start(f32[1,2048]{1,0:T(1,128)S(1)} %get-tuple-element.349) | copy-start | bytes 24580
  208.5 26.2 %copy-start.2 = (bf16[4,2048,2048]{2,1,0:T(8,128)(2,1)S(1)}, bf16[4,2048,2048]{2,1,0:T(8,128)(2,1)}, u32[]{:S(2)}) copy-start(bf16[4,2048,2048]{2,1,0:T(8,128)(2,1)} %all-gather.8.cloned.1.call-done) | copy-start | bytes 100663296
  266.8 247.9 %all-gather.10.cloned.1.call-start = ((), (), s32[]{:S(2)}) async-start(), calls=%async_computation.1 | async-start | bytes 5242880 | tf_op jit(solution)/shard_map/all_gather | solution.py:258
  282.2 489.4 %all-gather.14.cloned.1.call-start = ((), (), s32[]{:S(2)}) async-start(), calls=%async_computation.3 | async-start | bytes 47579136 | tf_op jit(solution)/shard_map/all_gather | solution.py:229
  282.7 820.6 %all-gather.18.cloned.1.call-start = ((), (), s32[]{:S(2)}) async-start(), calls=%async_computation.5 | async-start | bytes 5242880 | tf_op jit(solution)/shard_map/all_gather | solution.py:364
  289.3 64.9 %copy-start.132 = (f32[16,16]{1,0:T(8,128)}, f32[16,16]{1,0:T(8,128)S(1)}, u32[]{:S(2)}) copy-start(f32[16,16]{1,0:T(8,128)S(1)} %fusion.383) | copy-start | bytes 3076
  293.6 101.9 %copy-start.94 = (f32[256,16]{0,1:T(8,128)}, f32[256,16]{0,1:T(8,128)S(1)}, u32[]{:S(2)}) copy-start(f32[256,16]{0,1:T(8,128)S(1)} %fusion.428) | copy-start | bytes 49156
  416.3 687.0 %all-gather.20.cloned.1.call-start = ((), (), s32[]{:S(2)}) async-start(), calls=%async_computation.6 | async-start | bytes 5242880 | tf_op jit(solution)/shard_map/all_gather | solution.py:365
  527.6 18.5 %copy-start.88 = (f32[2,16,128]{2,1,0:T(8,128)}, f32[2,16,128]{2,1,0:T(8,128)S(1)}, u32[]{:S(2)}) copy-start(f32[2,16,128]{2,1,0:T(8,128)S(1)} %get-tuple-element.649) | copy-start | bytes 49156
  544.2 295.6 %copy-start.17 = (bf16[256,2048]{1,0:T(8,128)(2,1)}, bf16[256,2048]{1,0:T(8,128)(2,1)S(1)}, u32[]{:S(2)}) copy-start(bf16[256,2048]{1,0:T(8,128)(2,1)S(1)} %multiply_convert_fusion.12) | copy-start | bytes 3145732
  545.1 239.6 %copy-start.96 = (f32[256,16]{0,1:T(8,128)}, f32[256,16]{0,1:T(8,128)S(1)}, u32[]{:S(2)}) copy-start(f32[256,16]{0,1:T(8,128)S(1)} %fusion.393) | copy-start | bytes 49156
  546.1 306.4 %copy-start.154 = (f32[256,16]{0,1:T(8,128)}, f32[256,16]{0,1:T(8,128)S(1)}, u32[]{:S(2)}) copy-start(f32[256,16]{0,1:T(8,128)S(1)} %fusion.386) | copy-start | bytes 49156
  791.6 60.9 %copy-start.53 = (f32[256,5632]{1,0:T(8,128)}, f32[256,5632]{1,0:T(8,128)S(1)}, u32[]{:S(2)}) copy-start(f32[256,5632]{1,0:T(8,128)S(1)} %fusion.157) | copy-start | bytes 17301508
  806.1 19.6 %copy-start.60 = (f32[16,5632]{1,0:T(8,128)}, f32[16,5632]{1,0:T(8,128)S(1)}, u32[]{:S(2)}) copy-start(f32[16,5632]{1,0:T(8,128)S(1)} %fusion.99) | copy-start | bytes 1081348
  881.6 15.8 %slice-start.4 = ((s8[5767168]{0:T(1024)(128)(4,1)}), s8[4194304]{0:T(1024)(128)(4,1)S(1)}, s32[]{:S(2)}) async-start(s8[5767168]{0:T(1024)(128)(4,1)} %bitcast.776), calls=%async_computation.13 | async-start | bytes 8388608
  882.2 15.1 copy-start.123
  917.0 17.1 %copy-start.102 = (f32[256,16]{0,1:T(8,128)}, f32[256,16]{0,1:T(8,128)S(1)}, u32[]{:S(2)}) copy-start(f32[256,16]{0,1:T(8,128)S(1)} %fusion.170) | copy-start | bytes 49156
  921.6 29.4 %copy-start.104 = (f32[256,16]{0,1:T(8,128)}, f32[256,16]{0,1:T(8,128)S(1)}, u32[]{:S(2)}) copy-start(f32[256,16]{0,1:T(8,128)S(1)} %fusion.173) | copy-start | bytes 49156
  937.3 13.7 copy-start.7
  968.8 14.0 copy-start.5
  968.8 14.0 copy-start.89
  1003.1 21.4 %copy-start.18 = (bf16[256,2048]{1,0:T(8,128)(2,1)S(1)}, bf16[256,2048]{1,0:T(8,128)(2,1)}, u32[]{:S(2)}) copy-start(bf16[256,2048]{1,0:T(8,128)(2,1)} %copy-done.17) | copy-start | bytes 3145732
  1003.1 21.4 %copy-start.77 = (f32[2048,16]{0,1:T(8,128)S(1)}, f32[2048,16]{0,1:T(8,128)}, u32[]{:S(2)}) copy-start(f32[2048,16]{0,1:T(8,128)} %fusion.240) | copy-start | bytes 393220
  1003.1 21.4 %copy-start.105 = (f32[256,16]{0,1:T(8,128)S(1)}, f32[256,16]{0,1:T(8,128)}, u32[]{:S(2)}) copy-start(f32[256,16]{0,1:T(8,128)} %copy-done.104) | copy-start | bytes 49156
  1003.1 379.6 %all-reduce.5.cloned.1.call-start = ((), (), s32[]{:S(2)}) async-start(), calls=%async_computation.7 | async-start | bytes 172032 | tf_op jit(solution)/shard_map/psum | solution.py:424
  1025.1 21.0 %copy-start.12 = (f32[4,16,2048]{2,1,0:T(8,128)S(1)}, f32[4,16,2048]{2,1,0:T(8,128)}, u32[]{:S(2)}) copy-start(f32[4,16,2048]{2,1,0:T(8,128)} %param.28) | copy-start | bytes 1572868
  1025.1 21.0 %copy-start.121 = (f32[2048]{0:T(1024)S(1)}, f32[2048]{0:T(1024)}, u32[]{:S(2)}) copy-start(f32[2048]{0:T(1024)} %copy-done.120) | copy-start | bytes 24580
  1046.2 25.1 %copy-start.40 = (bf16[2,128,16,128]{3,2,1,0:T(8,128)(2,1)S(1)}, bf16[2,128,16,128]{3,2,1,0:T(8,128)(2,1)}, u32[]{:S(2)}) copy-start(bf16[2,128,16,128]{3,2,1,0:T(8,128)(2,1)} %copy.48) | copy-start | bytes 3145732
  1046.2 25.1 %copy-start.75 = (f32[2048,16]{0,1:T(8,128)S(1)}, f32[2048,16]{0,1:T(8,128)}, u32[]{:S(2)}) copy-start(f32[2048,16]{0,1:T(8,128)} %fusion.244) | copy-start | bytes 393220
  1046.2 25.1 %copy-start.107 = (f32[256,16]{0,1:T(8,128)S(1)}, f32[256,16]{0,1:T(8,128)}, u32[]{:S(2)}) copy-start(f32[256,16]{0,1:T(8,128)} %copy-done.106) | copy-start | bytes 49156
  1046.2 26.3 %copy-start.145 = (f32[16,16]{1,0:T(8,128)S(1)}, f32[16,16]{1,0:T(8,128)}, u32[]{:S(2)}) copy-start(f32[16,16]{1,0:T(8,128)} %copy-done.144) | copy-start | bytes 3076
  1046.2 26.6 %copy-start.9 = (f32[256,2048]{1,0:T(8,128)S(1)}, f32[256,2048]{1,0:T(8,128)}, u32[]{:S(2)}) copy-start(f32[256,2048]{1,0:T(8,128)} %copy-done.8) | copy-start | bytes 6291460
  1046.2 26.6 %copy-start.73 = (f32[16,2048]{1,0:T(8,128)S(1)}, f32[16,2048]{1,0:T(8,128)}, u32[]{:S(2)}) copy-start(f32[16,2048]{1,0:T(8,128)} %get-tuple-element.360) | copy-start | bytes 393220
  1046.2 26.6 %copy-start.99 = (f32[256,16]{0,1:T(8,128)S(1)}, f32[256,16]{0,1:T(8,128)}, u32[]{:S(2)}) copy-start(f32[256,16]{0,1:T(8,128)} %copy-done.98) | copy-start | bytes 49156
  1046.2 26.6 %copy-start.112 = (f32[2048]{0:T(1024)S(1)}, f32[2048]{0:T(1024)}, u32[]{:S(2)}) copy-start(f32[2048]{0:T(1024)} %get-tuple-element.313) | copy-start | bytes 24580
  1046.3 26.6 %copy-start.164 = (f32[2048]{0:T(1024)S(1)}, f32[2048]{0:T(1024)}, u32[]{:S(2)}) copy-start(f32[2048]{0:T(1024)} %get-tuple-element.296) | copy-start | bytes 24580
  1055.3 20.0 %copy-start.44 = (f32[16,2048]{1,0:T(8,128)S(1)}, f32[16,2048]{1,0:T(8,128)}, u32[]{:S(2)}) copy-start(f32[16,2048]{1,0:T(8,128)} %param.34) | copy-start | bytes 393220
  1055.4 20.0 %copy-start.87 = (f32[2048]{0:T(1024)S(1)}, f32[2048]{0:T(1024)}, u32[]{:S(2)}) copy-start(f32[2048]{0:T(1024)} %get-tuple-element.274) | copy-start | bytes 24580
  1055.4 20.0 %copy-start.135 = (f32[16,16]{1,0:T(8,128)S(1)}, f32[16,16]{1,0:T(8,128)}, u32[]{:S(2)}) copy-start(f32[16,16]{1,0:T(8,128)} %copy-done.134) | copy-start | bytes 3076
  1055.4 21.0 %copy-start.137 = (f32[16,16]{1,0:T(8,128)S(1)}, f32[16,16]{1,0:T(8,128)}, u32[]{:S(2)}) copy-start(f32[16,16]{1,0:T(8,128)} %copy-done.136) | copy-start | bytes 3076
  1055.4 21.4 %copy-start.133 = (f32[16,16]{1,0:T(8,128)S(1)}, f32[16,16]{1,0:T(8,128)}, u32[]{:S(2)}) copy-start(f32[16,16]{1,0:T(8,128)} %copy-done.132) | copy-start | bytes 3076
  1055.9 21.3 %copy-start.33 = (bf16[2,128,2048]{2,1,0:T(8,128)(2,1)S(1)}, bf16[2,128,2048]{2,1,0:T(8,128)(2,1)}, u32[]{:S(2)}) copy-start(bf16[2,128,2048]{2,1,0:T(8,128)(2,1)} %param.23) | copy-start | bytes 3145732
  1055.9 21.3 %copy-start.74 = (f32[16,2048]{1,0:T(8,128)S(1)}, f32[16,2048]{1,0:T(8,128)}, u32[]{:S(2)}) copy-start(f32[16,2048]{1,0:T(8,128)} %get-tuple-element.374) | copy-start | bytes 393220
  1056.0 21.3 %copy-start.101 = (f32[256,16]{0,1:T(8,128)S(1)}, f32[256,16]{0,1:T(8,128)}, u32[]{:S(2)}) copy-start(f32[256,16]{0,1:T(8,128)} %copy-done.100) | copy-start | bytes 49156
  1056.0 21.3 %copy-start.125 = (f32[2048]{0:T(1024)S(1)}, f32[2048]{0:T(1024)}, u32[]{:S(2)}) copy-start(f32[2048]{0:T(1024)} %copy-done.123) | copy-start | bytes 24580
  1056.0 21.3 %copy-start.161 = (f32[2048]{0:T(1024)S(1)}, f32[2048]{0:T(1024)}, u32[]{:S(2)}) copy-start(f32[2048]{0:T(1024)} %get-tuple-element.273) | copy-start | bytes 24580
  1077.3 18.3 %slice-start.2 = ((s8[5767168]{0:T(1024)(128)(4,1)}), s8[4194304]{0:T(1024)(128)(4,1)S(1)}, s32[]{:S(2)}) async-start(s8[5767168]{0:T(1024)(128)(4,1)} %bitcast.743), calls=%async_computation.11 | async-start | bytes 8388608
  1077.3 21.4 %slice-start = ((s8[5767168]{0:T(1024)(128)(4,1)}), s8[4194304]{0:T(1024)(128)(4,1)S(1)}, s32[]{:S(2)}) async-start(s8[5767168]{0:T(1024)(128)(4,1)} %bitcast.741), calls=%async_computation.9 | async-start | bytes 8388608
  1080.8 14.8 slice-start.3
  1080.8 14.8 copy-start.127
  1080.8 14.8 copy-start.155
  1080.8 17.9 %slice-start.1 = ((s8[5767168]{0:T(1024)(128)(4,1)}), s8[1572864]{0:T(1024)(128)(4,1)S(1)}, s32[]{:S(2)}) async-start(s8[5767168]{0:T(1024)(128)(4,1)} %bitcast.741), calls=%async_computation.10 | async-start | bytes 3145728
  1254.6 274.9 %all-reduce.7.cloned.1.call-start = ((), (), s32[]{:S(2)}) async-start(), calls=%async_computation.8 | async-start | bytes 5046272 | tf_op jit(solution)/shard_map/psum | solution.py:424
  1382.7 158.5 %copy-start.181 = (f32[2048]{0:T(1024)S(1)}, f32[2048]{0:T(1024)}, u32[]{:S(2)}) copy-start(f32[2048]{0:T(1024)} %get-tuple-element.710) | copy-start | bytes 24580
  (145 other events, 850.5 us)
Sparse Core Ops, SparseCore 0:
  11.1 197.3 all-gather.7
  211.3 142.7 all-gather.15
  355.7 78.7 all-gather.11
  435.9 78.7 all-gather.9
  517.4 254.0 all-gather.13
  772.9 78.7 all-gather.17
  1003.2 78.8 all-gather.19
  1254.8 127.8 all-reduce.4
  1389.7 139.8 all-reduce.6
where the time goes:
time: 1550 us
  waiting for transfers between devices  828 us (53%)
  matrix products  485 us (31%)
  local copies, waits for them, and re-layouts  96.7 us (6%)
  other arithmetic  94.3 us (6%)
  blocking collectives  27.3 us (2%)
  between operations  16.8 us (1%)
    psum x2, waiting for transfers between devices, body(): lax.psum((attention_down_grad, attention_up_grad, attention_magnitude_gra...  273 us
    all_gather x1, waiting for transfers between devices, body(): lax.all_gather(expand_base, ('dp', 'seq'), axis=1, tiled=True)  213 us
    all_gather x1, waiting for transfers between devices, body(): lax.all_gather(attention_base, ('dp', 'seq'), axis=1, tiled=True)  190 us
    dot_general x7, matrix products, project_back(): jnp.dot(frozen_weight, scaled_up_weight.T, precision=highest_precision, p...  91.1 us
    dot_general x7, matrix products, prepare_weights(): jnp.dot(adapter_down_weight.T, frozen_weight, precision=highest_precision...  77.4 us
    all_gather x1, waiting for transfers between devices, body(): lax.all_gather(values_local, 'seq', axis=1, tiled=True)  73.8 us
    dot_general x7, matrix products, project_back(): jnp.einsum('to,io->ti', direction_gradient.astype(jnp.bfloat16), frozen_w...  63.7 us
    all_gather x1, waiting for transfers between devices, body(): lax.all_gather(contract_base, ('dp', 'seq'), axis=1, tiled=True)  60.5 us
  transfers between devices with their start and end apart: 9, of which 7 were waited for; matrix products, arithmetic and copies ran while one was open for 32% of the time, Pallas kernels for 0%

commit v1 on v0

v1 whole, which is shorter than its diff:
```python
import functools

import jax
import jax.numpy as jnp
from jax import lax
from jax.experimental import pallas as pl
from jax.experimental.pallas import tpu as pltpu
from jax.sharding import Mesh
from jax.sharding import PartitionSpec as P

HEAD_DIM = 128
SCALE = 2.0
BF = jnp.bfloat16
F32 = jnp.float32
ALL = ("yy", "xx", "core", "seq")
WORD = 512


def mm(a, b, dims=((1,), (0,))):
    return lax.dot_general(a, b, (dims, ((), ())), preferred_element_type=F32)


def nt(a, b):
    return mm(a, b, ((1,), (1,)))


def tn(a, b):
    return mm(a, b, ((0,), (0,)))


def take(a, index, axis):
    return lax.dynamic_index_in_dim(a, index, axis, keepdims=False)


def swap(a, name):
    return lax.ppermute(a, name, [(0, 1), (1, 0)])


def shift(a, name, step):
    size = lax.axis_size(name)
    return lax.ppermute(a, name, [(i, (i + step) % size) for i in range(size)])


def pair(mine, other, index, axis=0):
    first = jnp.where(index == 0, mine, other)
    second = jnp.where(index == 0, other, mine)
    return jnp.stack([first, second], axis=axis)


def put(buffer, block, index, axis):
    return lax.dynamic_update_slice_in_dim(buffer, jnp.expand_dims(block, axis), index, axis)


def rms(v):
    return v * lax.rsqrt(jnp.mean(v * v, axis=-1, keepdims=True) + 1e-05)


def rms_back(v, grad):
    inverse = lax.rsqrt(jnp.mean(v * v, axis=-1, keepdims=True) + 1e-05)
    inner = jnp.mean(v * grad, axis=-1, keepdims=True)
    return grad * inverse - v * (inner * inverse * inverse * inverse)


def merged(base, down, up):
    product = lax.dot_general(
        down, up, (((down.ndim - 1,), (up.ndim - 2,)), (tuple(range(down.ndim - 2)),) * 2),
        precision=lax.Precision.HIGHEST, preferred_element_type=F32,
    )
    return (base.astype(F32) + SCALE * product).astype(BF)


class Box:
    def __init__(self, arrays):
        self.arrays = list(arrays)


class Links:
    def __init__(self, depth):
        self.depth = depth
        self.sent = {}

    def hold(self, link, arrays):
        history = self.sent.setdefault(link, [])
        if len(history) >= self.depth:
            old = history[-self.depth]
            both = lax.optimization_barrier((list(arrays), old.arrays))
            arrays, old.arrays = both[0], both[1]
        return arrays

    def send(self, link, box, move):
        box.arrays = list(self.hold(link, box.arrays))
        result = Box([move(a) for a in box.arrays])
        self.sent[link].append(result)
        return result


class Gathered:
    def __init__(self, over_x):
        self.over_x = over_x
        self.blocks = []

    def add(self, box, turn, far, step):
        self.blocks.append((box, turn, far, step))

    def build(self, index):
        y, x, z = lax.axis_index("yy"), lax.axis_index("xx"), lax.axis_index("seq")
        ny, count = lax.axis_size("yy"), lax.axis_size("seq")
        piece = self.blocks[0][0].arrays[index]
        lead = piece.ndim - 2
        shape = (ny,) + ((2,) if self.over_x else ()) + piece.shape[:lead] + (count,) + piece.shape[lead:]
        buffer = jnp.zeros(shape, piece.dtype)
        for box, turn, far, step in self.blocks:
            block = jnp.expand_dims(box.arrays[index], lead)[None]
            start = [(y - turn) % ny]
            if self.over_x:
                block = block[None]
                start.append(1 - x if far else x)
            start += [0] * lead + [(z - step) % count, 0, 0]
            buffer = lax.dynamic_update_slice(buffer, block, [jnp.int32(s) for s in start])
        return buffer


def turned(v, cosine, sine):
    return v * cosine + pltpu.roll(v, HEAD_DIM // 2, 1) * sine


def qkv_kernel(rotated, h_ref, v_ref, m_ref, cos_ref, sin_ref, t_ref, p_ref, n_ref):
    block = v_ref[...]
    t = jnp.dot(h_ref[...], block, preferred_element_type=F32)
    wide = block.astype(F32)
    norm = jnp.sqrt(jnp.sum(wide * wide, axis=0, keepdims=True))
    n_ref[...] = norm
    t_ref[...] = t.astype(BF)
    scaled = t * (m_ref[...] / norm)

    @pl.when(pl.program_id(0) < rotated)
    def _():
        for part in range(t.shape[1] // HEAD_DIM):
            columns = slice(part * HEAD_DIM, (part + 1) * HEAD_DIM)
            p_ref[:, columns] = turned(scaled[:, columns], cos_ref[...], sin_ref[...]).astype(BF)

    @pl.when(pl.program_id(0) >= rotated)
    def _():
        p_ref[...] = scaled.astype(BF)


def qkv_forward(h, weight, magnitude, cosine, sine):
    rows, depth = h.shape
    columns = weight.shape[1]
    width = 2 * HEAD_DIM
    rotated = columns * 2 // 3 // width
    whole = lambda j: (0, 0)
    strip = lambda j: (0, j)
    return pl.pallas_call(
        functools.partial(qkv_kernel, rotated),
        grid=(columns // width,),
        in_specs=[
            pl.BlockSpec((rows, depth), whole),
            pl.BlockSpec((depth, width), strip),
            pl.BlockSpec((1, width), strip),
            pl.BlockSpec((rows, HEAD_DIM), whole),
            pl.BlockSpec((rows, HEAD_DIM), whole),
        ],
        out_specs=[
            pl.BlockSpec((rows, width), strip),
            pl.BlockSpec((rows, width), strip),
            pl.BlockSpec((1, width), strip),
        ],
        out_shape=[
            jax.ShapeDtypeStruct((rows, columns), BF),
            jax.ShapeDtypeStruct((rows, columns), BF),
            jax.ShapeDtypeStruct((1, columns), F32),
        ],
        compiler_params=pltpu.CompilerParams(vmem_limit_bytes=32 << 20),
        cost_estimate=pl.CostEstimate(
            flops=2 * rows * depth * columns, bytes_accessed=2 * depth * columns + 6 * rows * columns,
            transcendentals=columns,
        ),
        name="qkv_forward",
    )(h, weight, magnitude, cosine, sine)


def softmax_block(q, k, bias):
    scores = nt(q, k) * HEAD_DIM ** (-0.5) + bias
    weights = jnp.exp(scores - jnp.max(scores, axis=-1, keepdims=True))
    return weights / jnp.sum(weights, axis=-1, keepdims=True)


def attend_kernel(q_ref, k_ref, v_ref, bias_ref, o_ref):
    probs = softmax_block(q_ref[...], k_ref[...], bias_ref[...])
    o_ref[...] = mm(probs.astype(BF), v_ref[...]).astype(BF)


def attend_back_kernel(q_ref, k_ref, v_ref, g_ref, bias_ref, dq_ref, dk_ref, dv_ref):
    q, k, g = q_ref[...], k_ref[...], g_ref[...]
    probs = softmax_block(q, k, bias_ref[...])
    grad = nt(g, v_ref[...])
    inner = jnp.sum(probs * grad, axis=-1, keepdims=True)
    raw = (probs * (grad - inner) * HEAD_DIM ** (-0.5)).astype(BF)
    dq_ref[...] = mm(raw, k)
    dk_ref[...] = tn(raw, q)
    dv_ref[...] = tn(probs.astype(BF), g)


def attention_call(kernel, name, heads, q, kv, offsets, extra, bias, outs):
    rows, keys = bias.shape
    head = lambda base: lambda j: (0, base + j)
    specs = [
        pl.BlockSpec((rows, HEAD_DIM), head(0)),
        pl.BlockSpec((keys, HEAD_DIM), head(offsets[0])),
        pl.BlockSpec((keys, HEAD_DIM), head(offsets[1])),
    ]
    specs += [pl.BlockSpec((rows, HEAD_DIM), head(0)) for _ in extra]
    specs.append(pl.BlockSpec((rows, keys), lambda j: (0, 0)))
    return pl.pallas_call(
        kernel,
        grid=(heads,),
        in_specs=specs,
        out_specs=[pl.BlockSpec((length, HEAD_DIM), head(0)) for length, _ in outs],
        out_shape=[jax.ShapeDtypeStruct((length, heads * HEAD_DIM), kind) for length, kind in outs],
        compiler_params=pltpu.CompilerParams(vmem_limit_bytes=48 << 20),
        cost_estimate=pl.CostEstimate(
            flops=4 * len(outs) * rows * keys * HEAD_DIM * heads,
            bytes_accessed=8 * rows * HEAD_DIM * heads, transcendentals=rows * keys * heads,
        ),
        name=name,
    )(q, kv, kv, *extra, bias)


def attend_back_turn_kernel(
    q_ref, k_ref, v_ref, g_ref, bias_ref, tq_ref, tk_ref, tv_ref, s_ref, r_ref, cos_ref, sin_ref, dt_ref, dm_ref
):
    q, k, g = q_ref[...], k_ref[...], g_ref[...]
    probs = softmax_block(q, k, bias_ref[...])
    grad = nt(g, v_ref[...])
    inner = jnp.sum(probs * grad, axis=-1, keepdims=True)
    raw = (probs * (grad - inner) * HEAD_DIM ** (-0.5)).astype(BF)
    cosine, sine = cos_ref[...], -sin_ref[...]
    plain = (turned(mm(raw, k), cosine, sine), turned(tn(raw, q), cosine, sine), tn(probs.astype(BF), g))
    for member, t_ref in enumerate((tq_ref, tk_ref, tv_ref)):
        dt_ref[member] = (plain[member] * s_ref[member]).astype(BF)
        dm_ref[member] = jnp.sum(plain[member] * t_ref[...].astype(F32), axis=0, keepdims=True) * r_ref[member]


def attend_back_turn(heads, qkv, grad, bias, t, factor, inverse, cosine, sine):
    rows = bias.shape[0]
    head = lambda base: lambda j: (0, base + j)
    whole = lambda j: (0, 0)
    block = lambda base: pl.BlockSpec((rows, HEAD_DIM), head(base))
    member = lambda j: (0, 0, j)
    return pl.pallas_call(
        attend_back_turn_kernel,
        grid=(heads,),
        in_specs=[
            block(0), block(heads), block(2 * heads), block(0),
            pl.BlockSpec((rows, rows), whole),
            block(0), block(heads), block(2 * heads),
            pl.BlockSpec((3, 1, HEAD_DIM), member),
            pl.BlockSpec((3, 1, HEAD_DIM), member),
            pl.BlockSpec((rows, HEAD_DIM), whole),
            pl.BlockSpec((rows, HEAD_DIM), whole),
        ],
        out_specs=[pl.BlockSpec((3, rows, HEAD_DIM), member), pl.BlockSpec((3, 1, HEAD_DIM), member)],
        out_shape=[
            jax.ShapeDtypeStruct((3, rows, heads * HEAD_DIM), BF),
            jax.ShapeDtypeStruct((3, 1, heads * HEAD_DIM), F32),
        ],
        compiler_params=pltpu.CompilerParams(vmem_limit_bytes=48 << 20),
        cost_estimate=pl.CostEstimate(
            flops=10 * rows * rows * HEAD_DIM * heads, bytes_accessed=20 * rows * HEAD_DIM * heads,
            transcendentals=rows * rows * heads,
        ),
        name="attend_back_turn",
    )(qkv, qkv, qkv, grad, bias, t, t, t, factor, inverse, cosine, sine)


def words_out(ref, start, value):
    rows, columns = value.shape
    for chunk in range(-(-columns // WORD)):
        left = chunk * WORD
        used = min(WORD, columns - left)
        ref[chunk, start : start + rows, :used] = value[:, left : left + used]
        if used < WORD:
            ref[chunk, start : start + rows, used:] = jnp.zeros((rows, WORD - used), F32)


def row_of(row, rows=8):
    return jnp.concatenate([row, jnp.zeros((rows - row.shape[0], row.shape[1]), F32)], axis=0)


def qkv_back_kernel(
    dt_ref, v_ref, h_ref, low_ref, up_ref, cross_ref, s_ref, n_ref, dm_ref, out_ref, shared_ref, core_ref, acc_ref
):
    member = pl.program_id(0)
    dt, weight = dt_ref[0], v_ref[...]
    update = nt(dt, weight)

    @pl.when(member == 0)
    def _():
        acc_ref[...] = update

    @pl.when(member > 0)
    def _():
        acc_ref[...] += update

    @pl.when(member == pl.num_programs(0) - 1)
    def _():
        out_ref[...] = acc_ref[...].astype(BF)

    up = up_ref[0]
    pull = -s_ref[0] * dm_ref[0] / n_ref[0]
    low_grad = nt(dt, up.astype(BF)).astype(BF)
    words_out(shared_ref, 0, SCALE * (tn(low_grad, h_ref[...]) + nt((up * pull).astype(BF), weight)))
    words_out(core_ref, 0, SCALE * (mm(low_ref[0], dt) + cross_ref[0] * pull))


def qkv_back(dt, weight, h, low, up, cross, factor, norm, dm):
    members, rows, columns = dt.shape
    width = h.shape[1]
    rank = up.shape[1]
    step = lambda j: (j, 0, 0)
    small = pl.BlockSpec((1, 1, columns), step)
    return pl.pallas_call(
        qkv_back_kernel,
        grid=(members,),
        in_specs=[
            pl.BlockSpec((1, rows, columns), step),
            pl.BlockSpec((width, columns), lambda j: (0, j)),
            pl.BlockSpec((rows, width), lambda j: (0, 0)),
            pl.BlockSpec((1, rank, rows), step),
            pl.BlockSpec((1, rank, columns), step),
            pl.BlockSpec((1, rank, columns), step),
            small, small, small,
        ],
        out_specs=[
            pl.BlockSpec((rows, width), lambda j: (0, 0)),
            pl.BlockSpec((width // WORD, rank, WORD), lambda j: (0, j, 0)),
            pl.BlockSpec((columns // WORD, rank, WORD), lambda j: (0, j, 0)),
        ],
        out_shape=[
            jax.ShapeDtypeStruct((rows, width), BF),
            jax.ShapeDtypeStruct((width // WORD, members * rank, WORD), F32),
            jax.ShapeDtypeStruct((columns // WORD, members * rank, WORD), F32),
        ],
        scratch_shapes=[pltpu.VMEM((rows, width), F32)],
        compiler_params=pltpu.CompilerParams(vmem_limit_bytes=48 << 20),
        cost_estimate=pl.CostEstimate(
            flops=2 * members * rows * columns * width, bytes_accessed=2 * members * width * columns,
            transcendentals=0,
        ),
        name="qkv_back",
    )(dt, weight, h, low, up, cross, factor, norm, dm)


def out_adapter_kernel(dt_ref, v_ref, u_ref, down_ref, up_ref, s_ref, n_ref, dm_ref, own_ref, shared_ref, core_ref):
    dt, weight, u = dt_ref[...], v_ref[...], u_ref[...]
    down, up = down_ref[...], up_ref[...]
    rank = up.shape[0]
    pull = -s_ref[...] * dm_ref[...] / n_ref[...]
    low_grad = nt(dt, up.astype(BF)).astype(BF)
    low = nt(down, u).astype(BF)
    words_out(core_ref, 0, SCALE * (tn(low_grad, u) + nt((up * pull).astype(BF), weight)))
    words_out(shared_ref, 0, SCALE * (mm(low, dt) + mm(down, weight) * pull))
    words_out(shared_ref, rank, row_of(own_ref[...]))


def out_adapter(dt, weight, u, down, up, factor, norm, dm_pair, dm_own):
    rank, width = up.shape
    inside = u.shape[1]
    return pl.pallas_call(
        out_adapter_kernel,
        out_shape=[
            jax.ShapeDtypeStruct((width // WORD, rank + 8, WORD), F32),
            jax.ShapeDtypeStruct((inside // WORD, rank, WORD), F32),
        ],
        compiler_params=pltpu.CompilerParams(vmem_limit_bytes=48 << 20),
        cost_estimate=pl.CostEstimate(
            flops=2 * width * inside * 256, bytes_accessed=2 * width * inside, transcendentals=0
        ),
        name="out_adapter",
    )(dt, weight, u, down, up, factor, norm, dm_pair, dm_own)


def chunks_of(columns, width):
    return [(left, min(left + width, columns)) for left in range(0, columns, width)]


def feed_kernel(
    h_ref, g_ref, expand_ref, contract_ref, s_ref, back_ref, out_ref, dt_ref, hidden_ref, dm_ref
):
    h, g = h_ref[...], g_ref[...]
    quarter = hidden_ref.shape[1]

    @pl.when(pl.program_id(0) == 0)
    def _():
        dm_ref[...] = jnp.zeros_like(dm_ref)

    for left, right in chunks_of(quarter, 512):
        near, far = slice(left, right), slice(quarter + left, quarter + right)
        gate_t = mm(h, expand_ref[:, near])
        up_t = mm(h, expand_ref[:, far])
        grad = mm(g, contract_ref[:, near])
        gate = gate_t * s_ref[:, near]
        up = up_t * s_ref[:, far]
        sigmoid = 1.0 / (1.0 + jnp.exp(-gate))
        silu = gate * sigmoid
        hidden_ref[:, near] = (silu * up).astype(BF)
        up_grad = grad * silu
        gate_grad = grad * up * (sigmoid + silu * (1.0 - sigmoid))
        dm_ref[:, near] += jnp.sum(gate_grad * gate_t, axis=0, keepdims=True)
        dm_ref[:, far] += jnp.sum(up_grad * up_t, axis=0, keepdims=True)
        dt_ref[:, near] = (gate_grad * s_ref[:, near]).astype(BF)
        dt_ref[:, far] = (up_grad * s_ref[:, far]).astype(BF)
    back_ref[...] = nt(dt_ref[...], expand_ref[...]).astype(BF)
    out_ref[...] = nt(hidden_ref[...], contract_ref[...]).astype(BF)


def feed_forward_back(h, g, expand, contract, factor):
    rows, width = h.shape
    double = expand.shape[1]
    quarter = double // 2
    block = rows // 2
    row = lambda i: (i, 0)
    whole = lambda i: (0, 0)
    once = pl.Buffered(1)
    return pl.pallas_call(
        feed_kernel,
        grid=(rows // block,),
        in_specs=[
            pl.BlockSpec((block, width), row),
            pl.BlockSpec((block, width), row),
            pl.BlockSpec((width, double), whole, pipeline_mode=once),
            pl.BlockSpec((width, quarter), whole, pipeline_mode=once),
            pl.BlockSpec((1, double), whole),
        ],
        out_specs=[
            pl.BlockSpec((block, width), row),
            pl.BlockSpec((block, width), row),
            pl.BlockSpec((block, double), row),
            pl.BlockSpec((block, quarter), row),
            pl.BlockSpec((1, double), whole),
        ],
        out_shape=[
            jax.ShapeDtypeStruct((rows, width), BF),
            jax.ShapeDtypeStruct((rows, width), BF),
            jax.ShapeDtypeStruct((rows, double), BF),
            jax.ShapeDtypeStruct((rows, quarter), BF),
            jax.ShapeDtypeStruct((1, double), F32),
        ],
        compiler_params=pltpu.CompilerParams(vmem_limit_bytes=56 << 20),
        cost_estimate=pl.CostEstimate(
            flops=12 * rows * width * quarter, bytes_accessed=6 * width * quarter + 18 * rows * quarter,
            transcendentals=rows * quarter,
        ),
        name="feed_forward_back",
    )(h, g, expand, contract, factor)


def feed_adapter_kernel(h_ref, g_ref, dt_ref, hidden_ref, down_ref, up_ref, cdown_ref, cup_ref, *refs):
    shared_ref, quad_ref = refs[-2:]
    rank = cup_ref.shape[0]
    h, g, dt, hidden = h_ref[...], g_ref[...], dt_ref[...], hidden_ref[...]
    quarter = hidden.shape[1]
    down, up, cdown, cup = down_ref[...], up_ref[...], cdown_ref[...], cup_ref[...]
    halves = (slice(0, quarter), slice(quarter, 2 * quarter))
    shared, quads = [], []
    low = nt(down, h).astype(BF)
    for member, part in enumerate(halves):
        place = slice(member * rank, (member + 1) * rank)
        low_grad = nt(dt[:, part], up[member].astype(BF)).astype(BF)
        shared.append(tn(low_grad, h))
        quads.append(mm(low[place], dt[:, part]))
    low_grad = nt(g, cup.astype(BF)).astype(BF)
    quads.append(tn(low_grad, hidden))
    shared.append(mm(nt(cdown, hidden).astype(BF), g))
    if len(refs) == 2:
        for member in range(3):
            rows = slice(member * rank, (member + 1) * rank)
            shared_ref[rows] = shared[member]
            quad_ref[rows] = quads[member]
        return
    shared_in, quad_in, expand_ref, contract_ref, pull_ref, dm_ref, cpull_ref, cdm_ref = refs[:-2]
    for member, part in enumerate(halves):
        rows = slice(member * rank, (member + 1) * rank)
        pull = pull_ref[:, part]
        weight = expand_ref[:, part]
        total = shared[member] + shared_in[rows] + nt((up[member] * pull).astype(BF), weight)
        words_out(shared_ref, member * rank, SCALE * total)
        total = quads[member] + quad_in[rows] + mm(down[rows], weight) * pull
        words_out(quad_ref, member * rank, SCALE * total)
    rows = slice(2 * rank, 3 * rank)
    total = quads[2] + quad_in[rows] + mm((cup * cpull_ref[...]).astype(BF), contract_ref[...])
    words_out(quad_ref, 2 * rank, SCALE * total)
    total = shared[2] + shared_in[rows] + nt(cdown, contract_ref[...]) * cpull_ref[...]
    words_out(shared_ref, 2 * rank, SCALE * total)
    words_out(shared_ref, 3 * rank, row_of(cdm_ref[...]))
    both = jnp.concatenate([dm_ref[:, part] for part in halves], axis=0)
    words_out(quad_ref, 3 * rank, row_of(both))


def feed_adapter(h, g, dt, hidden, down, up, cdown, cup, last=None):
    rank, width = cup.shape
    quarter = hidden.shape[1]
    if last is None:
        shapes = [(3 * rank, width), (3 * rank, quarter)]
    else:
        shapes = [(width // WORD, 3 * rank + 8, WORD), (-(-quarter // WORD), 3 * rank + 8, WORD)]
    return pl.pallas_call(
        feed_adapter_kernel,
        out_shape=[jax.ShapeDtypeStruct(shape, F32) for shape in shapes],
        compiler_params=pltpu.CompilerParams(vmem_limit_bytes=56 << 20),
        cost_estimate=pl.CostEstimate(
            flops=8 * h.shape[0] * width * 512, bytes_accessed=8 * h.shape[0] * width, transcendentals=0
        ),
        name="feed_adapter",
    )(h, g, dt, hidden, down, up, cdown, cup, *(last or ()))


def turn_back_kernel(rotated, g_ref, t_ref, s_ref, r_ref, cos_ref, sin_ref, dt_ref, dm_ref):
    grad = g_ref[...]

    def finish(plain):
        dt_ref[0] = (plain * s_ref[...]).astype(BF)
        dm_ref[...] = jnp.sum(plain * t_ref[...].astype(F32), axis=0, keepdims=True) * r_ref[...]

    @pl.when(pl.program_id(0) < rotated)
    def _():
        finish(turned(grad, cos_ref[...], -sin_ref[...]))

    @pl.when(pl.program_id(0) >= rotated)
    def _():
        finish(grad)


def turn_back(grads, t, factor, inverse, cosine, sine):
    rows, columns = t.shape
    whole = lambda j: (0, 0)
    strip = lambda j: (0, j)
    heads = columns // HEAD_DIM
    each = heads // 3
    return pl.pallas_call(
        functools.partial(turn_back_kernel, 2 * each),
        grid=(heads,),
        in_specs=[
            pl.BlockSpec((rows, HEAD_DIM), strip),
            pl.BlockSpec((rows, HEAD_DIM), strip),
            pl.BlockSpec((1, HEAD_DIM), strip),
            pl.BlockSpec((1, HEAD_DIM), strip),
            pl.BlockSpec((rows, HEAD_DIM), whole),
            pl.BlockSpec((rows, HEAD_DIM), whole),
        ],
        out_specs=[
            pl.BlockSpec((1, rows, HEAD_DIM), lambda j: (j // each, 0, j % each)),
            pl.BlockSpec((1, HEAD_DIM), strip),
        ],
        out_shape=[
            jax.ShapeDtypeStruct((3, rows, columns // 3), BF),
            jax.ShapeDtypeStruct((1, columns), F32),
        ],
        name="turn_back",
    )(grads, t, factor, inverse, cosine, sine)


def unpacked(words, columns):
    return jnp.concatenate([words[i] for i in range(words.shape[0])], axis=1)[:, :columns]


def pad_rows(a, multiple):
    short = -a.shape[0] % multiple
    return jnp.pad(a, ((0, short), (0, 0))) if short else a


def halve(a, name, index):
    parts = a.reshape(2, a.shape[0] // 2, a.shape[1])
    return take(parts, index, 0) + swap(take(parts, 1 - index, 0), name)


def join(a, name, index):
    return pair(a, swap(a, name), index).reshape(2 * a.shape[0], a.shape[1])


def spread(a, name):
    size, place = lax.axis_size(name), lax.axis_index(name)
    parts = a.reshape(size, a.shape[0] // size, a.shape[1])
    total = take(parts, place, 0)
    for step in range(1, size):
        total = total + shift(take(parts, (place + step) % size, 0), name, step)
    return total


def collect(a, name):
    size, place = lax.axis_size(name), lax.axis_index(name)
    buffer = jnp.zeros((size,) + a.shape, a.dtype)
    buffer = put(buffer, a, place, 0)
    for step in range(1, size):
        buffer = put(buffer, shift(a, name, step), (place - step) % size, 0)
    return buffer.reshape(size * a.shape[0], a.shape[1])


def reduce_all(shared, by_core, by_quad):
    c, x = lax.axis_index("core"), lax.axis_index("xx")
    unit = lax.axis_size("yy") * lax.axis_size("seq")
    half = halve(pad_rows(shared, 16), "core", c)
    stack = half if by_core is None else jnp.concatenate([half, by_core], axis=0)
    quarter = halve(pad_rows(stack, 16), "xx", x)
    last = quarter if by_quad is None else jnp.concatenate([quarter, by_quad], axis=0)
    last = pad_rows(last, 8 * unit)
    last = collect(collect(spread(spread(last, "yy"), "seq"), "seq"), "yy")
    joined = join(last[: quarter.shape[0]], "xx", x)
    everywhere = join(joined[: half.shape[0]], "core", c)
    cores = None
    if by_core is not None:
        mine = joined[half.shape[0] : half.shape[0] + by_core.shape[0]]
        cores = pair(mine, swap(mine, "core"), c)
    quads = None
    if by_quad is not None:
        mine = last[quarter.shape[0] : quarter.shape[0] + by_quad.shape[0]]
        both = pair(mine, swap(mine, "xx"), x)
        quads = pair(both, swap(both, "core"), c, axis=1)
    return everywhere, cores, quads


def body(
    tokens,
    cotangent,
    attention_base,
    expand_base,
    contract_base,
    attention_down,
    attention_up,
    attention_magnitude,
    expand_down,
    expand_up,
    expand_magnitude,
    contract_down,
    contract_up,
    contract_magnitude,
    prompt_length,
    response_length,
):
    y, x = lax.axis_index("yy"), lax.axis_index("xx")
    c, z = lax.axis_index("core"), lax.axis_index("seq")
    ny, count = lax.axis_size("yy"), lax.axis_size("seq")
    own_rows, local, width = tokens.shape
    rows = 2 * own_rows
    split = count // rows
    piece = local // (2 * split)
    half = count * piece
    blocks = ny * 2
    rank = attention_down.shape[-1]
    unit = attention_base.shape[1]
    hidden_size = expand_base.shape[-1]
    quarter = hidden_size // 4
    place = ((y * 2 + x) * 2 + c) * count + z
    sub = z % split

    def by_core(a):
        shaped = a.reshape(a.shape[:-1] + (blocks, 2, a.shape[-1] // blocks // 2))
        axis = a.ndim
        flat = a.shape[:-1] + (a.shape[-1] // 2,)
        return take(shaped, c, axis).reshape(flat), take(shaped, 1 - c, axis).reshape(flat)

    def by_quarter(a):
        shaped = a.reshape(a.shape[:-1] + (4, quarter))
        return take(shaped, 2 * x + c, a.ndim - 1)

    down_rows = lax.dynamic_slice_in_dim(attention_down, place * unit, unit, 1)
    attention = merged(attention_base, down_rows, attention_up)
    mine, other = by_core(attention[:3])
    mine = mine.transpose(1, 0, 2).reshape(unit, -1)
    other = other.transpose(1, 0, 2).reshape(unit, -1)
    qkv_piece = pair(mine, swap(other, "core"), c)

    def relayout_start(a):
        shaped = a.reshape(own_rows, split, 2, piece, width)
        kept, sent = take(shaped, c, 2), take(shaped, 1 - c, 2)
        return Box([pair(kept, swap(sent, "core"), c).reshape(count, piece, width)])

    def exchange(a):
        return lax.all_to_all(a, "seq", 0, 0, tiled=True)

    def ring(box):
        return links.send("seq", box, lambda a: shift(a, "seq", 1))

    def across(box, turn):
        return links.send("yy", box, lambda a: shift(a, "yy", turn)) if turn else box

    links = Links(2)
    out_piece = attention[3]
    attention_boxes = [Box([qkv_piece, out_piece])]
    attention_far = [links.send("xx", attention_boxes[0], lambda a: swap(a, "xx"))]

    expand_rows = lax.dynamic_slice_in_dim(expand_down, place * unit, unit, 1)
    expand = merged(expand_base, expand_rows, expand_up)
    contract_columns = lax.dynamic_slice_in_dim(contract_up, place * unit, unit, 1)
    contract = merged(contract_base.T, contract_columns.T, contract_down.T)
    feed = jnp.stack([expand[0], expand[1], contract], axis=1).reshape(unit, 3, 2, 2, quarter)
    by_x = pair(take(feed, c, 3), swap(take(feed, 1 - c, 3), "core"), c)
    far = links.send("xx", Box([take(by_x, 1 - x, 3)]), lambda a: swap(a, "xx"))
    feed_piece = pair(take(by_x, x, 3), far.arrays[0], x)
    expand_piece = feed_piece[:, :, :, :2].reshape(2, 2, unit, 2 * quarter)

    for step in range(1, count):
        attention_boxes.append(ring(attention_boxes[-1]))
    tokens_moved = links.send("seq", relayout_start(tokens), exchange)
    expand_boxes, contract_boxes = [Box([expand_piece])], [Box([feed_piece[:, :, :, 2]])]
    for step in range(1, count):
        expand_boxes.append(ring(expand_boxes[-1]))
        contract_boxes.append(ring(contract_boxes[-1]))
        if step == 1:
            cotangent_moved = links.send("seq", relayout_start(cotangent), exchange)

    attention_all, expand_all, contract_all = Gathered(True), Gathered(False), Gathered(False)

    def feed_step(step):
        for boxes, gathered in ((expand_boxes, expand_all), (contract_boxes, contract_all)):
            for turn in range(ny):
                gathered.add(across(boxes[step], turn), turn, False, step)

    def attention_step(step):
        for turn in range(ny):
            near = across(attention_boxes[step], turn)
            if step == 0 and turn == 0:
                other = attention_far[0]
            else:
                other = links.send("xx", near, lambda a: swap(a, "xx"))
            attention_all.add(near, turn, False, step)
            attention_all.add(other, turn, True, step)

    for step in range(count):
        if step >= 2:
            feed_step(step - 2)
        attention_step(step)
    for step in range(max(count - 2, 0), count):
        feed_step(step)

    tokens_own = tokens_moved.arrays[0].reshape(half, width)
    tokens_both = jnp.concatenate([tokens_own, swap(tokens_own, "core")], axis=0)
    qkv_weight = attention_all.build(0).reshape(width, -1)
    out_weight = attention_all.build(1).reshape(width // 2, width)
    expand_weight = expand_all.build(0).reshape(width, 2 * quarter)
    contract_weight = contract_all.build(0).reshape(width, quarter)

    def positions_of(sub_place, core_place):
        source = jnp.arange(count, dtype=jnp.int32)[:, None] * local
        inner = sub_place * 2 * piece + core_place * piece + jnp.arange(piece, dtype=jnp.int32)[None]
        return (source + inner).reshape(half)

    query_place = jnp.concatenate([positions_of(sub, c), positions_of(sub, 1 - c)])
    key_place = jnp.concatenate(
        [positions_of((sub - step) % split, side) for step in range(split) for side in (c, 1 - c)]
    )
    totals = (prompt_length + response_length).astype(F32)
    total = take(pair(totals, swap(totals, "core"), c).reshape(rows), z // split, 0).astype(jnp.int32)
    allowed = (key_place[None] <= query_place[:, None]) & (key_place[None] < total)
    bias = jnp.where(allowed, 0.0, -1e30).astype(F32)
    frequency = 10000.0 ** (-jnp.arange(HEAD_DIM // 2).astype(F32) / (HEAD_DIM // 2))
    angles = query_place.astype(F32)[:, None] * frequency[None]
    cosine = jnp.concatenate([jnp.cos(angles)] * 2, axis=1)
    sine = jnp.concatenate([-jnp.sin(angles), jnp.sin(angles)], axis=1)

    heads = width // 2 // HEAD_DIM
    rows_both = tokens_both.astype(F32)
    first = rms(rows_both).astype(BF)
    magnitude = by_core(attention_magnitude[:3])[0].reshape(1, -1)
    qkv_t, qkv_p, qkv_norm = qkv_forward(first, qkv_weight, magnitude, cosine, sine)

    def share(a, step):
        perm = [(i, (i // split) * split + (i % split + step) % split) for i in range(count)]
        return lax.ppermute(a, "seq", perm)

    if split == 1:
        kv, offsets = qkv_p, (heads, 2 * heads)
    else:
        own_kv = qkv_p[:, heads * HEAD_DIM :]
        kv = jnp.concatenate([own_kv] + [share(own_kv, step) for step in range(1, split)], axis=0)
        offsets = (0, heads)
    (mixed,) = attention_call(
        attend_kernel, "attend", heads, qkv_p, kv, offsets, [], bias, [(2 * half, BF)]
    )

    def core_scatter(partial):
        return partial[:half].astype(F32) + swap(partial[half:].astype(BF), "core").astype(F32)

    def core_join(own):
        return jnp.concatenate([own, swap(own, "core")], axis=0)

    out_square = jnp.sum(out_weight.astype(F32) ** 2, axis=0, keepdims=True)
    out_norm = jnp.sqrt(out_square + swap(out_square, "core"))
    out_scale = attention_magnitude[3:] / out_norm
    out_t = core_scatter(mm(mixed, out_weight))
    rows_own = tokens_own.astype(F32)
    middle = rows_own + out_t * out_scale
    second_own = rms(middle).astype(BF)
    second_near = core_join(second_own)
    second_own_far = swap(second_own, "xx")
    second_far = core_join(second_own_far)

    cotangent_own = cotangent_moved.arrays[0].reshape(half, width)
    grad_own = cotangent_own.astype(F32)
    contract_square = jnp.sum(contract_weight.astype(F32) ** 2, axis=1)[None]
    contract_square = contract_square + swap(contract_square, "core")
    contract_norm = jnp.sqrt(contract_square + swap(contract_square, "xx"))
    contract_scale = contract_magnitude[None] / contract_norm
    scaled = (grad_own * contract_scale).astype(BF)
    scaled_near = core_join(scaled)
    scaled_far = core_join(swap(scaled, "xx"))
    expand_norm = jnp.sqrt(jnp.sum(expand_weight.astype(F32) ** 2, axis=0, keepdims=True))
    expand_scale = by_quarter(expand_magnitude).reshape(1, -1) / expand_norm
    back_far, out_far, dt_far, hidden_far, dm_far = feed_forward_back(
        second_far, scaled_far, expand_weight, contract_weight, expand_scale
    )
    back_near, out_near, dt_near, hidden_near, dm_near = feed_forward_back(
        second_near, scaled_near, expand_weight, contract_weight, expand_scale
    )

    def quad_scatter(near, far):
        far_sum = core_scatter(far).astype(BF)
        return core_scatter(near) + swap(far_sum, "xx").astype(F32)

    second_grad = quad_scatter(back_near, back_far)
    middle_grad = grad_own + rms_back(middle, second_grad)
    contract_t = quad_scatter(out_near, out_far)
    output_own = (middle + contract_t * contract_scale).astype(BF)

    out_dm = jnp.sum(middle_grad * out_t, axis=0, keepdims=True) / out_norm
    out_dt = core_join((middle_grad * out_scale).astype(BF))
    mixed_grad = nt(out_dt, out_weight).astype(BF)
    keys = 2 * half * split
    members = lambda a: a.reshape(3, 1, width // 2)
    qkv_scale = magnitude / qkv_norm

    def reunite(a):
        parts = a.reshape(split, 2 * half, -1)
        total = parts[0]
        for step in range(1, split):
            total = total + share(parts[step].astype(BF), -step).astype(F32)
        return total

    if split > 1:
        dq, dk, dv = attention_call(
            attend_back_kernel, "attend_back", heads, qkv_p, kv, offsets, [mixed_grad], bias,
            [(2 * half, F32), (keys, F32), (keys, F32)],
        )
        grads = jnp.concatenate([dq, reunite(dk), reunite(dv)], axis=1)
        qkv_dt, qkv_dm = turn_back(grads, qkv_t, qkv_scale, 1.0 / qkv_norm, cosine, sine)
        qkv_dm = members(qkv_dm)
    else:
        qkv_dt, qkv_dm = attend_back_turn(
            heads, qkv_p, mixed_grad, bias, qkv_t, members(qkv_scale), members(1.0 / qkv_norm), cosine, sine
        )
    core_up = by_core(attention_up[:3])[0]
    downs = attention_down[:3].transpose(0, 2, 1).reshape(3 * rank, width).astype(BF)
    low = nt(downs, first).astype(BF).reshape(3, rank, 2 * half)
    cross = mm(downs, qkv_weight)
    cross = jnp.stack(
        [cross[i * rank : (i + 1) * rank, i * width // 2 : (i + 1) * width // 2] for i in range(3)]
    )
    first_part, qkv_shared, qkv_core = qkv_back(
        qkv_dt, qkv_weight, first, low, core_up, cross, members(qkv_scale), members(qkv_norm), qkv_dm
    )
    first_grad = core_scatter(first_part)
    tokens_grad_own = middle_grad + rms_back(rows_own, first_grad)

    gate_up = jnp.stack([by_quarter(expand_up[i]) for i in range(2)])
    feed_downs = expand_down.transpose(0, 2, 1).reshape(2 * rank, width).astype(BF)
    contract_rows = take(contract_down.T.reshape(rank, 4, quarter), 2 * x + c, 1).astype(BF)
    expand_dm = (dm_near + dm_far) / expand_norm
    contract_dm = jnp.sum(grad_own * contract_t, axis=0, keepdims=True) / contract_norm
    contract_sum = contract_dm + swap(contract_dm, "core")
    contract_sum = contract_sum + swap(contract_sum, "xx")
    part = feed_adapter(
        second_far, scaled_far, dt_far, hidden_far, feed_downs, gate_up, contract_rows, contract_up
    )
    pulls = (-expand_scale * expand_dm / expand_norm, -contract_scale * contract_sum / contract_norm)
    feed_words, feed_quad_words = feed_adapter(
        second_near, scaled_near, dt_near, hidden_near, feed_downs, gate_up, contract_rows, contract_up,
        (*part, expand_weight, contract_weight, pulls[0], expand_dm, pulls[1], contract_dm),
    )
    flat = lambda a: a.reshape(-1, WORD)
    feed_shared, _, feed_quads = reduce_all(flat(feed_words), None, flat(feed_quad_words))

    out_rows = by_core(attention_down[3].T)[0].astype(BF)
    out_words, out_core_words = out_adapter(
        out_dt, out_weight, mixed, out_rows, attention_up[3], out_scale, out_norm, out_dm + swap(out_dm, "core"),
        out_dm,
    )
    dm_words = jnp.pad(qkv_dm[:, 0], ((0, 5), (0, 0)))
    dm_words = jnp.stack([dm_words[:, i : i + WORD] for i in range(0, width // 2, WORD)])
    shared = jnp.concatenate([flat(qkv_shared), flat(out_words)])
    cores = jnp.concatenate([flat(qkv_core), flat(dm_words), flat(out_core_words)])
    attention_shared, attention_cores, _ = reduce_all(shared, cores, None)

    def interleave(parts):
        shaped = [p.reshape(p.shape[0], blocks, 1, -1) for p in parts]
        return jnp.concatenate(shaped, axis=2).reshape(parts[0].shape[0], -1)

    used = flat(qkv_shared).shape[0]
    qkv_down_all = unpacked(attention_shared[:used].reshape(qkv_shared.shape), width)
    out_all = unpacked(attention_shared[used : used + flat(out_words).shape[0]].reshape(out_words.shape), width)
    core_parts = []
    for side in range(2):
        start, parts = 0, []
        for words in (qkv_core, dm_words, out_core_words):
            used = flat(words).shape[0]
            parts.append(unpacked(attention_cores[side, start : start + used].reshape(words.shape), width // 2))
            start += used
        core_parts.append(parts)
    qkv_up_all, qkv_dm_all, out_down_all = (interleave([core_parts[0][i], core_parts[1][i]]) for i in range(3))
    attention_down_grad = (
        jnp.concatenate([qkv_down_all, out_down_all]).reshape(4, rank, width).transpose(0, 2, 1)
    )
    attention_up_grad = jnp.concatenate([qkv_up_all, out_all[:rank]]).reshape(4, rank, width)
    attention_magnitude_grad = jnp.concatenate([qkv_dm_all[:3], out_all[rank : rank + 1]])

    feed_all = unpacked(feed_shared[: flat(feed_words).shape[0]].reshape(feed_words.shape), width)
    quad_all = jnp.concatenate(
        [unpacked(feed_quads[i, j].reshape(feed_quad_words.shape), quarter) for i in range(2) for j in range(2)],
        axis=1,
    )

    def restore(own):
        joined = own.reshape(count, piece, width)
        joined = lax.all_to_all(joined, "seq", 0, 0, tiled=True)
        shaped = joined.reshape(2, own_rows, split, piece, width)
        kept, sent = take(shaped, c, 0), take(shaped, 1 - c, 0)
        return pair(kept, swap(sent, "core"), c, axis=2).reshape(own_rows, local, width)

    layer_output = restore(output_own)
    tokens_grad = restore(tokens_grad_own.astype(BF)).astype(F32)
    return (
        layer_output,
        tokens_grad,
        attention_down_grad,
        attention_up_grad,
        attention_magnitude_grad,
        feed_all[: 2 * rank].reshape(2, rank, width).transpose(0, 2, 1),
        quad_all[: 2 * rank].reshape(2, rank, hidden_size),
        quad_all[3 * rank : 3 * rank + 2],
        quad_all[2 * rank : 3 * rank].T,
        feed_all[2 * rank : 3 * rank],
        feed_all[3 * rank],
    )


def solution(mesh):
    devices = mesh.devices
    chips = devices.shape[0] // 2
    fine = Mesh(devices.reshape(chips // 2, 2, 2, devices.shape[1]), ALL)
    dp = ("yy", "xx", "core")
    every = ("yy", "xx", "core", "seq")
    placed = (
        P(dp, "seq", None),
        P(dp, "seq", None),
        P(None, every, None),
        P(None, every, None),
        P(None, every),
        P(),
        P(),
        P(),
        P(),
        P(),
        P(),
        P(),
        P(),
        P(),
        P(dp),
        P(dp),
    )
    return jax.shard_map(
        body,
        mesh=fine,
        in_specs=placed,
        out_specs=(P(dp, "seq", None), P(dp, "seq", None)) + (P(),) * 9,
        check_vma=False,
    )
```

time: 1550 us -> 801 us (0.52)
  waiting for transfers between devices: 828 us -> 290 us
  matrix products: 485 us -> 29.5 us
  Pallas kernels: 0 us -> 146 us
  starting transfers between devices: 0.36 us -> 95.1 us
  local copies, waits for them, and re-layouts: 96.7 us -> 156 us
  blocking collectives: 27.3 us -> 0 us
  other arithmetic: 94.3 us -> 73.6 us
    all_gather x7 -> x0, waiting for transfers between devices: 553 us -> none  [the longest x1 213 us: body(): lax.all_gather(expand_base, ('dp', 'seq'), axis=1, tiled=True)]
    dot_general x121 -> x7, matrix products: 485 us -> 29.5 us  [the longest x4 19.3 us: mm(): return lax.dot_general(a, b, (dims, ((), ())), preferred_element_type=F32)]
    psum x2 -> x0, waiting for transfers between devices: 273 us -> none  [body(): lax.psum((attention_down_grad, attention_up_grad, attention_magnitude_gra...]
    ppermute x0 -> x101, waiting for transfers between devices: none -> 267 us  [the longest x44 176 us: shift(): return lax.ppermute(a, name, [(i, (i + step) % size) for i in range(size)])]
    pallas_call x0 -> x9, Pallas kernels: none -> 146 us  [the longest x2 57.2 us: feed_forward_back(): pl.pallas_call(feed_kernel, grid=(rows // block,), in_specs=[pl.BlockSpec...]
    ppermute x0 -> x101, starting transfers between devices: none -> 76.2 us  [the longest x44 43.4 us: shift(): return lax.ppermute(a, name, [(i, (i + step) % size) for i in range(size)])]
    dynamic_update_slice x2 -> x57, local copies, waits for them, and re-layouts: 0.02 us -> 74.4 us  [the longest x47 70.4 us: build(): lax.dynamic_update_slice(buffer, block, [jnp.int32(s) for s in start])]
    dot_general x3 -> x0, other arithmetic: 37.9 us -> none  [prepare_weights(): jnp.einsum('io,io->o', frozen_weight, frozen_weight, preferred_element_ty...]
  transfers between devices with their start and end apart: 9 -> 105, of which waited for: 7 -> 42; matrix products, arithmetic and copies ran while one was open for 32% -> 29% of each run, Pallas kernels for 0% -> 12%
where the time goes in v1:
time: 801 us; the launch traced here: 794 us
  waiting for transfers between devices  290 us (36%)
  local copies, waits for them, and re-layouts  156 us (19%)
  Pallas kernels  146 us (18%)
  starting transfers between devices  95.1 us (12%)
  other arithmetic  73.6 us (9%)
  matrix products  29.5 us (4%)
    ppermute x44, waiting for transfers between devices, shift(): return lax.ppermute(a, name, [(i, (i + step) % size) for i in range(size)])  176 us
    ppermute x57, waiting for transfers between devices, swap(): return lax.ppermute(a, name, [(0, 1), (1, 0)])  90.2 us
    dynamic_update_slice x47, local copies, waits for them, and re-layouts, build(): lax.dynamic_update_slice(buffer, block, [jnp.int32(s) for s in start])  70.4 us
    pallas_call x2, Pallas kernels, feed_forward_back(): pl.pallas_call(feed_kernel, grid=(rows // block,), in_specs=[pl.BlockSpec...  57.2 us
    ppermute x44, starting transfers between devices, shift(): return lax.ppermute(a, name, [(i, (i + step) % size) for i in range(size)])  43.4 us
    ppermute x57, starting transfers between devices, swap(): return lax.ppermute(a, name, [(0, 1), (1, 0)])  32.8 us
    pallas_call x2, Pallas kernels, feed_adapter(): pl.pallas_call(feed_adapter_kernel, out_shape=[jax.ShapeDtypeStruct(shape...  29.3 us
    all_to_all x2, waiting for transfers between devices, restore(): joined = lax.all_to_all(joined, 'seq', 0, 0, tiled=True)  23.3 us
  transfers between devices with their start and end apart: 105, of which 42 were waited for; matrix products, arithmetic and copies ran while one was open for 29% of the time, Pallas kernels for 12%

profile of v1, /device:TPU:0, one launch (start us, length us, event | category | flops | bytes accessed | tf_op | source)
XLA Modules:
  0.0 793.6 jit_solution(9405071578705577961)
XLA Ops:
  0.7 3.6 fusion.7
  5.2 2.9 collective-permute-start.12
  15.7 2.5 fusion.3
  24.3 4.9 dynamic-slice_reduce_fusion.1
  31.3 4.0 fusion.1
  38.4 2.5 broadcast_in_dim.100
  45.7 6.2 broadcast_in_dim.97
  63.3 22.6 %collective-permute-done.6 = bf16[64,2048]{1,0:T(8,128)(2,1)S(1)} collective-permute-done((bf16[64,2048]{1,0:T(8,128)(2,1)}, bf16[64,2048]{1,0:T(8,128)(2,1)S(1)}, u32[]{:S(2)}, u32[]{:S(2)}) %collective-permute-start.6) | collective-permute-done | bytes 262176 | tf_op jit(solution)/shard_map/ppermute | solution.py:41
  93.3 3.8 collective-permute-done.7
  97.1 15.3 %collective-permute-done.5 = bf16[2,64,3072]{2,1,0:T(8,128)(2,1)} collective-permute-done((bf16[2,64,3072]{2,1,0:T(8,128)(2,1)S(1)}, bf16[2,64,3072]{2,1,0:T(8,128)(2,1)}, u32[]{:S(2)}, u32[]{:S(2)}) %collective-permute-start.5) | collective-permute-done | bytes 786464 | tf_op jit(solution)/shard_map/ppermute | solution.py:41
  112.4 5.6 all-to-all-start
  125.0 15.7 %collective-permute-done.13 = bf16[2,64,3072]{2,1,0:T(8,128)(2,1)} collective-permute-done((bf16[2,64,3072]{2,1,0:T(8,128)(2,1)}, bf16[2,64,3072]{2,1,0:T(8,128)(2,1)}, u32[]{:S(2)}, u32[]{:S(2)}) %collective-permute-start.13) | collective-permute-done | bytes 786464 | tf_op jit(solution)/shard_map/ppermute | solution.py:41
  141.8 5.6 broadcast_in_dim.105
  150.7 5.7 collective-permute-done.20
  162.0 3.7 collective-permute-done.16
  174.9 2.5 bitcast_dynamic-update-slice_fusion.17
  177.4 3.2 broadcast_in_dim.103
  188.7 5.4 collective-permute-done.21
  196.5 3.5 all-to-all-start.1
  200.0 2.6 bitcast_dynamic-update-slice_fusion.6
  202.6 9.4 %collective-permute-done.30 = bf16[2,2,64,1408]{3,2,1,0:T(8,128)(2,1)} collective-permute-done((bf16[2,2,64,1408]{3,2,1,0:T(8,128)(2,1)}, bf16[2,2,64,1408]{3,2,1,0:T(8,128)(2,1)}, u32[]{:S(2)}, u32[]{:S(2)}) %collective-permute-start.30) | collective-permute-done | bytes 720928 | tf_op jit(solution)/shard_map/ppermute | solution.py:41
  216.1 2.6 bitcast_dynamic-update-slice_fusion.5
  221.9 16.5 %collective-permute-done.22 = bf16[2,64,3072]{2,1,0:T(8,128)(2,1)} collective-permute-done((bf16[2,64,3072]{2,1,0:T(8,128)(2,1)}, bf16[2,64,3072]{2,1,0:T(8,128)(2,1)}, u32[]{:S(2)}, u32[]{:S(2)}) %collective-permute-start.22) | collective-permute-done | bytes 786464 | tf_op jit(solution)/shard_map/ppermute | solution.py:41
  250.8 15.5 %collective-permute-done.32 = bf16[2,2,64,2816]{3,2,1,0:T(8,128)(2,1)S(1)} collective-permute-done((bf16[2,2,64,2816]{3,2,1,0:T(8,128)(2,1)}, bf16[2,2,64,2816]{3,2,1,0:T(8,128)(2,1)S(1)}, u32[]{:S(2)}, u32[]{:S(2)}) %collective-permute-start.32) | collective-permute-done | bytes 1441824 | tf_op jit(solution)/shard_map/ppermute | solution.py:41
  273.7 9.2 %collective-permute-done.38 = bf16[2,2,64,1408]{3,2,1,0:T(8,128)(2,1)S(1)} collective-permute-done((bf16[2,2,64,1408]{3,2,1,0:T(8,128)(2,1)}, bf16[2,2,64,1408]{3,2,1,0:T(8,128)(2,1)S(1)}, u32[]{:S(2)}, u32[]{:S(2)}) %collective-permute-start.38) | collective-permute-done | bytes 720928 | tf_op jit(solution)/shard_map/ppermute | solution.py:41
  288.0 13.3 %collective-permute-done.34 = bf16[64,2048]{1,0:T(8,128)(2,1)S(1)} collective-permute-done((bf16[64,2048]{1,0:T(8,128)(2,1)}, bf16[64,2048]{1,0:T(8,128)(2,1)S(1)}, u32[]{:S(2)}, u32[]{:S(2)}) %collective-permute-start.34) | collective-permute-done | bytes 262176 | tf_op jit(solution)/shard_map/ppermute | solution.py:41
  308.3 2.6 bitcast_dynamic-update-slice_fusion.3
  318.8 3.1 multiply_reduce_fusion.2
  324.6 21.1 %collective-permute-done.48 = bf16[2,2,64,1408]{3,2,1,0:T(8,128)(2,1)S(1)} collective-permute-done((bf16[2,2,64,1408]{3,2,1,0:T(8,128)(2,1)S(1)}, bf16[2,2,64,1408]{3,2,1,0:T(8,128)(2,1)S(1)}, u32[]{:S(2)}, u32[]{:S(2)}) %collective-permute-start.48) | collective-permute-done | bytes 720928 | tf_op jit(solution)/shard_map/ppermute | solution.py:41
  348.7 14.2 %qkv_forward.1 = (bf16[512,3072]{1,0:T(8,128)(2,1)S(1)}, bf16[512,3072]{1,0:T(8,128)(2,1)S(1)}, f32[1,3072]{1,0:T(1,128)S(1)}) custom-call(bf16[512,2048]{1,0:T(8,128)(2,1)S(1)} %copy-done.6, bf16[2048,3072]{1,0:T(8,128)(2,1)} %bitcast.60.v_ref, f32[1,3072]{1,0:T(1,128)S(1)} %bitcast.537, f32[512,128]{1,0:T(8,128)S(1)} %copy-done.12, ...), custom_call_target="tpu_custom_call" | custom-call | flops 6442450944 | bytes 22020096 | tf_op jit(solution)/shard_map/qkv_forward/pallas_call | solution.py:154
  365.2 8.6 %attend.1.u_ref = bf16[512,1024]{1,0:T(8,128)(2,1)S(1)} custom-call(bf16[512,3072]{1,0:T(8,128)(2,1)S(1)} %get-tuple-element.153.q_ref.k_ref.v_ref, bf16[512,3072]{1,0:T(8,128)(2,1)S(1)} %get-tuple-element.153.q_ref.k_ref.v_ref, bf16[512,3072]{1,0:T(8,128)(2,1)S(1)} %get-tuple-element.153.q_ref.k_ref.v_ref, f32[512,512]{1,0:T(8,128)S(1)} %copy-done.4), custom_call_target="tpu_custom_call" | custom-call | flops 1073741824 | bytes 4194304 | tf_op jit(solution)/shard_map/attend/pallas_call | solution.py:215
  375.8 3.9 multiply_reduce_fusion.1
  379.9 4.5 fusion.64
  387.0 2.7 bitcast_dynamic-update-slice_fusion.2
  394.4 2.6 bitcast_dynamic-update-slice_fusion.1
  397.3 19.9 %collective-permute-done.60 = bf16[256,2048]{1,0:T(8,128)(2,1)S(1)} collective-permute-done((bf16[256,2048]{1,0:T(8,128)(2,1)S(1)}, bf16[256,2048]{1,0:T(8,128)(2,1)S(1)}, u32[]{:S(2)}, u32[]{:S(2)}) %collective-permute-start.60) | collective-permute-done | bytes 1048608 | tf_op jit(solution)/shard_map/ppermute | solution.py:36
  419.8 17.8 %collective-permute-done.58 = bf16[256,2048]{1,0:T(8,128)(2,1)S(1)} collective-permute-done((bf16[256,2048]{1,0:T(8,128)(2,1)S(1)}, bf16[256,2048]{1,0:T(8,128)(2,1)S(1)}, u32[]{:S(2)}, u32[]{:S(2)}) %collective-permute-start.58) | collective-permute-done | bytes 1048608 | tf_op jit(solution)/shard_map/ppermute | solution.py:36
  438.8 6.6 multiply_reduce_fusion
  445.5 2.8 pad_maximum_fusion.1.h_ref
  453.8 28.5 %feed_forward_back.3 = (bf16[512,2048]{1,0:T(8,128)(2,1)}, bf16[512,2048]{1,0:T(8,128)(2,1)}, bf16[512,2816]{1,0:T(8,128)(2,1)}, bf16[512,1408]{1,0:T(8,128)(2,1)}, f32[1,2816]{1,0:T(1,128)}) custom-call(bf16[512,2048]{1,0:T(8,128)(2,1)} %copy-done.57, bf16[512,2048]{1,0:T(8,128)(2,1)} %copy-done.56, bf16[2048,2816]{1,0:T(8,128)(2,1)} %bitcast.118.expand_ref.refs_2_, ...), custom_call_target="tpu_custom_call" | custom-call | flops 17716740096 | bytes 30277632 | tf_op jit(solution)/shard_map/feed_forward_back/pallas_call | solution.py:426
  482.3 2.5 slice.350
  486.4 28.7 %feed_forward_back.2 = (bf16[512,2048]{1,0:T(8,128)(2,1)}, bf16[512,2048]{1,0:T(8,128)(2,1)}, bf16[512,2816]{1,0:T(8,128)(2,1)}, bf16[512,1408]{1,0:T(8,128)(2,1)}, f32[1,2816]{1,0:T(1,128)}) custom-call(bf16[512,2048]{1,0:T(8,128)(2,1)} %pad_maximum_fusion.1.h_ref, bf16[512,2048]{1,0:T(8,128)(2,1)} %pad_maximum_fusion.2.g_ref, ...), custom_call_target="tpu_custom_call" | custom-call | flops 17716740096 | bytes 30277632 | tf_op jit(solution)/shard_map/feed_forward_back/pallas_call | solution.py:426
  515.1 2.5 slice.348
  538.9 8.0 %collective-permute-done.67 = bf16[256,2048]{1,0:T(8,128)(2,1)} collective-permute-done((bf16[256,2048]{1,0:T(8,128)(2,1)}, bf16[256,2048]{1,0:T(8,128)(2,1)}, u32[]{:S(2)}, u32[]{:S(2)}) %collective-permute-start.67) | collective-permute-done | bytes 1048608 | tf_op jit(solution)/shard_map/ppermute | solution.py:36
  549.4 19.6 %collective-permute-done.63 = bf16[256,2048]{1,0:T(8,128)(2,1)} collective-permute-done((bf16[256,2048]{1,0:T(8,128)(2,1)}, bf16[256,2048]{1,0:T(8,128)(2,1)}, u32[]{:S(2)}, u32[]{:S(2)}) %collective-permute-start.63) | collective-permute-done | bytes 1048608 | tf_op jit(solution)/shard_map/ppermute | solution.py:36
  569.0 6.0 fusion.13
  577.9 9.2 %feed_adapter.2 = (f32[48,2048]{1,0:T(8,128)}, f32[48,1408]{1,0:T(8,128)}) custom-call(bf16[512,2048]{1,0:T(8,128)(2,1)} %copy-done.57, bf16[512,2048]{1,0:T(8,128)(2,1)} %copy-done.56, bf16[512,2816]{1,0:T(8,128)(2,1)} %get-tuple-element.191.dt_ref, bf16[512,1408]{1,0:T(8,128)(2,1)} %get-tuple-element.192.hidden_ref, bf16[32,2048]{1,0:T(8,128)(2,1)} %bitcast.591, ...), custom_call_target="tpu_custom_call" | custom-call | flops 4294967296 | bytes 8388608 | tf_op jit(solution)/shard_map/feed_adapter/pallas_call | solution.py:508
  587.8 20.1 %feed_adapter.3 = (f32[4,56,512]{2,1,0:T(8,128)}, f32[3,56,512]{2,1,0:T(8,128)}) custom-call(bf16[512,2048]{1,0:T(8,128)(2,1)} %pad_maximum_fusion.1.h_ref, bf16[512,2048]{1,0:T(8,128)(2,1)} %pad_maximum_fusion.2.g_ref, bf16[512,2816]{1,0:T(8,128)(2,1)} %get-tuple-element.189.dt_ref, bf16[512,1408]{1,0:T(8,128)(2,1)} %get-tuple-element.190.hidden_ref, ...), custom_call_target="tpu_custom_call" | custom-call | flops 4294967296 | bytes 8388608 | tf_op jit(solution)/shard_map/feed_adapter/pallas_call | solution.py:508
  613.6 2.6 convolution_convert_fusion.1
  616.2 2.5 collective-permute-done.88
  619.2 7.0 convolution_bitcast_fusion
  627.2 3.5 collective-permute-start.92
  633.1 2.8 collective-permute-done.91
  650.0 5.0 all-to-all-start.2
  660.0 5.2 convolution_convert_fusion.g_ref
  665.2 14.3 %attend_back_turn.1 = (bf16[3,512,1024]{2,1,0:T(8,128)(2,1)S(1)}, f32[3,1,1024]{2,1,0:T(1,128)S(1)}) custom-call(bf16[512,3072]{1,0:T(8,128)(2,1)} %copy-done.2, bf16[512,3072]{1,0:T(8,128)(2,1)} %copy-done.2, bf16[512,3072]{1,0:T(8,128)(2,1)} %copy-done.2, bf16[512,1024]{1,0:T(8,128)(2,1)S(1)} %convolution_convert_fusion.g_ref, f32[512,512]{1,0:T(8,128)S(1)} %copy-done.5, ...), custom_call_target="tpu_custom_call" | custom-call | flops 2684354560 | bytes 10485760 | tf_op jit(solution)/shard_map/attend_back_turn/pallas_call | solution.py:251
  682.9 5.2 out_adapter.1
  688.2 16.6 %qkv_back.1 = (bf16[512,2048]{1,0:T(8,128)(2,1)S(1)}, f32[4,48,512]{2,1,0:T(8,128)S(1)}, f32[2,48,512]{2,1,0:T(8,128)S(1)}) custom-call(bf16[3,512,1024]{2,1,0:T(8,128)(2,1)} %copy-done.25, bf16[2048,3072]{1,0:T(8,128)(2,1)} %bitcast.60.v_ref, bf16[512,2048]{1,0:T(8,128)(2,1)S(1)} %copy-done.7, bf16[3,16,512]{2,1,0:T(8,128)(2,1)S(1)} %bitcast.539, ...), custom_call_target="tpu_custom_call" | custom-call | flops 6442450944 | bytes 12582912 | tf_op jit(solution)/shard_map/qkv_back/pallas_call | solution.py:323
  709.3 6.5 collective-permute-done.73
  716.9 5.3 collective-permute-done.74
  732.9 2.9 collective-permute-start.79
  750.0 4.3 collective-permute-done.82
  756.7 4.7 all-to-all-start.3
  764.4 23.3 %all-to-all-done.3 = bf16[4,64,2048]{2,1,0:T(8,128)(2,1)S(1)} async-done(((bf16[4,64,2048]{2,1,0:T(8,128)(2,1)}), bf16[4,64,2048]{2,1,0:T(8,128)(2,1)S(1)}, u32[]{:S(2)}, u32[]{:S(2)}) %all-to-all-start.3) | async-done | bytes 1048608 | tf_op jit(solution)/shard_map/all_to_all | solution.py:924
  (617 shorter events, 254.2 us)
Async XLA Ops:
  5.2 55.4 %collective-permute-start.12 = (bf16[64,2048]{1,0:T(8,128)(2,1)}, bf16[64,2048]{1,0:T(8,128)(2,1)}, u32[]{:S(2)}, u32[]{:S(2)}) collective-permute-start(bf16[64,2048]{1,0:T(8,128)(2,1)} %slice_bitcast_fusion.1), channel_id=1, source_target_pairs={{0,8},{8,0},{1,9},{9,1},{2,10},{10,2},{3,11},{11,3},{4,12},{12,4},... | collective-permute-start | bytes 786440 | tf_op jit(solution)/shard_map/ppermute | solution.py:36
  8.1 77.8 %collective-permute-start.10 = (bf16[64,2048]{1,0:T(8,128)(2,1)}, bf16[64,2048]{1,0:T(8,128)(2,1)}, u32[]{:S(2)}, u32[]{:S(2)}) collective-permute-start(bf16[64,2048]{1,0:T(8,128)(2,1)} %slice_bitcast_fusion.1), channel_id=1, source_target_pairs={{0,16},{16,0},{1,17},{17,1},{2,18},{18,2},{3,19},{19,3},{4,20},{20... | collective-permute-start | bytes 786440 | tf_op jit(solution)/shard_map/ppermute | solution.py:41
  9.6 32.0 %collective-permute-start.40 = (f32[2]{0:T(128)S(1)}, f32[2]{0:T(128)S(1)}, u32[]{:S(2)}, u32[]{:S(2)}) collective-permute-start(f32[2]{0:T(128)S(1)} %add_convert_fusion.3), channel_id=1, source_target_pairs={{0,4},{4,0},{1,5},{5,1},{2,6},{6,2},{3,7},{7,3},{8,12},{12,8},{9,1... | collective-permute-start | bytes 32 | tf_op jit(solution)/shard_map/ppermute | solution.py:36
  10.6 42.3 %collective-permute-start.28 = (bf16[2,1,64,2048]{3,2,0,1:T(8,128)(2,1)}, bf16[2,1,64,2048]{3,2,0,1:T(8,128)(2,1)}, u32[]{:S(2)}, u32[]{:S(2)}) collective-permute-start(bf16[2,1,64,2048]{3,2,0,1:T(8,128)(2,1)} %dynamic-slice_bitcast_fusion.3), channel_id=1, source_target_pairs={{0,4},{4,0},{1,5},{5,1},{2,6},{6,2},{3,7},{7,3},{8,12},{12,8},{9,1... | collective-permute-start | bytes 1572872 | tf_op jit(solution)/shard_map/ppermute | solution.py:36
  12.9 43.0 %collective-permute-start.2 = (bf16[2,1,64,2048]{3,2,0,1:T(8,128)(2,1)}, bf16[2,1,64,2048]{3,2,0,1:T(8,128)(2,1)}, u32[]{:S(2)}, u32[]{:S(2)}) collective-permute-start(bf16[2,1,64,2048]{3,2,0,1:T(8,128)(2,1)} %dynamic-slice_bitcast_fusion.4), channel_id=1, source_target_pairs={{0,4},{4,0},{1,5},{5,1},{2,6},{6,2},{3,7},{7,3},{8,12},{12,8},{9,1... | collective-permute-start | bytes 1572872 | tf_op jit(solution)/shard_map/ppermute | solution.py:36
  52.9 34.4 %collective-permute-start.9 = (bf16[2,64,3072]{2,1,0:T(8,128)(2,1)}, bf16[2,64,3072]{2,1,0:T(8,128)(2,1)}, u32[]{:S(2)}, u32[]{:S(2)}) collective-permute-start(bf16[2,64,3072]{2,1,0:T(8,128)(2,1)} %pad_maximum_fusion.14), channel_id=1, source_target_pairs={{0,16},{16,0},{1,17},{17,1},{2,18},{18,2},{3,19},{19,3},{4,20},{20... | collective-permute-start | bytes 2359304 | tf_op jit(solution)/shard_map/ppermute | solution.py:41
  55.9 31.4 %collective-permute-start.11 = (bf16[2,64,3072]{2,1,0:T(8,128)(2,1)}, bf16[2,64,3072]{2,1,0:T(8,128)(2,1)S(1)}, u32[]{:S(2)}, u32[]{:S(2)}) collective-permute-start(bf16[2,64,3072]{2,1,0:T(8,128)(2,1)} %pad_maximum_fusion.14), channel_id=1, source_target_pairs={{0,8},{8,0},{1,9},{9,1},{2,10},{10,2},{3,11},{11,3},{4,12},{12,4},... | collective-permute-start | bytes 2359304 | tf_op jit(solution)/shard_map/ppermute | solution.py:36
  58.4 31.0 %collective-permute-start.4 = (bf16[2,64,3072]{2,1,0:T(8,128)(2,1)}, bf16[2,64,3072]{2,1,0:T(8,128)(2,1)S(1)}, u32[]{:S(2)}, u32[]{:S(2)}) collective-permute-start(bf16[2,64,3072]{2,1,0:T(8,128)(2,1)} %pad_maximum_fusion.14), channel_id=1, source_target_pairs={{0,1},{1,2},{2,3},{3,0},{4,5},{5,6},{6,7},{7,4},{8,9},{9,10},{10,1... | collective-permute-start | bytes 2359304 | tf_op jit(solution)/shard_map/ppermute | solution.py:41
  60.5 25.4 %collective-permute-start.6 = (bf16[64,2048]{1,0:T(8,128)(2,1)}, bf16[64,2048]{1,0:T(8,128)(2,1)S(1)}, u32[]{:S(2)}, u32[]{:S(2)}) collective-permute-start(bf16[64,2048]{1,0:T(8,128)(2,1)} %slice_bitcast_fusion.1), channel_id=1, source_target_pairs={{0,1},{1,2},{2,3},{3,0},{4,5},{5,6},{6,7},{7,4},{8,9},{9,10},{10,1... | collective-permute-start | bytes 786440 | tf_op jit(solution)/shard_map/ppermute | solution.py:41
  85.9 32.1 %collective-permute-start.1 = (bf16[2,64,3,1408]{3,1,2,0:T(8,128)(2,1)}, bf16[2,64,3,1408]{3,1,2,0:T(8,128)(2,1)}, u32[]{:S(2)}, u32[]{:S(2)}) collective-permute-start(bf16[2,64,3,1408]{3,1,2,0:T(8,128)(2,1)} %fusion.21), channel_id=1, source_target_pairs={{0,8},{8,0},{1,9},{9,1},{2,10},{10,2},{3,11},{11,3},{4,12},{12,4},... | collective-permute-start | bytes 3244040 | tf_op jit(solution)/shard_map/ppermute | solution.py:36
  87.3 72.8 %collective-permute-start.18 = (bf16[64,2048]{1,0:T(8,128)(2,1)}, bf16[64,2048]{1,0:T(8,128)(2,1)}, u32[]{:S(2)}, u32[]{:S(2)}) collective-permute-start(bf16[64,2048]{1,0:T(8,128)(2,1)} %collective-permute-done.10), channel_id=1, source_target_pairs={{0,8},{8,0},{1,9},{9,1},{2,10},{10,2},{3,11},{11,3},{4,12},{12,4},... | collective-permute-start | bytes 786440 | tf_op jit(solution)/shard_map/ppermute | solution.py:36
  88.0 72.7 %collective-permute-start.17 = (bf16[2,64,3072]{2,1,0:T(8,128)(2,1)}, bf16[2,64,3072]{2,1,0:T(8,128)(2,1)}, u32[]{:S(2)}, u32[]{:S(2)}) collective-permute-start(bf16[2,64,3072]{2,1,0:T(8,128)(2,1)} %collective-permute-done.9), channel_id=1, source_target_pairs={{0,8},{8,0},{1,9},{9,1},{2,10},{10,2},{3,11},{11,3},{4,12},{12,4},... | collective-permute-start | bytes 2359304 | tf_op jit(solution)/shard_map/ppermute | solution.py:36
  89.4 23.0 %collective-permute-start.5 = (bf16[2,64,3072]{2,1,0:T(8,128)(2,1)S(1)}, bf16[2,64,3072]{2,1,0:T(8,128)(2,1)}, u32[]{:S(2)}, u32[]{:S(2)}) collective-permute-start(bf16[2,64,3072]{2,1,0:T(8,128)(2,1)S(1)} %collective-permute-done.4), channel_id=1, source_target_pairs={{0,1},{1,2},{2,3},{3,0},{4,5},{5,6},{6,7},{7,4},{8,9},{9,10},{10,1... | collective-permute-start | bytes 2359304 | tf_op jit(solution)/shard_map/ppermute | solution.py:41
  112.4 28.4 %collective-permute-start.13 = (bf16[2,64,3072]{2,1,0:T(8,128)(2,1)}, bf16[2,64,3072]{2,1,0:T(8,128)(2,1)}, u32[]{:S(2)}, u32[]{:S(2)}) collective-permute-start(bf16[2,64,3072]{2,1,0:T(8,128)(2,1)} %collective-permute-done.5), channel_id=1, source_target_pairs={{0,1},{1,2},{2,3},{3,0},{4,5},{5,6},{6,7},{7,4},{8,9},{9,10},{10,1... | collective-permute-start | bytes 2359304 | tf_op jit(solution)/shard_map/ppermute | solution.py:41
  112.4 62.5 %all-to-all-start = ((bf16[4,64,2048]{2,1,0:T(8,128)(2,1)}), bf16[4,64,2048]{2,1,0:T(8,128)(2,1)S(1)}, u32[]{:S(2)}, u32[]{:S(2)}) async-start(bf16[4,64,2048]{2,1,0:T(8,128)(2,1)} %bitcast.550), calls=%async_computation | async-start | bytes 2097152 | tf_op jit(solution)/shard_map/all_to_all | solution.py:680
  120.8 38.3 %collective-permute-start.19 = (bf16[2,64,3072]{2,1,0:T(8,128)(2,1)S(1)}, bf16[2,64,3072]{2,1,0:T(8,128)(2,1)S(1)}, u32[]{:S(2)}, u32[]{:S(2)}) collective-permute-start(bf16[2,64,3072]{2,1,0:T(8,128)(2,1)S(1)} %copy-done.54), channel_id=1, source_target_pairs={{0,8},{8,0},{1,9},{9,1},{2,10},{10,2},{3,11},{11,3},{4,12},{12,4},... | collective-permute-start | bytes 2359304 | tf_op jit(solution)/shard_map/ppermute | solution.py:36
  123.9 42.9 %collective-permute-start.15 = (bf16[2,64,3072]{2,1,0:T(8,128)(2,1)S(1)}, bf16[2,64,3072]{2,1,0:T(8,128)(2,1)}, u32[]{:S(2)}, u32[]{:S(2)}) collective-permute-start(bf16[2,64,3072]{2,1,0:T(8,128)(2,1)S(1)} %copy-done.54), channel_id=1, source_target_pairs={{0,16},{16,0},{1,17},{17,1},{2,18},{18,2},{3,19},{19,3},{4,20},{20... | collective-permute-start | bytes 2359304 | tf_op jit(solution)/shard_map/ppermute | solution.py:41
  140.7 15.7 %collective-permute-start.20 = (bf16[64,2048]{1,0:T(8,128)(2,1)S(1)}, bf16[64,2048]{1,0:T(8,128)(2,1)S(1)}, u32[]{:S(2)}, u32[]{:S(2)}) collective-permute-start(bf16[64,2048]{1,0:T(8,128)(2,1)S(1)} %copy-done.64), channel_id=1, source_target_pairs={{0,8},{8,0},{1,9},{9,1},{2,10},{10,2},{3,11},{11,3},{4,12},{12,4},... | collective-permute-start | bytes 786440 | tf_op jit(solution)/shard_map/ppermute | solution.py:36
  159.2 35.0 %collective-permute-start.21 = (bf16[2,2,64,2816]{3,2,1,0:T(8,128)(2,1)S(1)}, bf16[2,2,64,2816]{3,2,1,0:T(8,128)(2,1)}, u32[]{:S(2)}, u32[]{:S(2)}) collective-permute-start(bf16[2,2,64,2816]{3,2,1,0:T(8,128)(2,1)S(1)} %bitcast.545), channel_id=1, source_target_pairs={{0,16},{16,0},{1,17},{17,1},{2,18},{18,2},{3,19},{19,3},{4,20},{20... | collective-permute-start | bytes 4325384 | tf_op jit(solution)/shard_map/ppermute | solution.py:41
  160.1 36.4 %collective-permute-start.29 = (bf16[2,2,64,2816]{3,2,1,0:T(8,128)(2,1)S(1)}, bf16[2,2,64,2816]{3,2,1,0:T(8,128)(2,1)}, u32[]{:S(2)}, u32[]{:S(2)}) collective-permute-start(bf16[2,2,64,2816]{3,2,1,0:T(8,128)(2,1)S(1)} %bitcast.546), channel_id=1, source_target_pairs={{0,1},{1,2},{2,3},{3,0},{4,5},{5,6},{6,7},{7,4},{8,9},{9,10},{10,1... | collective-permute-start | bytes 4325384 | tf_op jit(solution)/shard_map/ppermute | solution.py:41
  160.7 23.5 %collective-permute-start.27 = (bf16[64,2048]{1,0:T(8,128)(2,1)}, bf16[64,2048]{1,0:T(8,128)(2,1)S(1)}, u32[]{:S(2)}, u32[]{:S(2)}) collective-permute-start(bf16[64,2048]{1,0:T(8,128)(2,1)} %collective-permute-done.7), channel_id=1, source_target_pairs={{0,8},{8,0},{1,9},{9,1},{2,10},{10,2},{3,11},{11,3},{4,12},{12,4},... | collective-permute-start | bytes 786440 | tf_op jit(solution)/shard_map/ppermute | solution.py:36
  165.7 21.4 %collective-permute-start.26 = (bf16[2,64,3072]{2,1,0:T(8,128)(2,1)}, bf16[2,64,3072]{2,1,0:T(8,128)(2,1)}, u32[]{:S(2)}, u32[]{:S(2)}) collective-permute-start(bf16[2,64,3072]{2,1,0:T(8,128)(2,1)} %collective-permute-done.5), channel_id=1, source_target_pairs={{0,8},{8,0},{1,9},{9,1},{2,10},{10,2},{3,11},{11,3},{4,12},{12,4},... | collective-permute-start | bytes 2359304 | tf_op jit(solution)/shard_map/ppermute | solution.py:36
  166.8 55.1 %collective-permute-start.25 = (bf16[64,2048]{1,0:T(8,128)(2,1)}, bf16[64,2048]{1,0:T(8,128)(2,1)}, u32[]{:S(2)}, u32[]{:S(2)}) collective-permute-start(bf16[64,2048]{1,0:T(8,128)(2,1)} %collective-permute-done.16), channel_id=1, source_target_pairs={{0,8},{8,0},{1,9},{9,1},{2,10},{10,2},{3,11},{11,3},{4,12},{12,4},... | collective-permute-start | bytes 786440 | tf_op jit(solution)/shard_map/ppermute | solution.py:36
  184.2 37.7 %collective-permute-start.24 = (bf16[2,64,3072]{2,1,0:T(8,128)(2,1)}, bf16[2,64,3072]{2,1,0:T(8,128)(2,1)}, u32[]{:S(2)}, u32[]{:S(2)}) collective-permute-start(bf16[2,64,3072]{2,1,0:T(8,128)(2,1)} %collective-permute-done.15), channel_id=1, source_target_pairs={{0,8},{8,0},{1,9},{9,1},{2,10},{10,2},{3,11},{11,3},{4,12},{12,4},... | collective-permute-start | bytes 2359304 | tf_op jit(solution)/shard_map/ppermute | solution.py:36
  187.1 24.9 %collective-permute-start.30 = (bf16[2,2,64,1408]{3,2,1,0:T(8,128)(2,1)}, bf16[2,2,64,1408]{3,2,1,0:T(8,128)(2,1)}, u32[]{:S(2)}, u32[]{:S(2)}) collective-permute-start(bf16[2,2,64,1408]{3,2,1,0:T(8,128)(2,1)} %maximum_bitcast_fusion), channel_id=1, source_target_pairs={{0,1},{1,2},{2,3},{3,0},{4,5},{5,6},{6,7},{7,4},{8,9},{9,10},{10,1... | collective-permute-start | bytes 2162696 | tf_op jit(solution)/shard_map/ppermute | solution.py:41
  194.1 18.9 %collective-permute-start.31 = (bf16[2,2,64,1408]{3,2,1,0:T(8,128)(2,1)}, bf16[2,2,64,1408]{3,2,1,0:T(8,128)(2,1)}, u32[]{:S(2)}, u32[]{:S(2)}) collective-permute-start(bf16[2,2,64,1408]{3,2,1,0:T(8,128)(2,1)} %maximum_bitcast_fusion), channel_id=1, source_target_pairs={{0,16},{16,0},{1,17},{17,1},{2,18},{18,2},{3,19},{19,3},{4,20},{20... | collective-permute-start | bytes 2162696 | tf_op jit(solution)/shard_map/ppermute | solution.py:41
  196.5 22.1 %collective-permute-start.8 = (bf16[256,2048]{1,0:T(8,128)(2,1)S(1)}, bf16[256,2048]{1,0:T(8,128)(2,1)S(1)}, u32[]{:S(2)}, u32[]{:S(2)}) collective-permute-start(bf16[256,2048]{1,0:T(8,128)(2,1)S(1)} %bitcast.541), channel_id=1, source_target_pairs={{0,4},{4,0},{1,5},{5,1},{2,6},{6,2},{3,7},{7,3},{8,12},{12,8},{9,1... | collective-permute-start | bytes 3145736 | tf_op jit(solution)/shard_map/ppermute | solution.py:36
  196.5 71.6 %all-to-all-start.1 = ((bf16[4,64,2048]{2,1,0:T(8,128)(2,1)}), bf16[4,64,2048]{2,1,0:T(8,128)(2,1)S(1)}, u32[]{:S(2)}, u32[]{:S(2)}) async-start(bf16[4,64,2048]{2,1,0:T(8,128)(2,1)} %bitcast.549), calls=%async_computation.1 | async-start | bytes 2097152 | tf_op jit(solution)/shard_map/all_to_all | solution.py:680
  213.0 25.4 %collective-permute-start.22 = (bf16[2,64,3072]{2,1,0:T(8,128)(2,1)}, bf16[2,64,3072]{2,1,0:T(8,128)(2,1)}, u32[]{:S(2)}, u32[]{:S(2)}) collective-permute-start(bf16[2,64,3072]{2,1,0:T(8,128)(2,1)} %collective-permute-done.5), channel_id=1, source_target_pairs={{0,16},{16,0},{1,17},{17,1},{2,18},{18,2},{3,19},{19,3},{4,20},{20... | collective-permute-start | bytes 2359304 | tf_op jit(solution)/shard_map/ppermute | solution.py:41
  218.6 47.6 %collective-permute-start.32 = (bf16[2,2,64,2816]{3,2,1,0:T(8,128)(2,1)}, bf16[2,2,64,2816]{3,2,1,0:T(8,128)(2,1)S(1)}, u32[]{:S(2)}, u32[]{:S(2)}) collective-permute-start(bf16[2,2,64,2816]{3,2,1,0:T(8,128)(2,1)} %collective-permute-done.29), channel_id=1, source_target_pairs={{0,16},{16,0},{1,17},{17,1},{2,18},{18,2},{3,19},{19,3},{4,20},{20... | collective-permute-start | bytes 4325384 | tf_op jit(solution)/shard_map/ppermute | solution.py:41
  221.9 45.0 %collective-permute-start.46 = (bf16[2,2,64,2816]{3,2,1,0:T(8,128)(2,1)}, bf16[2,2,64,2816]{3,2,1,0:T(8,128)(2,1)}, u32[]{:S(2)}, u32[]{:S(2)}) collective-permute-start(bf16[2,2,64,2816]{3,2,1,0:T(8,128)(2,1)} %collective-permute-done.29), channel_id=1, source_target_pairs={{0,1},{1,2},{2,3},{3,0},{4,5},{5,6},{6,7},{7,4},{8,9},{9,10},{10,1... | collective-permute-start | bytes 4325384 | tf_op jit(solution)/shard_map/ppermute | solution.py:41
  238.4 47.5 %collective-permute-start.36 = (bf16[64,2048]{1,0:T(8,128)(2,1)}, bf16[64,2048]{1,0:T(8,128)(2,1)S(1)}, u32[]{:S(2)}, u32[]{:S(2)}) collective-permute-start(bf16[64,2048]{1,0:T(8,128)(2,1)} %collective-permute-done.23), channel_id=1, source_target_pairs={{0,8},{8,0},{1,9},{9,1},{2,10},{10,2},{3,11},{11,3},{4,12},{12,4},... | collective-permute-start | bytes 786440 | tf_op jit(solution)/shard_map/ppermute | solution.py:36
  239.5 47.0 %collective-permute-start.35 = (bf16[2,64,3072]{2,1,0:T(8,128)(2,1)}, bf16[2,64,3072]{2,1,0:T(8,128)(2,1)S(1)}, u32[]{:S(2)}, u32[]{:S(2)}) collective-permute-start(bf16[2,64,3072]{2,1,0:T(8,128)(2,1)} %collective-permute-done.22), channel_id=1, source_target_pairs={{0,8},{8,0},{1,9},{9,1},{2,10},{10,2},{3,11},{11,3},{4,12},{12,4},... | collective-permute-start | bytes 2359304 | tf_op jit(solution)/shard_map/ppermute | solution.py:36
  266.2 35.1 %collective-permute-start.33 = (bf16[2,64,3072]{2,1,0:T(8,128)(2,1)}, bf16[2,64,3072]{2,1,0:T(8,128)(2,1)S(1)}, u32[]{:S(2)}, u32[]{:S(2)}) collective-permute-start(bf16[2,64,3072]{2,1,0:T(8,128)(2,1)} %collective-permute-done.13), channel_id=1, source_target_pairs={{0,16},{16,0},{1,17},{17,1},{2,18},{18,2},{3,19},{19,3},{4,20},{20... | collective-permute-start | bytes 2359304 | tf_op jit(solution)/shard_map/ppermute | solution.py:41
  268.1 34.3 %collective-permute-start.47 = (bf16[2,2,64,1408]{3,2,1,0:T(8,128)(2,1)}, bf16[2,2,64,1408]{3,2,1,0:T(8,128)(2,1)S(1)}, u32[]{:S(2)}, u32[]{:S(2)}) collective-permute-start(bf16[2,2,64,1408]{3,2,1,0:T(8,128)(2,1)} %collective-permute-done.30), channel_id=1, source_target_pairs={{0,16},{16,0},{1,17},{17,1},{2,18},{18,2},{3,19},{19,3},{4,20},{20... | collective-permute-start | bytes 2162696 | tf_op jit(solution)/shard_map/ppermute | solution.py:41
  282.8 18.5 %collective-permute-start.34 = (bf16[64,2048]{1,0:T(8,128)(2,1)}, bf16[64,2048]{1,0:T(8,128)(2,1)S(1)}, u32[]{:S(2)}, u32[]{:S(2)}) collective-permute-start(bf16[64,2048]{1,0:T(8,128)(2,1)} %collective-permute-done.14), channel_id=1, source_target_pairs={{0,16},{16,0},{1,17},{17,1},{2,18},{18,2},{3,19},{19,3},{4,20},{20... | collective-permute-start | bytes 786440 | tf_op jit(solution)/shard_map/ppermute | solution.py:41
  285.9 29.3 %collective-permute-start.41 = (bf16[64,2048]{1,0:T(8,128)(2,1)}, bf16[64,2048]{1,0:T(8,128)(2,1)S(1)}, u32[]{:S(2)}, u32[]{:S(2)}) collective-permute-start(bf16[64,2048]{1,0:T(8,128)(2,1)} %collective-permute-done.14), channel_id=1, source_target_pairs={{0,8},{8,0},{1,9},{9,1},{2,10},{10,2},{3,11},{11,3},{4,12},{12,4},... | collective-permute-start | bytes 786440 | tf_op jit(solution)/shard_map/ppermute | solution.py:36
  286.5 24.4 %collective-permute-start.37 = (bf16[2,64,3072]{2,1,0:T(8,128)(2,1)}, bf16[2,64,3072]{2,1,0:T(8,128)(2,1)S(1)}, u32[]{:S(2)}, u32[]{:S(2)}) collective-permute-start(bf16[2,64,3072]{2,1,0:T(8,128)(2,1)} %collective-permute-done.13), channel_id=1, source_target_pairs={{0,8},{8,0},{1,9},{9,1},{2,10},{10,2},{3,11},{11,3},{4,12},{12,4},... | collective-permute-start | bytes 2359304 | tf_op jit(solution)/shard_map/ppermute | solution.py:36
  301.3 83.8 %collective-permute-start.54 = (bf16[2,2,64,2816]{3,2,1,0:T(8,128)(2,1)}, bf16[2,2,64,2816]{3,2,1,0:T(8,128)(2,1)}, u32[]{:S(2)}, u32[]{:S(2)}) collective-permute-start(bf16[2,2,64,2816]{3,2,1,0:T(8,128)(2,1)} %collective-permute-done.46), channel_id=1, source_target_pairs={{0,1},{1,2},{2,3},{3,0},{4,5},{5,6},{6,7},{7,4},{8,9},{9,10},{10,1... | collective-permute-start | bytes 4325384 | tf_op jit(solution)/shard_map/ppermute | solution.py:41
  301.3 44.4 %collective-permute-start.48 = (bf16[2,2,64,1408]{3,2,1,0:T(8,128)(2,1)S(1)}, bf16[2,2,64,1408]{3,2,1,0:T(8,128)(2,1)S(1)}, u32[]{:S(2)}, u32[]{:S(2)}) collective-permute-start(bf16[2,2,64,1408]{3,2,1,0:T(8,128)(2,1)S(1)} %collective-permute-done.38), channel_id=1, source_target_pairs={{0,1},{1,2},{2,3},{3,0},{4,5},{5,6},{6,7},{7,4},{8,9},{9,10},{10,1... | collective-permute-start | bytes 2162696 | tf_op jit(solution)/shard_map/ppermute | solution.py:41
  302.4 15.7 %collective-permute-start.42 = (bf16[64,2048]{1,0:T(8,128)(2,1)S(1)}, bf16[64,2048]{1,0:T(8,128)(2,1)S(1)}, u32[]{:S(2)}, u32[]{:S(2)}) collective-permute-start(bf16[64,2048]{1,0:T(8,128)(2,1)S(1)} %collective-permute-done.34), channel_id=1, source_target_pairs={{0,8},{8,0},{1,9},{9,1},{2,10},{10,2},{3,11},{11,3},{4,12},{12,4},... | collective-permute-start | bytes 786440 | tf_op jit(solution)/shard_map/ppermute | solution.py:36
  310.9 36.9 %collective-permute-start.39 = (bf16[2,64,3072]{2,1,0:T(8,128)(2,1)S(1)}, bf16[2,64,3072]{2,1,0:T(8,128)(2,1)S(1)}, u32[]{:S(2)}, u32[]{:S(2)}) collective-permute-start(bf16[2,64,3072]{2,1,0:T(8,128)(2,1)S(1)} %collective-permute-done.33), channel_id=1, source_target_pairs={{0,8},{8,0},{1,9},{9,1},{2,10},{10,2},{3,11},{11,3},{4,12},{12,4},... | collective-permute-start | bytes 2359304 | tf_op jit(solution)/shard_map/ppermute | solution.py:36
  315.3 30.4 %collective-permute-start.49 = (bf16[2,2,64,1408]{3,2,1,0:T(8,128)(2,1)S(1)}, bf16[2,2,64,1408]{3,2,1,0:T(8,128)(2,1)S(1)}, u32[]{:S(2)}, u32[]{:S(2)}) collective-permute-start(bf16[2,2,64,1408]{3,2,1,0:T(8,128)(2,1)S(1)} %collective-permute-done.38), channel_id=1, source_target_pairs={{0,16},{16,0},{1,17},{17,1},{2,18},{18,2},{3,19},{19,3},{4,20},{20... | collective-permute-start | bytes 2162696 | tf_op jit(solution)/shard_map/ppermute | solution.py:41
  323.1 62.0 %collective-permute-start.55 = (bf16[2,2,64,2816]{3,2,1,0:T(8,128)(2,1)}, bf16[2,2,64,2816]{3,2,1,0:T(8,128)(2,1)}, u32[]{:S(2)}, u32[]{:S(2)}) collective-permute-start(bf16[2,2,64,2816]{3,2,1,0:T(8,128)(2,1)} %collective-permute-done.46), channel_id=1, source_target_pairs={{0,16},{16,0},{1,17},{17,1},{2,18},{18,2},{3,19},{19,3},{4,20},{20... | collective-permute-start | bytes 4325384 | tf_op jit(solution)/shard_map/ppermute | solution.py:41
  345.7 29.2 %collective-permute-start.50 = (bf16[2,2,64,1408]{3,2,1,0:T(8,128)(2,1)S(1)}, bf16[2,2,64,1408]{3,2,1,0:T(8,128)(2,1)S(1)}, u32[]{:S(2)}, u32[]{:S(2)}) collective-permute-start(bf16[2,2,64,1408]{3,2,1,0:T(8,128)(2,1)S(1)} %collective-permute-done.48), channel_id=1, source_target_pairs={{0,16},{16,0},{1,17},{17,1},{2,18},{18,2},{3,19},{19,3},{4,20},{20... | collective-permute-start | bytes 2162696 | tf_op jit(solution)/shard_map/ppermute | solution.py:41
  385.1 52.5 %collective-permute-start.56 = (bf16[2,2,64,2816]{3,2,1,0:T(8,128)(2,1)}, bf16[2,2,64,2816]{3,2,1,0:T(8,128)(2,1)S(1)}, u32[]{:S(2)}, u32[]{:S(2)}) collective-permute-start(bf16[2,2,64,2816]{3,2,1,0:T(8,128)(2,1)} %collective-permute-done.54), channel_id=1, source_target_pairs={{0,16},{16,0},{1,17},{17,1},{2,18},{18,2},{3,19},{19,3},{4,20},{20... | collective-permute-start | bytes 4325384 | tf_op jit(solution)/shard_map/ppermute | solution.py:41
  391.0 26.2 %collective-permute-start.60 = (bf16[256,2048]{1,0:T(8,128)(2,1)S(1)}, bf16[256,2048]{1,0:T(8,128)(2,1)S(1)}, u32[]{:S(2)}, u32[]{:S(2)}) collective-permute-start(bf16[256,2048]{1,0:T(8,128)(2,1)S(1)} %fusion.12), channel_id=1, source_target_pairs={{0,8},{8,0},{1,9},{9,1},{2,10},{10,2},{3,11},{11,3},{4,12},{12,4},... | collective-permute-start | bytes 3145736 | tf_op jit(solution)/shard_map/ppermute | solution.py:36
  392.1 26.2 %collective-permute-start.53 = (bf16[256,2048]{1,0:T(8,128)(2,1)S(1)}, bf16[256,2048]{1,0:T(8,128)(2,1)S(1)}, u32[]{:S(2)}, u32[]{:S(2)}) collective-permute-start(bf16[256,2048]{1,0:T(8,128)(2,1)S(1)} %fusion.12), channel_id=1, source_target_pairs={{0,4},{4,0},{1,5},{5,1},{2,6},{6,2},{3,7},{7,3},{8,12},{12,8},{9,1... | collective-permute-start | bytes 3145736 | tf_op jit(solution)/shard_map/ppermute | solution.py:36
  393.3 44.3 %collective-permute-start.58 = (bf16[256,2048]{1,0:T(8,128)(2,1)S(1)}, bf16[256,2048]{1,0:T(8,128)(2,1)S(1)}, u32[]{:S(2)}, u32[]{:S(2)}) collective-permute-start(bf16[256,2048]{1,0:T(8,128)(2,1)S(1)} %multiply_convert_fusion.1), channel_id=1, source_target_pairs={{0,8},{8,0},{1,9},{9,1},{2,10},{10,2},{3,11},{11,3},{4,12},{12,4},... | collective-permute-start | bytes 3145736 | tf_op jit(solution)/shard_map/ppermute | solution.py:36
  397.0 48.4 %collective-permute-start.45 = (bf16[256,2048]{1,0:T(8,128)(2,1)S(1)}, bf16[256,2048]{1,0:T(8,128)(2,1)}, u32[]{:S(2)}, u32[]{:S(2)}) collective-permute-start(bf16[256,2048]{1,0:T(8,128)(2,1)S(1)} %multiply_convert_fusion.1), channel_id=1, source_target_pairs={{0,4},{4,0},{1,5},{5,1},{2,6},{6,2},{3,7},{7,3},{8,12},{12,8},{9,1... | collective-permute-start | bytes 3145736 | tf_op jit(solution)/shard_map/ppermute | solution.py:36
  417.2 32.4 %collective-permute-start.61 = (bf16[256,2048]{1,0:T(8,128)(2,1)S(1)}, bf16[256,2048]{1,0:T(8,128)(2,1)}, u32[]{:S(2)}, u32[]{:S(2)}) collective-permute-start(bf16[256,2048]{1,0:T(8,128)(2,1)S(1)} %collective-permute-done.60), channel_id=1, source_target_pairs={{0,4},{4,0},{1,5},{5,1},{2,6},{6,2},{3,7},{7,3},{8,12},{12,8},{9,1... | collective-permute-start | bytes 3145736 | tf_op jit(solution)/shard_map/ppermute | solution.py:36
  485.8 33.4 %collective-permute-start.66 = (bf16[256,2048]{1,0:T(8,128)(2,1)}, bf16[256,2048]{1,0:T(8,128)(2,1)S(1)}, u32[]{:S(2)}, u32[]{:S(2)}) collective-permute-start(bf16[256,2048]{1,0:T(8,128)(2,1)} %slice.354), channel_id=1, source_target_pairs={{0,4},{4,0},{1,5},{5,1},{2,6},{6,2},{3,7},{7,3},{8,12},{12,8},{9,1... | collective-permute-start | bytes 3145736 | tf_op jit(solution)/shard_map/ppermute | solution.py:36
  486.4 35.8 %collective-permute-start.62 = (bf16[256,2048]{1,0:T(8,128)(2,1)}, bf16[256,2048]{1,0:T(8,128)(2,1)S(1)}, u32[]{:S(2)}, u32[]{:S(2)}) collective-permute-start(bf16[256,2048]{1,0:T(8,128)(2,1)} %slice.350), channel_id=1, source_target_pairs={{0,4},{4,0},{1,5},{5,1},{2,6},{6,2},{3,7},{7,3},{8,12},{12,8},{9,1... | collective-permute-start | bytes 3145736 | tf_op jit(solution)/shard_map/ppermute | solution.py:36
  518.7 20.2 %collective-permute-start.65 = (bf16[256,2048]{1,0:T(8,128)(2,1)}, bf16[256,2048]{1,0:T(8,128)(2,1)}, u32[]{:S(2)}, u32[]{:S(2)}) collective-permute-start(bf16[256,2048]{1,0:T(8,128)(2,1)} %slice.352), channel_id=1, source_target_pairs={{0,4},{4,0},{1,5},{5,1},{2,6},{6,2},{3,7},{7,3},{8,12},{12,8},{9,1... | collective-permute-start | bytes 3145736 | tf_op jit(solution)/shard_map/ppermute | solution.py:36
  519.2 30.1 %collective-permute-start.57 = (bf16[256,2048]{1,0:T(8,128)(2,1)}, bf16[256,2048]{1,0:T(8,128)(2,1)}, u32[]{:S(2)}, u32[]{:S(2)}) collective-permute-start(bf16[256,2048]{1,0:T(8,128)(2,1)} %slice.348), channel_id=1, source_target_pairs={{0,4},{4,0},{1,5},{5,1},{2,6},{6,2},{3,7},{7,3},{8,12},{12,8},{9,1... | collective-permute-start | bytes 3145736 | tf_op jit(solution)/shard_map/ppermute | solution.py:36
  520.6 26.3 %collective-permute-start.67 = (bf16[256,2048]{1,0:T(8,128)(2,1)}, bf16[256,2048]{1,0:T(8,128)(2,1)}, u32[]{:S(2)}, u32[]{:S(2)}) collective-permute-start(bf16[256,2048]{1,0:T(8,128)(2,1)} %add_convert_fusion), channel_id=1, source_target_pairs={{0,8},{8,0},{1,9},{9,1},{2,10},{10,2},{3,11},{11,3},{4,12},{12,4},... | collective-permute-start | bytes 3145736 | tf_op jit(solution)/shard_map/ppermute | solution.py:36
  523.5 45.4 %collective-permute-start.63 = (bf16[256,2048]{1,0:T(8,128)(2,1)}, bf16[256,2048]{1,0:T(8,128)(2,1)}, u32[]{:S(2)}, u32[]{:S(2)}) collective-permute-start(bf16[256,2048]{1,0:T(8,128)(2,1)} %add_convert_fusion.2), channel_id=1, source_target_pairs={{0,8},{8,0},{1,9},{9,1},{2,10},{10,2},{3,11},{11,3},{4,12},{12,4},... | collective-permute-start | bytes 3145736 | tf_op jit(solution)/shard_map/ppermute | solution.py:36
  638.5 21.5 %collective-permute-start.68 = (bf16[256,2048]{1,0:T(8,128)(2,1)}, bf16[256,2048]{1,0:T(8,128)(2,1)}, u32[]{:S(2)}, u32[]{:S(2)}) collective-permute-start(bf16[256,2048]{1,0:T(8,128)(2,1)} %multiply_convert_fusion), channel_id=1, source_target_pairs={{0,4},{4,0},{1,5},{5,1},{2,6},{6,2},{3,7},{7,3},{8,12},{12,8},{9,1... | collective-permute-start | bytes 3145736 | tf_op jit(solution)/shard_map/ppermute | solution.py:36
  650.0 81.7 %all-to-all-start.2 = ((bf16[4,64,2048]{2,1,0:T(8,128)(2,1)}), bf16[4,64,2048]{2,1,0:T(8,128)(2,1)}, u32[]{:S(2)}, u32[]{:S(2)}) async-start(bf16[4,64,2048]{2,1,0:T(8,128)(2,1)} %bitcast.547), calls=%async_computation.2 | async-start | bytes 2097152 | tf_op jit(solution)/shard_map/all_to_all | solution.py:924
  657.9 47.8 %collective-permute-start.97 = (f32[56,512]{1,0:T(8,128)S(1)}, f32[56,512]{1,0:T(8,128)S(1)}, u32[]{:S(2)}, u32[]{:S(2)}) collective-permute-start(f32[56,512]{1,0:T(8,128)S(1)} %slice.452), channel_id=1, source_target_pairs={{0,8},{8,0},{1,9},{9,1},{2,10},{10,2},{3,11},{11,3},{4,12},{12,4},... | collective-permute-start | bytes 344072 | tf_op jit(solution)/shard_map/ppermute | solution.py:36
  658.0 51.3 %collective-permute-start.99 = (f32[168,512]{1,0:T(8,128)S(1)}, f32[168,512]{1,0:T(8,128)S(1)}, u32[]{:S(2)}, u32[]{:S(2)}) collective-permute-start(f32[168,512]{1,0:T(8,128)S(1)} %slice.458), channel_id=1, source_target_pairs={{0,8},{8,0},{1,9},{9,1},{2,10},{10,2},{3,11},{11,3},{4,12},{12,4},... | collective-permute-start | bytes 1032200 | tf_op jit(solution)/shard_map/ppermute | solution.py:36
  705.1 40.9 %collective-permute-start.69 = (bf16[256,2048]{1,0:T(8,128)(2,1)S(1)}, bf16[256,2048]{1,0:T(8,128)(2,1)S(1)}, u32[]{:S(2)}, u32[]{:S(2)}) collective-permute-start(bf16[256,2048]{1,0:T(8,128)(2,1)S(1)} %slice.361), channel_id=1, source_target_pairs={{0,4},{4,0},{1,5},{5,1},{2,6},{6,2},{3,7},{7,3},{8,12},{12,8},{9,1... | collective-permute-start | bytes 3145736 | tf_op jit(solution)/shard_map/ppermute | solution.py:36
  732.8 21.6 %collective-permute-start.64 = (bf16[2,1,64,2048]{3,2,0,1:T(8,128)(2,1)S(1)}, bf16[2,1,64,2048]{3,2,0,1:T(8,128)(2,1)S(1)}, u32[]{:S(2)}, u32[]{:S(2)}) collective-permute-start(bf16[2,1,64,2048]{3,2,0,1:T(8,128)(2,1)S(1)} %dynamic-slice_bitcast_fusion.2), channel_id=1, source_target_pairs={{0,4},{4,0},{1,5},{5,1},{2,6},{6,2},{3,7},{7,3},{8,12},{12,8},{9,1... | collective-permute-start | bytes 1572872 | tf_op jit(solution)/shard_map/ppermute | solution.py:36
  756.7 31.0 %all-to-all-start.3 = ((bf16[4,64,2048]{2,1,0:T(8,128)(2,1)}), bf16[4,64,2048]{2,1,0:T(8,128)(2,1)S(1)}, u32[]{:S(2)}, u32[]{:S(2)}) async-start(bf16[4,64,2048]{2,1,0:T(8,128)(2,1)} %bitcast.141), calls=%async_computation.3 | async-start | bytes 2097152 | tf_op jit(solution)/shard_map/all_to_all | solution.py:924
  (129 other events, 1588.9 us)

commit v2 on v1

v2 whole, which is shorter than its diff:
```python
import functools

import jax
import jax.numpy as jnp
from jax import lax
from jax.experimental import pallas as pl
from jax.experimental.pallas import tpu as pltpu
from jax.sharding import Mesh
from jax.sharding import PartitionSpec as P

HEAD_DIM = 128
SCALE = 2.0
BF = jnp.bfloat16
F32 = jnp.float32
ALL = ("yy", "xx", "core", "seq")
WORD = 512


def mm(a, b, dims=((1,), (0,))):
    return lax.dot_general(a, b, (dims, ((), ())), preferred_element_type=F32)


def nt(a, b):
    return mm(a, b, ((1,), (1,)))


def tn(a, b):
    return mm(a, b, ((0,), (0,)))


def take(a, index, axis):
    return lax.dynamic_index_in_dim(a, index, axis, keepdims=False)


def swap(a, name):
    return lax.ppermute(a, name, [(0, 1), (1, 0)])


def shift(a, name, step):
    size = lax.axis_size(name)
    return lax.ppermute(a, name, [(i, (i + step) % size) for i in range(size)])


def pair(mine, other, index, axis=0):
    first = jnp.where(index == 0, mine, other)
    second = jnp.where(index == 0, other, mine)
    return jnp.stack([first, second], axis=axis)


def put(buffer, block, index, axis):
    return lax.dynamic_update_slice_in_dim(buffer, jnp.expand_dims(block, axis), index, axis)


def rms(v):
    return v * lax.rsqrt(jnp.mean(v * v, axis=-1, keepdims=True) + 1e-05)


def rms_back(v, grad):
    inverse = lax.rsqrt(jnp.mean(v * v, axis=-1, keepdims=True) + 1e-05)
    inner = jnp.mean(v * grad, axis=-1, keepdims=True)
    return grad * inverse - v * (inner * inverse * inverse * inverse)


def merged(base, down, up):
    product = lax.dot_general(
        down.astype(BF), up.astype(BF), (((down.ndim - 1,), (up.ndim - 2,)), (tuple(range(down.ndim - 2)),) * 2),
        preferred_element_type=F32,
    )
    return (base.astype(F32) + SCALE * product).astype(BF)


class Box:
    def __init__(self, array):
        self.array = array


class Links:
    def __init__(self, depth, boxes, buffers):
        self.depth = depth
        self.boxes = boxes
        self.buffers = buffers
        self.rounds = []
        self.placed = 0

    def run(self, queues):
        boxes = self.boxes
        while any(queues):
            ready = set(boxes)
            self.place(len(self.rounds) - self.depth)
            self.rounds.append([])
            for queue in queues:
                for place, (source, result, move) in enumerate(queue):
                    if source in ready:
                        queue.pop(place)
                        self.send(boxes, source, result, move)
                        break

    def place(self, until):
        while self.placed < until:
            for name, box in self.rounds[self.placed]:
                for buffer in self.buffers.values():
                    buffer.put(name, box.array)
            self.placed += 1

    def send(self, boxes, source, result, move):
        box = boxes[source]
        if len(self.rounds) > self.depth:
            old = [b for name, b in self.rounds[-1 - self.depth] if b is not box and "_" not in name]
            held = [b for b in self.buffers.values() if b.pending()]
            both = lax.optimization_barrier((box.array, [b.array for b in old], [b.array for b in held]))
            box.array = both[0]
            for b, array in zip(old + held, both[1] + both[2]):
                b.array = array
        boxes[result] = Box(move(box.array))
        self.rounds[-1].append((result, boxes[result]))


class Buffer:
    def __init__(self, shape, free, blocks):
        self.array = unwritten(shape, BF)
        self.free = free
        self.blocks = blocks

    def pending(self):
        return len(self.blocks) > self.free

    def put(self, name, block):
        if name in self.blocks:
            part, start = self.blocks.pop(name)(block)
            self.array = lax.dynamic_update_slice(self.array, part, [jnp.int32(v) for v in start])


def unwritten(shape, kind):
    return pl.pallas_call(
        lambda ref: None, out_shape=jax.ShapeDtypeStruct(shape, kind),
        out_specs=pl.BlockSpec(memory_space=pl.ANY), name="unwritten",
    )()


def turned(v, cosine, sine):
    return v * cosine + pltpu.roll(v, HEAD_DIM // 2, 1) * sine


def qkv_kernel(rotated, h_ref, v_ref, down_ref, m_ref, cos_ref, sin_ref, t_ref, p_ref, n_ref, cross_ref):
    block = v_ref[...]
    rows = h_ref.shape[0]
    both = jnp.dot(jnp.concatenate([h_ref[...], down_ref[...]], axis=0), block, preferred_element_type=F32)
    cross_ref[...] = both[rows:]
    t = both[:rows]
    wide = block.astype(F32)
    norm = jnp.sqrt(jnp.sum(wide * wide, axis=0, keepdims=True))
    n_ref[...] = norm
    t_ref[...] = t.astype(BF)
    scaled = t * (m_ref[...] / norm)

    @pl.when(pl.program_id(0) < rotated)
    def _():
        for part in range(t.shape[1] // HEAD_DIM):
            columns = slice(part * HEAD_DIM, (part + 1) * HEAD_DIM)
            p_ref[:, columns] = turned(scaled[:, columns], cos_ref[...], sin_ref[...]).astype(BF)

    @pl.when(pl.program_id(0) >= rotated)
    def _():
        p_ref[...] = scaled.astype(BF)


def qkv_forward(h, weight, downs, magnitude, cosine, sine):
    rows, depth = h.shape
    columns = magnitude.shape[1]
    width = 2 * HEAD_DIM
    rotated = columns * 2 // 3 // width
    whole = lambda j: (0, 0)
    strip = lambda j: (0, j)
    return pl.pallas_call(
        functools.partial(qkv_kernel, rotated),
        grid=(columns // width,),
        in_specs=[
            pl.BlockSpec((rows, depth), whole),
            pl.BlockSpec((depth, width), strip),
            pl.BlockSpec(downs.shape, whole),
            pl.BlockSpec((1, width), strip),
            pl.BlockSpec((rows, HEAD_DIM), whole),
            pl.BlockSpec((rows, HEAD_DIM), whole),
        ],
        out_specs=[
            pl.BlockSpec((rows, width), strip),
            pl.BlockSpec((rows, width), strip),
            pl.BlockSpec((1, width), strip),
            pl.BlockSpec((downs.shape[0], width), strip),
        ],
        out_shape=[
            jax.ShapeDtypeStruct((rows, columns), BF),
            jax.ShapeDtypeStruct((rows, columns), BF),
            jax.ShapeDtypeStruct((1, columns), F32),
            jax.ShapeDtypeStruct((downs.shape[0], columns), F32),
        ],
        compiler_params=pltpu.CompilerParams(vmem_limit_bytes=32 << 20),
        cost_estimate=pl.CostEstimate(
            flops=2 * rows * depth * columns, bytes_accessed=2 * depth * columns + 6 * rows * columns,
            transcendentals=columns,
        ),
        name="qkv_forward",
    )(h, weight, downs, magnitude, cosine, sine)


def softmax_block(q, k, bias):
    scores = nt(q, k) * HEAD_DIM ** (-0.5) + bias
    weights = jnp.exp(scores - jnp.max(scores, axis=-1, keepdims=True))
    return weights / jnp.sum(weights, axis=-1, keepdims=True)


def attend_kernel(q_ref, k_ref, v_ref, bias_ref, o_ref):
    probs = softmax_block(q_ref[...], k_ref[...], bias_ref[...])
    o_ref[...] = mm(probs.astype(BF), v_ref[...]).astype(BF)


def attend_back_kernel(q_ref, k_ref, v_ref, g_ref, bias_ref, dq_ref, dk_ref, dv_ref):
    q, k, g = q_ref[...], k_ref[...], g_ref[...]
    probs = softmax_block(q, k, bias_ref[...])
    grad = nt(g, v_ref[...])
    inner = jnp.sum(probs * grad, axis=-1, keepdims=True)
    raw = (probs * (grad - inner) * HEAD_DIM ** (-0.5)).astype(BF)
    dq_ref[...] = mm(raw, k)
    dk_ref[...] = tn(raw, q)
    dv_ref[...] = tn(probs.astype(BF), g)


def attention_call(kernel, name, heads, q, kv, offsets, extra, bias, outs):
    rows, keys = bias.shape
    head = lambda base: lambda j: (0, base + j)
    specs = [
        pl.BlockSpec((rows, HEAD_DIM), head(0)),
        pl.BlockSpec((keys, HEAD_DIM), head(offsets[0])),
        pl.BlockSpec((keys, HEAD_DIM), head(offsets[1])),
    ]
    specs += [pl.BlockSpec((rows, HEAD_DIM), head(0)) for _ in extra]
    specs.append(pl.BlockSpec((rows, keys), lambda j: (0, 0)))
    return pl.pallas_call(
        kernel,
        grid=(heads,),
        in_specs=specs,
        out_specs=[pl.BlockSpec((length, HEAD_DIM), head(0)) for length, _ in outs],
        out_shape=[jax.ShapeDtypeStruct((length, heads * HEAD_DIM), kind) for length, kind in outs],
        compiler_params=pltpu.CompilerParams(vmem_limit_bytes=48 << 20),
        cost_estimate=pl.CostEstimate(
            flops=4 * len(outs) * rows * keys * HEAD_DIM * heads,
            bytes_accessed=8 * rows * HEAD_DIM * heads, transcendentals=rows * keys * heads,
        ),
        name=name,
    )(q, kv, kv, *extra, bias)


def attend_back_turn_kernel(
    q_ref, k_ref, v_ref, g_ref, bias_ref, tq_ref, tk_ref, tv_ref, s_ref, r_ref, cos_ref, sin_ref, dt_ref, dm_ref
):
    q, k, g = q_ref[...], k_ref[...], g_ref[...]
    probs = softmax_block(q, k, bias_ref[...])
    grad = nt(g, v_ref[...])
    inner = jnp.sum(probs * grad, axis=-1, keepdims=True)
    raw = (probs * (grad - inner) * HEAD_DIM ** (-0.5)).astype(BF)
    cosine, sine = cos_ref[...], -sin_ref[...]
    plain = (turned(mm(raw, k), cosine, sine), turned(tn(raw, q), cosine, sine), tn(probs.astype(BF), g))
    for member, t_ref in enumerate((tq_ref, tk_ref, tv_ref)):
        dt_ref[member] = (plain[member] * s_ref[member]).astype(BF)
        dm_ref[member] = jnp.sum(plain[member] * t_ref[...].astype(F32), axis=0, keepdims=True) * r_ref[member]


def attend_back_turn(heads, qkv, grad, bias, t, factor, inverse, cosine, sine):
    rows = bias.shape[0]
    head = lambda base: lambda j: (0, base + j)
    whole = lambda j: (0, 0)
    block = lambda base: pl.BlockSpec((rows, HEAD_DIM), head(base))
    member = lambda j: (0, 0, j)
    return pl.pallas_call(
        attend_back_turn_kernel,
        grid=(heads,),
        in_specs=[
            block(0), block(heads), block(2 * heads), block(0),
            pl.BlockSpec((rows, rows), whole),
            block(0), block(heads), block(2 * heads),
            pl.BlockSpec((3, 1, HEAD_DIM), member),
            pl.BlockSpec((3, 1, HEAD_DIM), member),
            pl.BlockSpec((rows, HEAD_DIM), whole),
            pl.BlockSpec((rows, HEAD_DIM), whole),
        ],
        out_specs=[pl.BlockSpec((3, rows, HEAD_DIM), member), pl.BlockSpec((3, 1, HEAD_DIM), member)],
        out_shape=[
            jax.ShapeDtypeStruct((3, rows, heads * HEAD_DIM), BF),
            jax.ShapeDtypeStruct((3, 1, heads * HEAD_DIM), F32),
        ],
        compiler_params=pltpu.CompilerParams(vmem_limit_bytes=48 << 20),
        cost_estimate=pl.CostEstimate(
            flops=10 * rows * rows * HEAD_DIM * heads, bytes_accessed=20 * rows * HEAD_DIM * heads,
            transcendentals=rows * rows * heads,
        ),
        name="attend_back_turn",
    )(qkv, qkv, qkv, grad, bias, t, t, t, factor, inverse, cosine, sine)


def words_out(ref, start, value):
    rows, columns = value.shape
    for chunk in range(-(-columns // WORD)):
        left = chunk * WORD
        used = min(WORD, columns - left)
        ref[chunk, start : start + rows, :used] = value[:, left : left + used]
        if used < WORD:
            ref[chunk, start : start + rows, used:] = jnp.zeros((rows, WORD - used), F32)


def row_of(row, rows=8):
    return jnp.concatenate([row, jnp.zeros((rows - row.shape[0], row.shape[1]), F32)], axis=0)


def qkv_back_kernel(
    dt_ref, v_ref, h_ref, low_ref, up_ref, cross_ref, s_ref, n_ref, dm_ref, out_ref, shared_ref, core_ref, acc_ref
):
    member = pl.program_id(0)
    dt, weight = dt_ref[0], v_ref[...]
    rows = dt.shape[0]
    up = up_ref[0]
    pull = -s_ref[0] * dm_ref[0] / n_ref[0]
    stacked = nt(jnp.concatenate([dt, (up * pull).astype(BF)], axis=0), weight)
    update = stacked[:rows]

    @pl.when(member == 0)
    def _():
        acc_ref[...] = update

    @pl.when(member > 0)
    def _():
        acc_ref[...] += update

    @pl.when(member == pl.num_programs(0) - 1)
    def _():
        out_ref[...] = acc_ref[...].astype(BF)

    low_grad = nt(up.astype(BF), dt).astype(BF)
    words_out(shared_ref, 0, SCALE * (mm(low_grad, h_ref[...]) + stacked[rows:]))
    words_out(core_ref, 0, SCALE * (mm(low_ref[0], dt) + cross_ref[0] * pull))


def qkv_back(dt, weight, h, low, up, cross, factor, norm, dm):
    members, rows, columns = dt.shape
    width = h.shape[1]
    rank = up.shape[1]
    step = lambda j: (j, 0, 0)
    small = pl.BlockSpec((1, 1, columns), step)
    return pl.pallas_call(
        qkv_back_kernel,
        grid=(members,),
        in_specs=[
            pl.BlockSpec((1, rows, columns), step),
            pl.BlockSpec((width, columns), lambda j: (0, j)),
            pl.BlockSpec((rows, width), lambda j: (0, 0)),
            pl.BlockSpec((1, rank, rows), step),
            pl.BlockSpec((1, rank, columns), step),
            pl.BlockSpec((1, rank, columns), step),
            small, small, small,
        ],
        out_specs=[
            pl.BlockSpec((rows, width), lambda j: (0, 0)),
            pl.BlockSpec((width // WORD, rank, WORD), lambda j: (0, j, 0)),
            pl.BlockSpec((columns // WORD, rank, WORD), lambda j: (0, j, 0)),
        ],
        out_shape=[
            jax.ShapeDtypeStruct((rows, width), BF),
            jax.ShapeDtypeStruct((width // WORD, members * rank, WORD), F32),
            jax.ShapeDtypeStruct((columns // WORD, members * rank, WORD), F32),
        ],
        scratch_shapes=[pltpu.VMEM((rows, width), F32)],
        compiler_params=pltpu.CompilerParams(vmem_limit_bytes=48 << 20),
        cost_estimate=pl.CostEstimate(
            flops=2 * members * rows * columns * width, bytes_accessed=2 * members * width * columns,
            transcendentals=0,
        ),
        name="qkv_back",
    )(dt, weight, h, low, up, cross, factor, norm, dm)


def out_adapter_kernel(
    dt_ref, w_ref, u_ref, down_ref, up_ref, s_ref, n_ref, dm_ref, own_ref, shared_ref, core_ref
):
    inside = u_ref.shape[1]
    dt, u, up, down = dt_ref[...], u_ref[...], up_ref[...], down_ref[...]
    rank = up.shape[0]
    pull = -s_ref[...] * dm_ref[...] / n_ref[...]
    low_grad = nt(up.astype(BF), dt).astype(BF)
    frozen = (up * pull).astype(BF)
    sides = (slice(0, inside), slice(inside, 2 * inside))
    words_out(core_ref, 0, SCALE * (mm(low_grad, u) + sum(nt(frozen[:, part], w_ref[i]) for i, part in enumerate(sides))))
    low = nt(down, u).astype(BF)
    cross = jnp.concatenate([mm(down, w_ref[i]) for i in range(2)], axis=1)
    words_out(shared_ref, 0, SCALE * (mm(low, dt) + cross * pull))
    words_out(shared_ref, rank, row_of(own_ref[...]))


def out_adapter(dt, weight, u, down, up, factor, norm, dm_pair, dm_own):
    rank, width = up.shape
    inside = u.shape[1]
    return pl.pallas_call(
        out_adapter_kernel,
        out_shape=[
            jax.ShapeDtypeStruct((width // WORD, rank + 8, WORD), F32),
            jax.ShapeDtypeStruct((inside // WORD, rank, WORD), F32),
        ],
        compiler_params=pltpu.CompilerParams(vmem_limit_bytes=48 << 20),
        cost_estimate=pl.CostEstimate(
            flops=2 * width * inside * 256, bytes_accessed=2 * width * inside, transcendentals=0
        ),
        name="out_adapter",
    )(dt, weight, u, down, up, factor, norm, dm_pair, dm_own)


def chunks_of(columns, width):
    return [(left, min(left + width, columns)) for left in range(0, columns, width)]


def feed_prepare_kernel(
    index_ref, base_ref, cbase_ref, down_ref, up_ref, cdown_ref, cup_ref, out_ref, square_ref
):
    quarter = base_ref.shape[2]
    for member in range(2):
        merged_block = base_ref[member].astype(F32) + SCALE * mm(down_ref[member].astype(BF), up_ref[member].astype(BF))
        out_ref[0, :, member * quarter : (member + 1) * quarter] = merged_block.astype(BF)
    merged_block = cbase_ref[...].astype(F32) + SCALE * mm(cdown_ref[...].astype(BF), cup_ref[...].astype(BF))
    out_ref[0, :, 2 * quarter :] = merged_block.T.astype(BF)
    square_ref[0] = jnp.sum(merged_block * merged_block, axis=0, keepdims=True)


def feed_prepare(core, place, base, cbase, down, up, cdown, cup_columns):
    unit = base.shape[1]
    quarter = base.shape[2] // 4
    rank = up.shape[1]
    at = lambda i, index: 2 * i + index[0]
    return pl.pallas_call(
        feed_prepare_kernel,
        grid_spec=pltpu.PrefetchScalarGridSpec(
            num_scalar_prefetch=1,
            grid=(2,),
            in_specs=[
                pl.BlockSpec((2, unit, quarter), lambda i, index: (0, 0, at(i, index))),
                pl.BlockSpec((quarter, unit), lambda i, index: (at(i, index), 0)),
                pl.BlockSpec((2, unit, rank), lambda i, index: (0, index[1], 0)),
                pl.BlockSpec((2, rank, quarter), lambda i, index: (0, 0, at(i, index))),
                pl.BlockSpec((quarter, rank), lambda i, index: (at(i, index), 0)),
                pl.BlockSpec((rank, unit), lambda i, index: (0, 0)),
            ],
            out_specs=[
                pl.BlockSpec((1, unit, 3 * quarter), lambda i, index: (i, 0, 0)),
                pl.BlockSpec((1, 1, unit), lambda i, index: (i, 0, 0)),
            ],
        ),
        out_shape=[
            jax.ShapeDtypeStruct((2, unit, 3 * quarter), BF),
            jax.ShapeDtypeStruct((2, 1, unit), F32),
        ],
        cost_estimate=pl.CostEstimate(
            flops=12 * unit * quarter * rank, bytes_accessed=24 * unit * quarter, transcendentals=0
        ),
        name="feed_prepare",
    )(jnp.stack([core, place]).astype(jnp.int32), base, cbase, down, up, cdown, cup_columns)


def feed_kernel(
    known_norm, h_ref, h_pair_ref, g_ref, g_pair_ref, weight_ref, m_ref, norm_in_ref, gs_ref, down_ref, up_ref, cdown_ref,
    cup_ref, back_ref, back_pair_ref, out_ref, out_pair_ref, shared_ref, quad_ref, dm_ref, norm_ref, cross_ref,
    ccross_ref, we_ref, wc_ref, dt_ref, hid_ref, sems
):
    half, width = h_ref.shape
    block = 2 * half
    quarter = wc_ref.shape[1]
    rank = cup_ref.shape[0]
    parts = chunks_of(quarter, 512)

    def copies(index, left, right):
        target = ((we_ref, left), (we_ref, quarter + left), (wc_ref, left))
        return [
            pltpu.make_async_copy(
                weight_ref.at[:, pl.ds(kind * quarter + left, right - left)], vmem.at[:, pl.ds(start, right - left)],
                sems.at[3 * index + kind],
            )
            for kind, (vmem, start) in enumerate(target)
        ]

    for index, (left, right) in enumerate(parts):
        for copy in copies(index, left, right):
            copy.start()
    if known_norm:
        norm_ref[...] = norm_in_ref[...]
    dt_ref[block:, :] = jnp.zeros((2 * rank, 2 * quarter), BF)
    h = jnp.concatenate([h_ref[...], h_pair_ref[...]], axis=0)
    g = jnp.concatenate([g_ref[...], g_pair_ref[...]], axis=0)
    g = (g.astype(F32) * gs_ref[...]).astype(BF)
    inputs = h if known_norm else jnp.concatenate([h, down_ref[...]], axis=0)
    for index, (left, right) in enumerate(parts):
        near, far = slice(left, right), slice(quarter + left, quarter + right)

        for copy in copies(index, left, right):
            copy.wait()
        if not known_norm:
            for part in (near, far):
                wide = we_ref[:, part].astype(F32)
                norm_ref[:, part] = jnp.sqrt(jnp.sum(wide * wide, axis=0, keepdims=True))
        gate_t = mm(inputs, we_ref[:, near])
        up_t = mm(inputs, we_ref[:, far])
        if not known_norm:
            cross_ref[:, near], cross_ref[:, far] = gate_t[block:], up_t[block:]
            gate_t, up_t = gate_t[:block], up_t[:block]
        grad = mm(g, wc_ref[:, near])
        gate_s = m_ref[:, near] / norm_ref[:, near]
        up_s = m_ref[:, far] / norm_ref[:, far]
        gate = gate_t * gate_s
        up = up_t * up_s
        sigmoid = 1.0 / (1.0 + jnp.exp(-gate))
        silu = gate * sigmoid
        hid_ref[:, near] = (silu * up).astype(BF)
        up_grad = grad * silu
        gate_grad = grad * up * (sigmoid + silu * (1.0 - sigmoid))
        dm_ref[:, near] = jnp.sum(gate_grad * gate_t, axis=0, keepdims=True)
        dm_ref[:, far] = jnp.sum(up_grad * up_t, axis=0, keepdims=True)
        dt_ref[:block, near] = (gate_grad * gate_s).astype(BF)
        dt_ref[:block, far] = (up_grad * up_s).astype(BF)

    norm = norm_ref[...]
    pull = -m_ref[...] * dm_ref[...] / (norm * norm * norm)
    for member in range(2):
        part = slice(member * quarter, (member + 1) * quarter)
        dt_ref[block + member * rank : block + (member + 1) * rank, part] = (up_ref[member] * pull[:, part]).astype(BF)
    both = nt(dt_ref[...], we_ref[...])
    back_ref[...] = both[:half].astype(BF)
    back_pair_ref[...] = both[half:block].astype(BF)
    hidden = hid_ref[...]
    if known_norm:
        out = nt(hidden, wc_ref[...])
        cross_ref[...] = jnp.zeros_like(cross_ref)
        ccross_ref[...] = jnp.zeros_like(ccross_ref)
    else:
        out = nt(jnp.concatenate([hidden, cdown_ref[...]], axis=0), wc_ref[...])
        ccross_ref[...] = out[block:]
    out_ref[...] = out[:half].astype(BF)
    out_pair_ref[...] = out[half:block].astype(BF)
    low = nt(down_ref[...], h).astype(BF)
    low_grads = []
    for member in range(2):
        rows = slice(member * rank, (member + 1) * rank)
        dt = dt_ref[:block, member * quarter : (member + 1) * quarter]
        low_grads.append(nt(up_ref[member].astype(BF), dt).astype(BF))
        quad_ref[rows] = mm(low[rows], dt)
    shared_ref[: 2 * rank] = both[block:] + mm(jnp.concatenate(low_grads, axis=0), h)
    quad_ref[2 * rank :] = mm(nt(cup_ref[...], g).astype(BF), hidden)
    shared_ref[2 * rank :] = mm(nt(cdown_ref[...], hidden).astype(BF), g)


def feed_forward_back(h, h_pair, g, g_pair, weight, magnitude, norm, factor, down, up, cdown, cup):
    half, width = h.shape
    quarter = weight.shape[1] // 3
    double = 2 * quarter
    rank = cup.shape[0]
    block = 2 * half
    known = norm is not None
    vmem = pl.BlockSpec(memory_space=pltpu.VMEM)
    any_space = pl.BlockSpec(memory_space=pl.ANY)
    rows = jax.ShapeDtypeStruct((half, width), BF)
    return pl.pallas_call(
        functools.partial(feed_kernel, known),
        in_specs=[vmem] * 4 + [any_space] + [vmem] * 7,
        out_specs=[vmem] * 10,
        out_shape=[
            rows, rows, rows, rows,
            jax.ShapeDtypeStruct((3 * rank, width), F32),
            jax.ShapeDtypeStruct((3 * rank, quarter), F32),
            jax.ShapeDtypeStruct((1, double), F32),
            jax.ShapeDtypeStruct((1, double), F32),
            jax.ShapeDtypeStruct((2 * rank, double), F32),
            jax.ShapeDtypeStruct((rank, width), F32),
        ],
        scratch_shapes=[
            pltpu.VMEM((width, double), BF),
            pltpu.VMEM((width, quarter), BF),
            pltpu.VMEM((block + 2 * rank, double), BF),
            pltpu.VMEM((block, quarter), BF),
            pltpu.SemaphoreType.DMA((3 * len(chunks_of(quarter, 512)),)),
        ],
        compiler_params=pltpu.CompilerParams(vmem_limit_bytes=58 << 20),
        cost_estimate=pl.CostEstimate(
            flops=12 * block * width * quarter, bytes_accessed=6 * width * quarter + 8 * block * width,
            transcendentals=block * quarter,
        ),
        name="feed_forward_back",
    )(h, h_pair, g, g_pair, weight, magnitude, norm if known else magnitude, factor, down, up, cdown, cup)


def feed_adapter_kernel(
    shared_far_ref, shared_ref, quad_far_ref, quad_ref, cross_ref, ccross_ref, up_ref, cup_ref, contract_ref, pull_ref,
    dm_ref, cpull_ref, cdm_ref, out_ref, quad_out_ref
):
    rank = cup_ref.shape[0]
    quarter = contract_ref.shape[1]
    cpull = cpull_ref[...]
    shared = shared_far_ref[...] + shared_ref[...]
    quads = quad_far_ref[...] + quad_ref[...]
    words_out(out_ref, 0, SCALE * shared[: 2 * rank])
    words_out(out_ref, 2 * rank, SCALE * (shared[2 * rank :] + ccross_ref[...] * cpull))
    words_out(out_ref, 3 * rank, row_of(cdm_ref[...]))
    for member in range(2):
        part = slice(member * quarter, (member + 1) * quarter)
        rows = slice(member * rank, (member + 1) * rank)
        words_out(quad_out_ref, member * rank, SCALE * (quads[rows] + cross_ref[rows, part] * pull_ref[:, part]))
    frozen = mm((cup_ref[...].astype(F32) * cpull).astype(BF), contract_ref[...])
    words_out(quad_out_ref, 2 * rank, SCALE * (quads[2 * rank :] + frozen))
    both = jnp.concatenate([dm_ref[:, :quarter], dm_ref[:, quarter:]], axis=0)
    words_out(quad_out_ref, 3 * rank, row_of(both))


def feed_adapter(*operands):
    rank, width = operands[7].shape
    quarter = operands[8].shape[1] // 3
    specs = [pl.BlockSpec(memory_space=pltpu.VMEM) for _ in operands]
    specs[8] = pl.BlockSpec((width, quarter), lambda i: (0, 2))
    return pl.pallas_call(
        feed_adapter_kernel,
        grid=(1,),
        in_specs=specs,
        out_specs=[pl.BlockSpec(memory_space=pltpu.VMEM)] * 2,
        out_shape=[
            jax.ShapeDtypeStruct((width // WORD, 3 * rank + 8, WORD), F32),
            jax.ShapeDtypeStruct((-(-quarter // WORD), 3 * rank + 8, WORD), F32),
        ],
        compiler_params=pltpu.CompilerParams(vmem_limit_bytes=48 << 20),
        cost_estimate=pl.CostEstimate(
            flops=2 * 256 * width * quarter, bytes_accessed=3 * width * quarter, transcendentals=0
        ),
        name="feed_adapter",
    )(*operands)


def turn_back_kernel(rotated, g_ref, t_ref, s_ref, r_ref, cos_ref, sin_ref, dt_ref, dm_ref):
    grad = g_ref[...]

    def finish(plain):
        dt_ref[0] = (plain * s_ref[...]).astype(BF)
        dm_ref[...] = jnp.sum(plain * t_ref[...].astype(F32), axis=0, keepdims=True) * r_ref[...]

    @pl.when(pl.program_id(0) < rotated)
    def _():
        finish(turned(grad, cos_ref[...], -sin_ref[...]))

    @pl.when(pl.program_id(0) >= rotated)
    def _():
        finish(grad)


def turn_back(grads, t, factor, inverse, cosine, sine):
    rows, columns = t.shape
    whole = lambda j: (0, 0)
    strip = lambda j: (0, j)
    heads = columns // HEAD_DIM
    each = heads // 3
    return pl.pallas_call(
        functools.partial(turn_back_kernel, 2 * each),
        grid=(heads,),
        in_specs=[
            pl.BlockSpec((rows, HEAD_DIM), strip),
            pl.BlockSpec((rows, HEAD_DIM), strip),
            pl.BlockSpec((1, HEAD_DIM), strip),
            pl.BlockSpec((1, HEAD_DIM), strip),
            pl.BlockSpec((rows, HEAD_DIM), whole),
            pl.BlockSpec((rows, HEAD_DIM), whole),
        ],
        out_specs=[
            pl.BlockSpec((1, rows, HEAD_DIM), lambda j: (j // each, 0, j % each)),
            pl.BlockSpec((1, HEAD_DIM), strip),
        ],
        out_shape=[
            jax.ShapeDtypeStruct((3, rows, columns // 3), BF),
            jax.ShapeDtypeStruct((1, columns), F32),
        ],
        name="turn_back",
    )(grads, t, factor, inverse, cosine, sine)


def unpacked(words, columns):
    return jnp.concatenate([words[i] for i in range(words.shape[0])], axis=1)[:, :columns]


def pad_rows(a, multiple):
    short = -a.shape[0] % multiple
    return jnp.pad(a, ((0, short), (0, 0))) if short else a


def halve(a, name, index):
    parts = a.reshape(2, a.shape[0] // 2, a.shape[1])
    return take(parts, index, 0) + swap(take(parts, 1 - index, 0).astype(BF), name).astype(F32)


def join(a, name, index):
    return pair(a, swap(a, name), index).reshape(2 * a.shape[0], a.shape[1])


def spread(a, name):
    size, place = lax.axis_size(name), lax.axis_index(name)
    parts = a.reshape(size, a.shape[0] // size, a.shape[1])
    total = take(parts, place, 0)
    for step in range(1, size):
        total = total + shift(take(parts, (place + step) % size, 0).astype(BF), name, step).astype(F32)
    return total


def collect(a, name):
    size, place = lax.axis_size(name), lax.axis_index(name)
    buffer = jnp.zeros((size,) + a.shape, a.dtype)
    buffer = put(buffer, a, place, 0)
    for step in range(1, size):
        buffer = put(buffer, shift(a, name, step), (place - step) % size, 0)
    return buffer.reshape(size * a.shape[0], a.shape[1])


def reduce_all(shared, by_core, by_quad, first_beside, beside):
    c, x = lax.axis_index("core"), lax.axis_index("xx")
    unit = lax.axis_size("yy") * lax.axis_size("seq")
    half = halve(pad_rows(shared, 16), "core", c)
    quarter = halve(pad_rows(jnp.concatenate([half, by_core], axis=0), 16), "xx", x)
    last = pad_rows(jnp.concatenate([quarter, by_quad], axis=0), 8 * unit)
    last, first_beside = lax.optimization_barrier((last, first_beside))
    last = spread(spread(last, "yy"), "seq").astype(BF)
    last, beside = lax.optimization_barrier((last, beside))
    last = collect(collect(last, "seq"), "yy")
    joined = join(last[: quarter.shape[0]], "xx", x)
    everywhere = join(joined[: half.shape[0]], "core", c)
    mine = joined[half.shape[0] : half.shape[0] + by_core.shape[0]]
    cores = pair(mine, swap(mine, "core"), c)
    mine = last[quarter.shape[0] : quarter.shape[0] + by_quad.shape[0]]
    both = pair(mine, swap(mine, "xx"), x)
    quads = pair(both, swap(both, "core"), c, axis=1)
    return everywhere, cores, quads, first_beside, beside


def body(
    tokens,
    cotangent,
    attention_base,
    expand_base,
    contract_base,
    attention_down,
    attention_up,
    attention_magnitude,
    expand_down,
    expand_up,
    expand_magnitude,
    contract_down,
    contract_up,
    contract_magnitude,
    prompt_length,
    response_length,
):
    y, x = lax.axis_index("yy"), lax.axis_index("xx")
    c, z = lax.axis_index("core"), lax.axis_index("seq")
    ny, count = lax.axis_size("yy"), lax.axis_size("seq")
    own_rows, local, width = tokens.shape
    rows = 2 * own_rows
    split = count // rows
    piece = local // (2 * split)
    half = count * piece
    blocks = ny * 2
    rank = attention_down.shape[-1]
    unit = attention_base.shape[1]
    hidden_size = expand_base.shape[-1]
    quarter = hidden_size // 4
    place = ((y * 2 + x) * 2 + c) * count + z
    sub = z % split

    def by_core(a):
        shaped = a.reshape(a.shape[:-1] + (blocks, 2, a.shape[-1] // blocks // 2))
        axis = a.ndim
        flat = a.shape[:-1] + (a.shape[-1] // 2,)
        return take(shaped, c, axis).reshape(flat), take(shaped, 1 - c, axis).reshape(flat)

    def by_quarter(a):
        shaped = a.reshape(a.shape[:-1] + (4, quarter))
        return take(shaped, 2 * x + c, a.ndim - 1)

    down_rows = lax.dynamic_slice_in_dim(attention_down, place * unit, unit, 1)
    attention = merged(attention_base, down_rows, attention_up)
    mine, other = by_core(attention[:3])
    mine = mine.transpose(1, 0, 2).reshape(unit, -1)
    other = other.transpose(1, 0, 2).reshape(unit, -1)
    qkv_piece = pair(mine, swap(other, "core"), c)
    out_halves = jnp.stack([attention[3][:, : width // 2], attention[3][:, width // 2 :]])
    attention_piece = jnp.concatenate([qkv_piece, out_halves], axis=2)
    (
        attention_piece, tokens, cotangent, expand_base, contract_base, attention_down, attention_up,
        attention_magnitude, expand_down, expand_up, expand_magnitude, contract_down, contract_up, contract_magnitude,
        prompt_length, response_length,
    ) = lax.optimization_barrier((
        attention_piece, tokens, cotangent, expand_base, contract_base, attention_down, attention_up,
        attention_magnitude, expand_down, expand_up, expand_magnitude, contract_down, contract_up, contract_magnitude,
        prompt_length, response_length,
    ))

    def relayout_start(a):
        shaped = a.reshape(own_rows, split, 2, piece, width)
        kept, sent = take(shaped, c, 2), take(shaped, 1 - c, 2)
        return pair(kept, swap(sent, "core"), c).reshape(count, piece, width)

    contract_columns = lax.dynamic_slice_in_dim(contract_up, place * unit, unit, 1)
    prepare = lambda core: feed_prepare(
        core, place, expand_base, contract_base, expand_down, expand_up, contract_down, contract_columns
    )
    feed_other, square_other = prepare(1 - c)
    feed_mine, square_mine = prepare(c)
    feed_other = swap(feed_other, "core")
    feed_near = pair(take(feed_mine, x, 0), take(feed_other, x, 0), c)
    feed_far = pair(take(feed_mine, 1 - x, 0), take(feed_other, 1 - x, 0), c)

    boxes = {
        "a0": Box(attention_piece),
        "m0": Box(feed_near),
        "feed": Box(feed_far),
        "tokens": Box(relayout_start(tokens)),
        "cotangent": Box(relayout_start(cotangent)),
    }
    inside = width // 2

    def qkv_place(turn, column, step):
        def of(block):
            part = block[..., : 3 * inside].reshape(1, 1, 2, 1, unit, 3 * inside)
            return part, [(y - turn) % ny, column, 0, (z - step) % count, 0, 0]

        return of

    def out_place(turn, column, step):
        def of(block):
            part = block[..., 3 * inside :].reshape(2, 1, 1, 1, unit, inside)
            return part, [0, (y - turn) % ny, column, (z - step) % count, 0, 0]

        return of

    def feed_place(turn, index, step):
        def of(block):
            return block.reshape(1, 1, 2, 1, unit, 3 * quarter), [(y - turn) % ny, index, 0, (z - step) % count, 0, 0]

        return of

    qkv_places, out_places, feed_places = {}, {}, {}
    for step in range(count):
        for turn in range(ny):
            tail = f"{step}y{turn}" if turn else f"{step}"
            for name, column in (("a" + tail, x), ("a" + tail + "x", 1 - x)):
                qkv_places[name] = qkv_place(turn, column, step)
                out_places[name] = out_place(turn, column, step)
            for index, side in ((x, "m"), (1 - x, "n")):
                feed_places[side + tail] = feed_place(turn, index, step)
    buffers = {
        "qkv": Buffer((ny, 2, 2, count, unit, 3 * inside), 4, qkv_places),
        "out": Buffer((2, ny, 2, count, unit, inside), 4, out_places),
        "feed": Buffer((ny, 2, 2, count, unit, 3 * quarter), 0, feed_places),
    }
    for name in ("qkv", "out"):
        buffers[name].put("a0", attention_piece)
    buffers["feed"].put("m0", feed_near)
    links = Links(2, boxes, buffers)
    cross_x = lambda a: swap(a, "xx")
    ring = lambda a: shift(a, "seq", 1)
    exchange = lambda a: lax.all_to_all(a, "seq", 0, 0, tiled=True)
    turns = range(1, ny)

    def moves_y(kind, step):
        return [(f"{kind}{step}", f"{kind}{step}y{turn}", functools.partial(shift, name="yy", step=turn)) for turn in turns]

    sides = "mn"
    back = lambda a: shift(a, "seq", -1)
    order = []
    for step in range(1, count):
        order.append((step - 1, step, ring))
    attention_z = [(f"a{source}", f"a{step}", move) for source, step, move in order]
    feed_z = [(f"{side}{source}", f"{side}{step}", move) for source, step, move in order for side in sides]
    z_queue = attention_z[:2] + [("tokens", "tokens_moved", exchange), ("cotangent", "cotangent_moved", exchange)]
    z_queue += attention_z[2:] + feed_z
    x_queue = [("a0", "a0x", cross_x)]
    y_queue = []
    late_x = [("cotangent_moved", "cotangent_far", cross_x)]
    steps = [0] + [step for _, step, _ in order]
    feed_moves = [move for step in steps for side in sides for move in moves_y(side, step)]
    for place_of, step in enumerate(steps):
        names = [f"a{step}"] + [f"a{step}y{turn}" for turn in turns]
        x_queue += [(name, name + "x", cross_x) for name in names if name != "a0"]
        if step == 0:
            x_queue.append(("feed", "n0", cross_x))
        y_queue += moves_y("a", step)
        if place_of >= 1:
            y_queue += feed_moves[:1]
            del feed_moves[:1]
    y_queue += feed_moves

    x_queue += late_x
    links.run([z_queue, x_queue, y_queue])
    links.place(len(links.rounds) - 2)
    while qkv_places:
        links.place(links.placed + 1)
    qkv_weight = buffers["qkv"].array.reshape(width, 3 * inside)
    out_weight = buffers["out"].array.reshape(2, inside, inside)
    tokens_own = boxes["tokens_moved"].array.reshape(half, width)
    tokens_both = jnp.concatenate([tokens_own, swap(tokens_own, "core")], axis=0)
    cotangent_own = boxes["cotangent_moved"].array.reshape(half, width)
    cotangent_far = boxes["cotangent_far"].array.reshape(half, width)

    def positions_of(sub_place, core_place):
        source = jnp.arange(count, dtype=jnp.int32)[:, None] * local
        inner = sub_place * 2 * piece + core_place * piece + jnp.arange(piece, dtype=jnp.int32)[None]
        return (source + inner).reshape(half)

    query_place = jnp.concatenate([positions_of(sub, c), positions_of(sub, 1 - c)])
    key_place = jnp.concatenate(
        [positions_of((sub - step) % split, side) for step in range(split) for side in (c, 1 - c)]
    )
    totals = (prompt_length + response_length).astype(F32)
    total = take(pair(totals, swap(totals, "core"), c).reshape(rows), z // split, 0).astype(jnp.int32)
    allowed = (key_place[None] <= query_place[:, None]) & (key_place[None] < total)
    bias = jnp.where(allowed, 0.0, -1e30).astype(F32)
    frequency = 10000.0 ** (-jnp.arange(HEAD_DIM // 2).astype(F32) / (HEAD_DIM // 2))
    angles = query_place.astype(F32)[:, None] * frequency[None]
    cosine = jnp.concatenate([jnp.cos(angles)] * 2, axis=1)
    sine = jnp.concatenate([-jnp.sin(angles), jnp.sin(angles)], axis=1)

    heads = width // 2 // HEAD_DIM
    rows_both = tokens_both.astype(F32)
    first = rms(rows_both).astype(BF)
    magnitude = by_core(attention_magnitude[:3])[0].reshape(1, -1)
    downs = attention_down[:3].transpose(0, 2, 1).reshape(3 * rank, width).astype(BF)
    qkv_t, qkv_p, qkv_norm, cross = qkv_forward(first, qkv_weight, downs, magnitude, cosine, sine)

    def share(a, step):
        perm = [(i, (i // split) * split + (i % split + step) % split) for i in range(count)]
        return lax.ppermute(a, "seq", perm)

    feed_buffer = buffers["feed"]
    if split == 1:
        kv, offsets = qkv_p, (heads, 2 * heads)
    else:
        own_kv = qkv_p[:, heads * HEAD_DIM :]
        kv = jnp.concatenate([own_kv] + [share(own_kv, step) for step in range(1, split)], axis=0)
        offsets = (0, heads)
    (mixed,) = attention_call(
        attend_kernel, "attend", heads, qkv_p, kv, offsets, [], bias, [(2 * half, BF)]
    )

    def core_scatter(partial):
        return partial[:half].astype(F32) + swap(partial[half:].astype(BF), "core").astype(F32)

    def core_join(own):
        return jnp.concatenate([own, swap(own, "core")], axis=0)

    out_rows = by_core(attention_down[3].T)[0].astype(BF)
    contract_square = (square_other + square_mine).sum(axis=0)
    qkv_p, contract_square = lax.optimization_barrier((qkv_p, contract_square))
    contract_square = join(join(collect(contract_square, "seq"), "core", c), "xx", x)
    contract_square = collect(contract_square, "yy").reshape(1, width)
    mixed, cotangent_far, out_weight, feed_buffer.array = lax.optimization_barrier(
        (mixed, cotangent_far, out_weight, feed_buffer.array)
    )
    links.place(len(links.rounds))
    feed_weight = feed_buffer.array.reshape(width, 3 * quarter)
    out_square = jnp.sum(out_weight.astype(F32) ** 2, axis=1).reshape(1, width)
    out_norm = jnp.sqrt(out_square + swap(out_square, "core"))
    out_scale = attention_magnitude[3:] / out_norm
    out_sent = [mm(mixed[half:], out_weight[i]).astype(BF) for i in range(2)]
    out_sent = swap(jnp.concatenate(out_sent, axis=1), "core").astype(F32)
    out_t = jnp.concatenate([mm(mixed[:half], out_weight[i]) for i in range(2)], axis=1) + out_sent
    rows_own = tokens_own.astype(F32)
    middle = rows_own + out_t * out_scale
    second_own = rms(middle).astype(BF)
    second_far = swap(second_own, "xx")
    second_near = (second_own, swap(second_own, "core"))
    second_far = (second_far, swap(second_far, "core"))
    low = nt(downs, first).astype(BF).reshape(3, rank, 2 * half)
    cross = jnp.stack(
        [cross[i * rank : (i + 1) * rank, i * width // 2 : (i + 1) * width // 2] for i in range(3)]
    )
    second_far, cross, low = lax.optimization_barrier((second_far, cross, low))

    gate_up = jnp.stack([by_quarter(expand_up[i]) for i in range(2)])
    feed_downs = expand_down.transpose(0, 2, 1).reshape(2 * rank, width).astype(BF)
    contract_rows = take(contract_down.T.reshape(rank, 4, quarter), 2 * x + c, 1).astype(BF)
    contract_ups = contract_up.astype(BF)
    expand_magnitudes = by_quarter(expand_magnitude).reshape(1, -1)
    grad_own = cotangent_own.astype(F32)
    cotangent_near = (cotangent_own, swap(cotangent_own, "core"))
    cotangent_far = (cotangent_far, swap(cotangent_far, "core"))
    contract_norm = jnp.sqrt(contract_square)
    contract_scale = contract_magnitude[None] / contract_norm
    def total(kept, sent):
        return kept.astype(F32) + swap(sent, "core").astype(F32)

    (
        back_far, back_sent, out_far, out_sent, shared_far, quads_far, dm_far, expand_norm, expand_cross, contract_cross
    ) = feed_forward_back(
        *second_far, *cotangent_far, feed_weight, expand_magnitudes, None, contract_scale,
        feed_downs, gate_up, contract_rows, contract_ups,
    )
    back_far = total(back_far, back_sent).astype(BF)
    second_near, back_far = lax.optimization_barrier((second_near, back_far))
    back_near, back_sent, out_near, out_near_sent, shared_near, quads_near, dm_near = feed_forward_back(
        *second_near, *cotangent_near, feed_weight, expand_magnitudes, expand_norm, contract_scale,
        feed_downs, gate_up, contract_rows, contract_ups,
    )[:7]
    back_near, back_sent, back_far = lax.optimization_barrier((back_near, back_sent, swap(back_far, "xx")))
    second_grad = total(back_near, back_sent) + back_far.astype(F32)
    middle_grad = grad_own + rms_back(middle, second_grad)

    out_dm = jnp.sum(middle_grad * out_t, axis=0, keepdims=True) / out_norm
    out_dt = core_join((middle_grad * out_scale).astype(BF))
    mixed_grad = sum(nt(out_dt[:, i * inside : (i + 1) * inside], out_weight[i]) for i in range(2)).astype(BF)
    out_far, back_far = lax.optimization_barrier((total(out_far, out_sent).astype(BF), back_far))
    out_far = swap(out_far, "xx")
    keys = 2 * half * split
    members = lambda a: a.reshape(3, 1, width // 2)
    qkv_scale = magnitude / qkv_norm

    def reunite(a):
        parts = a.reshape(split, 2 * half, -1)
        total = parts[0]
        for step in range(1, split):
            total = total + share(parts[step].astype(BF), -step).astype(F32)
        return total

    if split > 1:
        dq, dk, dv = attention_call(
            attend_back_kernel, "attend_back", heads, qkv_p, kv, offsets, [mixed_grad], bias,
            [(2 * half, F32), (keys, F32), (keys, F32)],
        )
        grads = jnp.concatenate([dq, reunite(dk), reunite(dv)], axis=1)
        qkv_dt, qkv_dm = turn_back(grads, qkv_t, qkv_scale, 1.0 / qkv_norm, cosine, sine)
        qkv_dm = members(qkv_dm)
    else:
        qkv_dt, qkv_dm = attend_back_turn(
            heads, qkv_p, mixed_grad, bias, qkv_t, members(qkv_scale), members(1.0 / qkv_norm), cosine, sine
        )
    core_up = by_core(attention_up[:3])[0]
    def restore_start(own):
        return lax.all_to_all(own.reshape(count, piece, width), "seq", 0, 0, tiled=True)

    qkv_dt, out_far, out_near, out_near_sent = lax.optimization_barrier((qkv_dt, out_far, out_near, out_near_sent))
    contract_t = total(out_near, out_near_sent) + out_far.astype(F32)
    output_own = (middle + contract_t * contract_scale).astype(BF)
    layer_moved = restore_start(output_own)
    first_part, qkv_shared, qkv_core = qkv_back(
        qkv_dt, qkv_weight, first, low, core_up, cross, members(qkv_scale), members(qkv_norm), qkv_dm
    )
    first_grad = core_scatter(first_part)
    tokens_grad_own = middle_grad + rms_back(rows_own, first_grad)

    def restore_end(moved):
        shaped = moved.reshape(2, own_rows, split, piece, width)
        kept, sent = take(shaped, c, 0), take(shaped, 1 - c, 0)
        return pair(kept, swap(sent, "core"), c, axis=2).reshape(own_rows, local, width)

    expand_sum = dm_near + dm_far
    expand_pull = -expand_magnitudes * expand_sum / (expand_norm * expand_norm * expand_norm)
    contract_dm = jnp.sum(grad_own * contract_t, axis=0, keepdims=True) / contract_norm
    contract_sum = contract_dm + swap(contract_dm, "core")
    contract_sum = contract_sum + swap(contract_sum, "xx")
    contract_pull = -contract_scale * contract_sum / contract_norm
    feed_words, feed_quad_words = feed_adapter(
        shared_far, shared_near, quads_far, quads_near, expand_cross, contract_cross, gate_up, contract_ups,
        feed_weight, expand_pull, expand_sum / expand_norm, contract_pull, contract_dm,
    )
    flat = lambda a: a.reshape(-1, WORD)

    out_words, out_core_words = out_adapter(
        out_dt, out_weight, mixed, out_rows, attention_up[3], out_scale, out_norm,
        out_dm + swap(out_dm, "core"), out_dm,
    )
    dm_words = jnp.pad(qkv_dm[:, 0], ((0, 5), (0, 0)))
    dm_words = jnp.stack([dm_words[:, i : i + WORD] for i in range(0, width // 2, WORD)])
    shared = jnp.concatenate([flat(qkv_shared), flat(out_words), flat(feed_words)])
    cores = jnp.concatenate([flat(qkv_core), flat(dm_words), flat(out_core_words)])
    attention_shared, attention_cores, feed_quads, layer_moved, tokens_moved = reduce_all(
        shared, cores, flat(feed_quad_words), layer_moved, restore_start(tokens_grad_own.astype(BF))
    )
    used = flat(qkv_shared).shape[0] + flat(out_words).shape[0]
    feed_shared = attention_shared[used:]

    def interleave(parts):
        shaped = [p.reshape(p.shape[0], blocks, 1, -1) for p in parts]
        return jnp.concatenate(shaped, axis=2).reshape(parts[0].shape[0], -1)

    used = flat(qkv_shared).shape[0]
    qkv_down_all = unpacked(attention_shared[:used].reshape(qkv_shared.shape), width)
    out_all = unpacked(attention_shared[used : used + flat(out_words).shape[0]].reshape(out_words.shape), width)
    core_parts = []
    for side in range(2):
        start, parts = 0, []
        for words in (qkv_core, dm_words, out_core_words):
            used = flat(words).shape[0]
            parts.append(unpacked(attention_cores[side, start : start + used].reshape(words.shape), width // 2))
            start += used
        core_parts.append(parts)
    qkv_up_all, qkv_dm_all, out_down_all = (interleave([core_parts[0][i], core_parts[1][i]]) for i in range(3))
    attention_down_grad = (
        jnp.concatenate([qkv_down_all, out_down_all]).reshape(4, rank, width).transpose(0, 2, 1)
    )
    attention_up_grad = jnp.concatenate([qkv_up_all, out_all[:rank]]).reshape(4, rank, width)
    attention_magnitude_grad = jnp.concatenate([qkv_dm_all[:3], out_all[rank : rank + 1]])

    feed_all = unpacked(feed_shared[: flat(feed_words).shape[0]].reshape(feed_words.shape), width)
    quad_all = jnp.concatenate(
        [unpacked(feed_quads[i, j].reshape(feed_quad_words.shape), quarter) for i in range(2) for j in range(2)],
        axis=1,
    )

    layer_output = restore_end(layer_moved)
    tokens_grad = restore_end(tokens_moved).astype(F32)
    return (
        layer_output,
        tokens_grad,
        attention_down_grad.astype(F32),
        attention_up_grad.astype(F32),
        attention_magnitude_grad.astype(F32),
        feed_all[: 2 * rank].reshape(2, rank, width).transpose(0, 2, 1).astype(F32),
        quad_all[: 2 * rank].reshape(2, rank, hidden_size).astype(F32),
        quad_all[3 * rank : 3 * rank + 2].astype(F32),
        quad_all[2 * rank : 3 * rank].T.astype(F32),
        feed_all[2 * rank : 3 * rank].astype(F32),
        feed_all[3 * rank].astype(F32),
    )


def solution(mesh):
    devices = mesh.devices
    chips = devices.shape[0] // 2
    fine = Mesh(devices.reshape(chips // 2, 2, 2, devices.shape[1]), ALL)
    dp = ("yy", "xx", "core")
    every = ("yy", "xx", "core", "seq")
    placed = (
        P(dp, "seq", None),
        P(dp, "seq", None),
        P(None, every, None),
        P(None, every, None),
        P(None, every),
        P(),
        P(),
        P(),
        P(),
        P(),
        P(),
        P(),
        P(),
        P(),
        P(dp),
        P(dp),
    )
    return jax.shard_map(
        body,
        mesh=fine,
        in_specs=placed,
        out_specs=(P(dp, "seq", None), P(dp, "seq", None)) + (P(),) * 9,
        check_vma=False,
    )
```

time: 801 us -> 647 us (0.81)
  waiting for transfers between devices: 290 us -> 198 us
  Pallas kernels: 146 us -> 130 us
  local copies, waits for them, and re-layouts: 156 us -> 141 us
  other arithmetic: 73.6 us -> 59.5 us
  matrix products: 29.5 us -> 19.2 us
  starting transfers between devices: 95.1 us -> 85.2 us
    ppermute x44 -> x33, waiting for transfers between devices: 176 us -> 98.9 us  [shift(): return lax.ppermute(a, name, [(i, (i + step) % size) for i in range(size)])]
    ppermute x57 -> x45, waiting for transfers between devices: 90.2 us -> 50.6 us  [swap(): return lax.ppermute(a, name, [(0, 1), (1, 0)])]
    all_to_all x4, waiting for transfers between devices: 23.3 us -> 48.7 us  [the longest x2 37.3 us: body(): exchange = lambda a: lax.all_to_all(a, 'seq', 0, 0, tiled=True)]
    broadcast_in_dim x5 -> x0, local copies, waits for them, and re-layouts: 17.5 us -> none  [the longest x4 17.4 us: build(): buffer = jnp.zeros(shape, piece.dtype)]
    pallas_call x4 -> x8, Pallas kernels: 86.5 us -> 73 us  [the longest x2 61.5 us: feed_forward_back(): pl.pallas_call(functools.partial(feed_kernel, known), in_specs=[vmem] * 4...]
    dynamic_update_slice x47, local copies, waits for them, and re-layouts: 70.4 us -> 83.2 us  [put(): lax.dynamic_update_slice(self.array, part, [jnp.int32(v) for v in start])]
    reduce_sum x4 -> x3, other arithmetic: 19.6 us -> 7.12 us  [the longest x1 3.74 us: body(): out_dm = jnp.sum(middle_grad * out_t, axis=0, keepdims=True) / out_norm]
    convert_element_type x5 -> x16, other arithmetic: 6.21 us -> 18.4 us  [the longest x1 3.09 us: body(): output_own = (middle + contract_t * contract_scale).astype(BF)]
  transfers between devices with their start and end apart: 105 -> 82, of which waited for: 42 -> 29; matrix products, arithmetic and copies ran while one was open for 29% -> 30% of each run, Pallas kernels for 12% -> 15%
where the time goes in v2:
time: 647 us; the launch traced here: 637 us
  waiting for transfers between devices  198 us (31%)
  local copies, waits for them, and re-layouts  141 us (22%)
  Pallas kernels  130 us (20%)
  starting transfers between devices  85.2 us (13%)
  other arithmetic  59.5 us (9%)
  matrix products  19.2 us (3%)
    ppermute x33, waiting for transfers between devices, shift(): return lax.ppermute(a, name, [(i, (i + step) % size) for i in range(size)])  98.9 us
    dynamic_update_slice x47, local copies, waits for them, and re-layouts, put(): lax.dynamic_update_slice(self.array, part, [jnp.int32(v) for v in start])  83.2 us
    pallas_call x2, Pallas kernels, feed_forward_back(): pl.pallas_call(functools.partial(feed_kernel, known), in_specs=[vmem] * 4...  61.5 us
    ppermute x45, waiting for transfers between devices, swap(): return lax.ppermute(a, name, [(0, 1), (1, 0)])  50.6 us
    ppermute x33, starting transfers between devices, shift(): return lax.ppermute(a, name, [(i, (i + step) % size) for i in range(size)])  47 us
    all_to_all x2, waiting for transfers between devices, body(): exchange = lambda a: lax.all_to_all(a, 'seq', 0, 0, tiled=True)  37.3 us
    ppermute x45, starting transfers between devices, swap(): return lax.ppermute(a, name, [(0, 1), (1, 0)])  22.5 us
    unnamed x220, local copies, waits for them, and re-layouts  20 us
  transfers between devices with their start and end apart: 82, of which 29 were waited for; matrix products, arithmetic and copies ran while one was open for 30% of the time, Pallas kernels for 15%

profile of v2, /device:TPU:0, one launch (start us, length us, event | category | flops | bytes accessed | tf_op | source)
XLA Modules:
  0.0 636.8 jit_solution(5141669673328057742)
XLA Ops:
  3.4 4.9 dynamic-slice_reduce_fusion.1
  15.8 2.5 collective-permute-start.4
  33.7 2.4 copy.103.cbase_ref
  36.1 3.9 feed_prepare.3
  40.0 3.9 feed_prepare.2
  67.9 3.5 all-to-all-start
  78.2 4.5 collective-permute-done.9
  96.3 7.3 %collective-permute-done.12 = bf16[2,64,4224]{2,1,0:T(8,128)(2,1)S(1)} collective-permute-done((bf16[2,64,4224]{2,1,0:T(8,128)(2,1)S(1)}, bf16[2,64,4224]{2,1,0:T(8,128)(2,1)S(1)}, u32[]{:S(2)}, u32[]{:S(2)}) %collective-permute-start.12) | collective-permute-done | bytes 1081376 | tf_op jit(solution)/shard_map/ppermute | solution.py:41
  103.6 2.3 collective-permute-done.11
  109.5 2.3 bitcast_dynamic-update-slice_fusion.14
  112.9 4.2 all-to-all-start.1
  117.1 9.0 %collective-permute-done.15 = bf16[2,64,4096]{2,1,0:T(8,128)(2,1)} collective-permute-done((bf16[2,64,4096]{2,1,0:T(8,128)(2,1)}, bf16[2,64,4096]{2,1,0:T(8,128)(2,1)}, u32[]{:S(2)}, u32[]{:S(2)}) %collective-permute-start.15) | collective-permute-done | bytes 1048608 | tf_op jit(solution)/shard_map/ppermute | solution.py:41
  128.8 5.8 collective-permute-done.13
  142.2 8.6 %collective-permute-done.16 = bf16[2,64,4096]{2,1,0:T(8,128)(2,1)} collective-permute-done((bf16[2,64,4096]{2,1,0:T(8,128)(2,1)}, bf16[2,64,4096]{2,1,0:T(8,128)(2,1)}, u32[]{:S(2)}, u32[]{:S(2)}) %collective-permute-start.16) | collective-permute-done | bytes 1048608 | tf_op jit(solution)/shard_map/ppermute | solution.py:36
  156.7 17.8 %collective-permute-done.19 = bf16[2,64,4224]{2,1,0:T(8,128)(2,1)S(1)} collective-permute-done((bf16[2,64,4224]{2,1,0:T(8,128)(2,1)}, bf16[2,64,4224]{2,1,0:T(8,128)(2,1)S(1)}, u32[]{:S(2)}, u32[]{:S(2)}) %collective-permute-start.19) | collective-permute-done | bytes 1081376 | tf_op jit(solution)/shard_map/ppermute | solution.py:41
  183.6 2.3 bitcast_dynamic-update-slice_fusion.12
  185.9 3.2 collective-permute-start.22
  190.7 7.2 %collective-permute-done.18 = bf16[2,64,4224]{2,1,0:T(8,128)(2,1)} collective-permute-done((bf16[2,64,4224]{2,1,0:T(8,128)(2,1)}, bf16[2,64,4224]{2,1,0:T(8,128)(2,1)}, u32[]{:S(2)}, u32[]{:S(2)}) %collective-permute-start.18) | collective-permute-done | bytes 1081376 | tf_op jit(solution)/shard_map/ppermute | solution.py:41
  205.9 3.1 collective-permute-start.25
  210.5 10.4 %collective-permute-done.22 = bf16[2,64,4224]{2,1,0:T(8,128)(2,1)S(1)} collective-permute-done((bf16[2,64,4224]{2,1,0:T(8,128)(2,1)S(1)}, bf16[2,64,4224]{2,1,0:T(8,128)(2,1)S(1)}, u32[]{:S(2)}, u32[]{:S(2)}) %collective-permute-start.22) | collective-permute-done | bytes 1081376 | tf_op jit(solution)/shard_map/ppermute | solution.py:41
  222.5 2.3 bitcast_dynamic-update-slice_fusion.10
  228.5 3.1 collective-permute-start.28
  231.5 37.3 %all-to-all-done.1 = bf16[4,64,2048]{2,1,0:T(8,128)(2,1)} async-done(((bf16[4,64,2048]{2,1,0:T(8,128)(2,1)}), bf16[4,64,2048]{2,1,0:T(8,128)(2,1)}, u32[]{:S(2)}, u32[]{:S(2)}) %all-to-all-start.1) | async-done | bytes 1048608 | tf_op jit(solution)/shard_map/all_to_all | solution.py:864
  276.7 2.5 bitcast_dynamic-update-slice_fusion.7
  279.2 2.5 bitcast_dynamic-update-slice_fusion.16
  281.7 14.4 %qkv_forward.1 = (bf16[512,3072]{1,0:T(8,128)(2,1)S(1)}, bf16[512,3072]{1,0:T(8,128)(2,1)S(1)}, f32[1,3072]{1,0:T(1,128)S(1)}, f32[48,3072]{1,0:T(8,128)S(1)}) custom-call(bf16[512,2048]{1,0:T(8,128)(2,1)S(1)} %copy-done.7, bf16[2048,3072]{1,0:T(8,128)(2,1)} %bitcast.95.v_ref, bf16[48,2048]{1,0:T(8,128)(2,1)S(1)} %bitcast.504, f32[1,3072]{1,0:T(1,128)S(1)} %bitcast.517, ...), custom_call_target="tpu_custom_call" | custom-call | flops 6442450944 | bytes 22020096 | tf_op jit(solution)/shard_map/qkv_forward/pallas_call | solution.py:174
  297.7 4.3 collective-permute-start.43
  303.7 2.4 bitcast_dynamic-update-slice_fusion.6
  306.1 2.3 bitcast_dynamic-update-slice_fusion.5
  309.8 3.0 collective-permute-done.45
  316.9 9.0 %attend.1.u_ref = bf16[512,1024]{1,0:T(8,128)(2,1)S(1)} custom-call(bf16[512,3072]{1,0:T(8,128)(2,1)S(1)} %get-tuple-element.408.q_ref.k_ref.v_ref, bf16[512,3072]{1,0:T(8,128)(2,1)S(1)} %get-tuple-element.408.q_ref.k_ref.v_ref, bf16[512,3072]{1,0:T(8,128)(2,1)S(1)} %get-tuple-element.408.q_ref.k_ref.v_ref, f32[512,512]{1,0:T(8,128)S(1)} %copy-done.4), custom_call_target="tpu_custom_call" | custom-call | flops 1073741824 | bytes 4194304 | tf_op jit(solution)/shard_map/attend/pallas_call | solution.py:238
  327.4 6.6 %collective-permute-done.48 = f32[16,64]{1,0:T(8,128)S(1)} collective-permute-done((f32[16,64]{1,0:T(8,128)S(1)}, f32[16,64]{1,0:T(8,128)S(1)}, u32[]{:S(2)}, u32[]{:S(2)}) %collective-permute-start.48) | collective-permute-done | bytes 4128 | tf_op jit(solution)/shard_map/ppermute | solution.py:41
  334.8 2.3 bitcast_dynamic-update-slice_fusion.4
  337.1 2.3 bitcast_dynamic-update-slice_fusion.3
  339.4 3.4 multiply_reduce_fusion
  342.7 2.3 fusion.32
  345.0 2.3 fusion.29
  348.0 2.4 bitcast_dynamic-update-slice_fusion.2
  351.1 2.3 fusion.13
  353.4 2.7 fusion.19
  359.8 2.4 bitcast_dynamic-update-slice_fusion.1
  362.1 23.0 %collective-permute-done.38.h_ref = bf16[256,2048]{1,0:T(8,128)(2,1)S(1)} collective-permute-done((bf16[256,2048]{1,0:T(8,128)(2,1)}, bf16[256,2048]{1,0:T(8,128)(2,1)S(1)}, u32[]{:S(2)}, u32[]{:S(2)}) %collective-permute-start.38) | collective-permute-done | bytes 1048608 | tf_op jit(solution)/shard_map/ppermute | solution.py:36
  389.8 31.0 %feed_forward_back.2 = (bf16[256,2048]{1,0:T(8,128)(2,1)}, bf16[256,2048]{1,0:T(8,128)(2,1)}, bf16[256,2048]{1,0:T(8,128)(2,1)}, bf16[256,2048]{1,0:T(8,128)(2,1...) custom-call(bf16[256,2048]{1,0:T(8,128)(2,1)} %copy-done.99, ...), custom_call_target="tpu_custom_call" | custom-call | flops 17716740096 | bytes 25690112 | tf_op jit(solution)/shard_map/feed_forward_back/pallas_call | solution.py:564
  427.7 30.5 %feed_forward_back.3 = (bf16[256,2048]{1,0:T(8,128)(2,1)}, bf16[256,2048]{1,0:T(8,128)(2,1)}, bf16[256,2048]{1,0:T(8,128)(2,1)}, bf16[256,2048]{1,0:T(8,128)(2,1...) custom-call(bf16[256,2048]{1,0:T(8,128)(2,1)} %multiply_convert_fusi, ...), custom_call_target="tpu_custom_call" | custom-call | flops 17716740096 | bytes 25690112 | tf_op jit(solution)/shard_map/feed_forward_back/pallas_call | solution.py:564
  463.9 2.7 dynamic-slice_reduce_fusion.2
  473.1 2.6 multiply_reduce_fusion.3
  475.8 3.7 multiply_reduce_fusion.2
  484.6 3.1 fusion.9
  487.7 3.2 add_convert_fusion.2.g_ref
  491.0 14.1 %attend_back_turn.1 = (bf16[3,512,1024]{2,1,0:T(8,128)(2,1)S(1)}, f32[3,1,1024]{2,1,0:T(1,128)S(1)}) custom-call(bf16[512,3072]{1,0:T(8,128)(2,1)} %copy-done.2, bf16[512,3072]{1,0:T(8,128)(2,1)} %copy-done.2, bf16[512,3072]{1,0:T(8,128)(2,1)} %copy-done.2, bf16[512,1024]{1,0:T(8,128)(2,1)S(1)} %add_convert_fusion.2.g_ref, f32[512,512]{1,0:T(8,128)S(1)} %copy-done.5, ...), custom_call_target="tpu_custom_call" | custom-call | flops 2684354560 | bytes 10485760 | tf_op jit(solution)/shard_map/attend_back_turn/pallas_call | solution.py:274
  506.7 2.4 collective-permute-done.55
  510.5 14.0 %qkv_back.1 = (bf16[512,2048]{1,0:T(8,128)(2,1)S(1)}, f32[4,48,512]{2,1,0:T(8,128)S(1)}, f32[2,48,512]{2,1,0:T(8,128)S(1)}) custom-call(bf16[3,512,1024]{2,1,0:T(8,128)(2,1)} %copy-done.48, bf16[2048,3072]{1,0:T(8,128)(2,1)} %bitcast.95.v_ref, bf16[512,2048]{1,0:T(8,128)(2,1)S(1)} %copy-done.8, bf16[3,16,512]{2,1,0:T(8,128)(2,1)S(1)} %bitcast.519, ...), custom_call_target="tpu_custom_call" | custom-call | flops 6442450944 | bytes 12582912 | tf_op jit(solution)/shard_map/qkv_back/pallas_call | solution.py:348
  528.5 3.1 add_convert_fusion
  534.4 5.2 out_adapter.1
  540.9 4.4 all-to-all-start.2
  549.0 3.6 feed_adapter.1
  557.3 2.8 fusion.8
  560.1 11.4 %all-to-all-done.2 = bf16[4,64,2048]{2,1,0:T(8,128)(2,1)} async-done(((bf16[4,64,2048]{2,1,0:T(8,128)(2,1)}), bf16[4,64,2048]{2,1,0:T(8,128)(2,1)}, u32[]{:S(2)}, u32[]{:S(2)}) %all-to-all-start.2) | async-done | bytes 1048608 | tf_op jit(solution)/shard_map/all_to_all | solution.py:1040
  571.6 3.5 all-to-all-start.3
  576.8 4.6 collective-permute-done.63
  587.3 10.6 %collective-permute-done.64 = bf16[48,512]{1,0:T(8,128)(2,1)S(1)} collective-permute-done((bf16[48,512]{1,0:T(8,128)(2,1)S(1)}, bf16[48,512]{1,0:T(8,128)(2,1)S(1)}, u32[]{:S(2)}, u32[]{:S(2)}) %collective-permute-start.64) | collective-permute-done | bytes 49184 | tf_op jit(solution)/shard_map/ppermute | solution.py:41
  598.0 6.7 %collective-permute-done.65 = bf16[48,512]{1,0:T(8,128)(2,1)S(1)} collective-permute-done((bf16[48,512]{1,0:T(8,128)(2,1)S(1)}, bf16[48,512]{1,0:T(8,128)(2,1)S(1)}, u32[]{:S(2)}, u32[]{:S(2)}) %collective-permute-start.65) | collective-permute-done | bytes 49184 | tf_op jit(solution)/shard_map/ppermute | solution.py:41
  606.9 5.3 collective-permute-done.69
  614.0 4.1 collective-permute-done.72
  (591 shorter events, 216.3 us)
Async XLA Ops:
  15.8 40.5 %collective-permute-start.4 = (bf16[2,64,4096]{2,1,0:T(8,128)(2,1)S(1)}, bf16[2,64,4096]{2,1,0:T(8,128)(2,1)}, u32[]{:S(2)}, u32[]{:S(2)}) collective-permute-start(bf16[2,64,4096]{2,1,0:T(8,128)(2,1)S(1)} %maximum_maximum_fusion), channel_id=1, source_target_pairs={{0,16},{16,0},{1,17},{17,1},{2,18},{18,2},{3,19},{19,3},{4,20},{20... | collective-permute-start | bytes 3145736 | tf_op jit(solution)/shard_map/ppermute | solution.py:41
  18.3 40.9 %collective-permute-start.3 = (bf16[2,64,4096]{2,1,0:T(8,128)(2,1)S(1)}, bf16[2,64,4096]{2,1,0:T(8,128)(2,1)}, u32[]{:S(2)}, u32[]{:S(2)}) collective-permute-start(bf16[2,64,4096]{2,1,0:T(8,128)(2,1)S(1)} %maximum_maximum_fusion), channel_id=1, source_target_pairs={{0,8},{8,0},{1,9},{9,1},{2,10},{10,2},{3,11},{11,3},{4,12},{12,4},... | collective-permute-start | bytes 3145736 | tf_op jit(solution)/shard_map/ppermute | solution.py:36
  19.8 34.4 %collective-permute-start.2 = (bf16[2,64,4096]{2,1,0:T(8,128)(2,1)S(1)}, bf16[2,64,4096]{2,1,0:T(8,128)(2,1)}, u32[]{:S(2)}, u32[]{:S(2)}) collective-permute-start(bf16[2,64,4096]{2,1,0:T(8,128)(2,1)S(1)} %maximum_maximum_fusion), channel_id=1, source_target_pairs={{0,1},{1,2},{2,3},{3,0},{4,5},{5,6},{6,7},{7,4},{8,9},{9,10},{10,1... | collective-permute-start | bytes 3145736 | tf_op jit(solution)/shard_map/ppermute | solution.py:41
  24.1 22.2 %collective-permute-start.31 = (f32[2]{0:T(128)S(1)}, f32[2]{0:T(128)S(1)}, u32[]{:S(2)}, u32[]{:S(2)}) collective-permute-start(f32[2]{0:T(128)S(1)} %add_convert_fusion.4), channel_id=1, source_target_pairs={{0,4},{4,0},{1,5},{5,1},{2,6},{6,2},{3,7},{7,3},{8,12},{12,8},{9,1... | collective-permute-start | bytes 32 | tf_op jit(solution)/shard_map/ppermute | solution.py:36
  32.6 16.4 %collective-permute-start.7 = (bf16[2,1,64,2048]{3,2,0,1:T(8,128)(2,1)}, bf16[2,1,64,2048]{3,2,0,1:T(8,128)(2,1)}, u32[]{:S(2)}, u32[]{:S(2)}) collective-permute-start(bf16[2,1,64,2048]{3,2,0,1:T(8,128)(2,1)} %dynamic-slice_bitcast_fusion.2), channel_id=1, source_target_pairs={{0,4},{4,0},{1,5},{5,1},{2,6},{6,2},{3,7},{7,3},{8,12},{12,8},{9,1... | collective-permute-start | bytes 1572872 | tf_op jit(solution)/shard_map/ppermute | solution.py:36
  49.0 7.8 %collective-permute-start.5 = (bf16[2,64,4224]{2,1,0:T(8,128)(2,1)}, bf16[2,64,4224]{2,1,0:T(8,128)(2,1)S(1)}, u32[]{:S(2)}, u32[]{:S(2)}) collective-permute-start(bf16[2,64,4224]{2,1,0:T(8,128)(2,1)} %get-tuple-element.253), channel_id=1, source_target_pairs={{0,4},{4,0},{1,5},{5,1},{2,6},{6,2},{3,7},{7,3},{8,12},{12,8},{9,1... | collective-permute-start | bytes 3244040 | tf_op jit(solution)/shard_map/ppermute | solution.py:36
  54.2 28.5 %collective-permute-start.10 = (bf16[2,64,4096]{2,1,0:T(8,128)(2,1)}, bf16[2,64,4096]{2,1,0:T(8,128)(2,1)}, u32[]{:S(2)}, u32[]{:S(2)}) collective-permute-start(bf16[2,64,4096]{2,1,0:T(8,128)(2,1)} %collective-permute-done.2), channel_id=1, source_target_pairs={{0,16},{16,0},{1,17},{17,1},{2,18},{18,2},{3,19},{19,3},{4,20},{20... | collective-permute-start | bytes 3145736 | tf_op jit(solution)/shard_map/ppermute | solution.py:41
  54.7 28.3 %collective-permute-start.8 = (bf16[2,64,4096]{2,1,0:T(8,128)(2,1)}, bf16[2,64,4096]{2,1,0:T(8,128)(2,1)}, u32[]{:S(2)}, u32[]{:S(2)}) collective-permute-start(bf16[2,64,4096]{2,1,0:T(8,128)(2,1)} %collective-permute-done.2), channel_id=1, source_target_pairs={{0,1},{1,2},{2,3},{3,0},{4,5},{5,6},{6,7},{7,4},{8,9},{9,10},{10,1... | collective-permute-start | bytes 3145736 | tf_op jit(solution)/shard_map/ppermute | solution.py:41
  56.3 26.4 %collective-permute-start.9 = (bf16[2,64,4096]{2,1,0:T(8,128)(2,1)}, bf16[2,64,4096]{2,1,0:T(8,128)(2,1)}, u32[]{:S(2)}, u32[]{:S(2)}) collective-permute-start(bf16[2,64,4096]{2,1,0:T(8,128)(2,1)} %collective-permute-done.4), channel_id=1, source_target_pairs={{0,8},{8,0},{1,9},{9,1},{2,10},{10,2},{3,11},{11,3},{4,12},{12,4},... | collective-permute-start | bytes 3145736 | tf_op jit(solution)/shard_map/ppermute | solution.py:36
  67.9 45.0 %all-to-all-start = ((bf16[4,64,2048]{2,1,0:T(8,128)(2,1)}), bf16[4,64,2048]{2,1,0:T(8,128)(2,1)S(1)}, u32[]{:S(2)}, u32[]{:S(2)}) async-start(bf16[4,64,2048]{2,1,0:T(8,128)(2,1)} %bitcast.12), calls=%async_computation | async-start | bytes 2097152 | tf_op jit(solution)/shard_map/all_to_all | solution.py:864
  71.5 32.1 %collective-permute-start.12 = (bf16[2,64,4224]{2,1,0:T(8,128)(2,1)S(1)}, bf16[2,64,4224]{2,1,0:T(8,128)(2,1)S(1)}, u32[]{:S(2)}, u32[]{:S(2)}) collective-permute-start(bf16[2,64,4224]{2,1,0:T(8,128)(2,1)S(1)} %copy-done.68), channel_id=1, source_target_pairs={{0,16},{16,0},{1,17},{17,1},{2,18},{18,2},{3,19},{19,3},{4,20},{20... | collective-permute-start | bytes 3244040 | tf_op jit(solution)/shard_map/ppermute | solution.py:41
  73.0 32.8 %collective-permute-start.11 = (bf16[2,64,4224]{2,1,0:T(8,128)(2,1)}, bf16[2,64,4224]{2,1,0:T(8,128)(2,1)}, u32[]{:S(2)}, u32[]{:S(2)}) collective-permute-start(bf16[2,64,4224]{2,1,0:T(8,128)(2,1)} %pad_maximum_fusion.3), channel_id=1, source_target_pairs={{0,8},{8,0},{1,9},{9,1},{2,10},{10,2},{3,11},{11,3},{4,12},{12,4},... | collective-permute-start | bytes 3244040 | tf_op jit(solution)/shard_map/ppermute | solution.py:36
  83.0 43.2 %collective-permute-start.15 = (bf16[2,64,4096]{2,1,0:T(8,128)(2,1)}, bf16[2,64,4096]{2,1,0:T(8,128)(2,1)}, u32[]{:S(2)}, u32[]{:S(2)}) collective-permute-start(bf16[2,64,4096]{2,1,0:T(8,128)(2,1)} %collective-permute-done.8), channel_id=1, source_target_pairs={{0,16},{16,0},{1,17},{17,1},{2,18},{18,2},{3,19},{19,3},{4,20},{20... | collective-permute-start | bytes 3145736 | tf_op jit(solution)/shard_map/ppermute | solution.py:41
  84.5 43.8 %collective-permute-start.14 = (bf16[2,64,4096]{2,1,0:T(8,128)(2,1)}, bf16[2,64,4096]{2,1,0:T(8,128)(2,1)}, u32[]{:S(2)}, u32[]{:S(2)}) collective-permute-start(bf16[2,64,4096]{2,1,0:T(8,128)(2,1)} %collective-permute-done.2), channel_id=1, source_target_pairs={{0,8},{8,0},{1,9},{9,1},{2,10},{10,2},{3,11},{11,3},{4,12},{12,4},... | collective-permute-start | bytes 3145736 | tf_op jit(solution)/shard_map/ppermute | solution.py:36
  105.9 44.9 %collective-permute-start.16 = (bf16[2,64,4096]{2,1,0:T(8,128)(2,1)}, bf16[2,64,4096]{2,1,0:T(8,128)(2,1)}, u32[]{:S(2)}, u32[]{:S(2)}) collective-permute-start(bf16[2,64,4096]{2,1,0:T(8,128)(2,1)} %collective-permute-done.10), channel_id=1, source_target_pairs={{0,8},{8,0},{1,9},{9,1},{2,10},{10,2},{3,11},{11,3},{4,12},{12,4},... | collective-permute-start | bytes 3145736 | tf_op jit(solution)/shard_map/ppermute | solution.py:36
  106.4 28.3 %collective-permute-start.13 = (bf16[2,64,4096]{2,1,0:T(8,128)(2,1)}, bf16[2,64,4096]{2,1,0:T(8,128)(2,1)}, u32[]{:S(2)}, u32[]{:S(2)}) collective-permute-start(bf16[2,64,4096]{2,1,0:T(8,128)(2,1)} %collective-permute-done.8), channel_id=1, source_target_pairs={{0,1},{1,2},{2,3},{3,0},{4,5},{5,6},{6,7},{7,4},{8,9},{9,10},{10,1... | collective-permute-start | bytes 3145736 | tf_op jit(solution)/shard_map/ppermute | solution.py:41
  108.0 44.4 %collective-permute-start.17 = (bf16[2,64,4224]{2,1,0:T(8,128)(2,1)}, bf16[2,64,4224]{2,1,0:T(8,128)(2,1)}, u32[]{:S(2)}, u32[]{:S(2)}) collective-permute-start(bf16[2,64,4224]{2,1,0:T(8,128)(2,1)} %collective-permute-done.11), channel_id=1, source_target_pairs={{0,16},{16,0},{1,17},{17,1},{2,18},{18,2},{3,19},{19,3},{4,20},{20... | collective-permute-start | bytes 3244040 | tf_op jit(solution)/shard_map/ppermute | solution.py:41
  112.9 155.9 %all-to-all-start.1 = ((bf16[4,64,2048]{2,1,0:T(8,128)(2,1)}), bf16[4,64,2048]{2,1,0:T(8,128)(2,1)}, u32[]{:S(2)}, u32[]{:S(2)}) async-start(bf16[4,64,2048]{2,1,0:T(8,128)(2,1)} %bitcast.28), calls=%async_computation.1 | async-start | bytes 2097152 | tf_op jit(solution)/shard_map/all_to_all | solution.py:864
  126.2 26.7 %collective-permute-start.6 = (bf16[256,2048]{1,0:T(8,128)(2,1)S(1)}, bf16[256,2048]{1,0:T(8,128)(2,1)S(1)}, u32[]{:S(2)}, u32[]{:S(2)}) collective-permute-start(bf16[256,2048]{1,0:T(8,128)(2,1)S(1)} %bitcast.521), channel_id=1, source_target_pairs={{0,4},{4,0},{1,5},{5,1},{2,6},{6,2},{3,7},{7,3},{8,12},{12,8},{9,1... | collective-permute-start | bytes 3145736 | tf_op jit(solution)/shard_map/ppermute | solution.py:36
  128.4 57.6 %collective-permute-start.20 = (bf16[2,64,4096]{2,1,0:T(8,128)(2,1)}, bf16[2,64,4096]{2,1,0:T(8,128)(2,1)S(1)}, u32[]{:S(2)}, u32[]{:S(2)}) collective-permute-start(bf16[2,64,4096]{2,1,0:T(8,128)(2,1)} %collective-permute-done.8), channel_id=1, source_target_pairs={{0,8},{8,0},{1,9},{9,1},{2,10},{10,2},{3,11},{11,3},{4,12},{12,4},... | collective-permute-start | bytes 3145736 | tf_op jit(solution)/shard_map/ppermute | solution.py:36
  134.6 39.9 %collective-permute-start.19 = (bf16[2,64,4224]{2,1,0:T(8,128)(2,1)}, bf16[2,64,4224]{2,1,0:T(8,128)(2,1)S(1)}, u32[]{:S(2)}, u32[]{:S(2)}) collective-permute-start(bf16[2,64,4224]{2,1,0:T(8,128)(2,1)} %pad_maximum_fusion.2), channel_id=1, source_target_pairs={{0,1},{1,2},{2,3},{3,0},{4,5},{5,6},{6,7},{7,4},{8,9},{9,10},{10,1... | collective-permute-start | bytes 3244040 | tf_op jit(solution)/shard_map/ppermute | solution.py:41
  150.8 35.1 %collective-permute-start.21 = (bf16[2,64,4096]{2,1,0:T(8,128)(2,1)}, bf16[2,64,4096]{2,1,0:T(8,128)(2,1)}, u32[]{:S(2)}, u32[]{:S(2)}) collective-permute-start(bf16[2,64,4096]{2,1,0:T(8,128)(2,1)} %collective-permute-done.13), channel_id=1, source_target_pairs={{0,16},{16,0},{1,17},{17,1},{2,18},{18,2},{3,19},{19,3},{4,20},{20... | collective-permute-start | bytes 3145736 | tf_op jit(solution)/shard_map/ppermute | solution.py:41
  152.3 53.6 %collective-permute-start.23 = (bf16[2,64,4096]{2,1,0:T(8,128)(2,1)}, bf16[2,64,4096]{2,1,0:T(8,128)(2,1)S(1)}, u32[]{:S(2)}, u32[]{:S(2)}) collective-permute-start(bf16[2,64,4096]{2,1,0:T(8,128)(2,1)} %collective-permute-done.15), channel_id=1, source_target_pairs={{0,8},{8,0},{1,9},{9,1},{2,10},{10,2},{3,11},{11,3},{4,12},{12,4},... | collective-permute-start | bytes 3145736 | tf_op jit(solution)/shard_map/ppermute | solution.py:36
  152.9 44.9 %collective-permute-start.18 = (bf16[2,64,4224]{2,1,0:T(8,128)(2,1)}, bf16[2,64,4224]{2,1,0:T(8,128)(2,1)}, u32[]{:S(2)}, u32[]{:S(2)}) collective-permute-start(bf16[2,64,4224]{2,1,0:T(8,128)(2,1)} %collective-permute-done.11), channel_id=1, source_target_pairs={{0,1},{1,2},{2,3},{3,0},{4,5},{5,6},{6,7},{7,4},{8,9},{9,10},{10,1... | collective-permute-start | bytes 3244040 | tf_op jit(solution)/shard_map/ppermute | solution.py:41
  174.6 31.3 %collective-permute-start.24 = (bf16[2,64,4224]{2,1,0:T(8,128)(2,1)S(1)}, bf16[2,64,4224]{2,1,0:T(8,128)(2,1)S(1)}, u32[]{:S(2)}, u32[]{:S(2)}) collective-permute-start(bf16[2,64,4224]{2,1,0:T(8,128)(2,1)S(1)} %collective-permute-done.19), channel_id=1, source_target_pairs={{0,16},{16,0},{1,17},{17,1},{2,18},{18,2},{3,19},{19,3},{4,20},{20... | collective-permute-start | bytes 3244040 | tf_op jit(solution)/shard_map/ppermute | solution.py:41
  185.9 35.0 %collective-permute-start.22 = (bf16[2,64,4224]{2,1,0:T(8,128)(2,1)S(1)}, bf16[2,64,4224]{2,1,0:T(8,128)(2,1)S(1)}, u32[]{:S(2)}, u32[]{:S(2)}) collective-permute-start(bf16[2,64,4224]{2,1,0:T(8,128)(2,1)S(1)} %collective-permute-done.19), channel_id=1, source_target_pairs={{0,1},{1,2},{2,3},{3,0},{4,5},{5,6},{6,7},{7,4},{8,9},{9,10},{10,1... | collective-permute-start | bytes 3244040 | tf_op jit(solution)/shard_map/ppermute | solution.py:41
  189.1 38.3 %collective-permute-start.26 = (bf16[2,64,4096]{2,1,0:T(8,128)(2,1)}, bf16[2,64,4096]{2,1,0:T(8,128)(2,1)S(1)}, u32[]{:S(2)}, u32[]{:S(2)}) collective-permute-start(bf16[2,64,4096]{2,1,0:T(8,128)(2,1)} %collective-permute-done.13), channel_id=1, source_target_pairs={{0,8},{8,0},{1,9},{9,1},{2,10},{10,2},{3,11},{11,3},{4,12},{12,4},... | collective-permute-start | bytes 3145736 | tf_op jit(solution)/shard_map/ppermute | solution.py:36
  203.3 25.1 %collective-permute-start.27 = (bf16[2,64,4224]{2,1,0:T(8,128)(2,1)}, bf16[2,64,4224]{2,1,0:T(8,128)(2,1)}, u32[]{:S(2)}, u32[]{:S(2)}) collective-permute-start(bf16[2,64,4224]{2,1,0:T(8,128)(2,1)} %collective-permute-done.18), channel_id=1, source_target_pairs={{0,16},{16,0},{1,17},{17,1},{2,18},{18,2},{3,19},{19,3},{4,20},{20... | collective-permute-start | bytes 3244040 | tf_op jit(solution)/shard_map/ppermute | solution.py:41
  205.9 64.4 %collective-permute-start.25 = (bf16[2,64,4224]{2,1,0:T(8,128)(2,1)}, bf16[2,64,4224]{2,1,0:T(8,128)(2,1)}, u32[]{:S(2)}, u32[]{:S(2)}) collective-permute-start(bf16[2,64,4224]{2,1,0:T(8,128)(2,1)} %collective-permute-done.18), channel_id=1, source_target_pairs={{0,1},{1,2},{2,3},{3,0},{4,5},{5,6},{6,7},{7,4},{8,9},{9,10},{10,1... | collective-permute-start | bytes 3244040 | tf_op jit(solution)/shard_map/ppermute | solution.py:41
  208.9 70.2 %collective-permute-start.29 = (bf16[2,64,4096]{2,1,0:T(8,128)(2,1)}, bf16[2,64,4096]{2,1,0:T(8,128)(2,1)}, u32[]{:S(2)}, u32[]{:S(2)}) collective-permute-start(bf16[2,64,4096]{2,1,0:T(8,128)(2,1)} %collective-permute-done.21), channel_id=1, source_target_pairs={{0,8},{8,0},{1,9},{9,1},{2,10},{10,2},{3,11},{11,3},{4,12},{12,4},... | collective-permute-start | bytes 3145736 | tf_op jit(solution)/shard_map/ppermute | solution.py:36
  220.9 58.2 %collective-permute-start.30 = (bf16[2,64,4224]{2,1,0:T(8,128)(2,1)S(1)}, bf16[2,64,4224]{2,1,0:T(8,128)(2,1)}, u32[]{:S(2)}, u32[]{:S(2)}) collective-permute-start(bf16[2,64,4224]{2,1,0:T(8,128)(2,1)S(1)} %collective-permute-done.22), channel_id=1, source_target_pairs={{0,16},{16,0},{1,17},{17,1},{2,18},{18,2},{3,19},{19,3},{4,20},{20... | collective-permute-start | bytes 3244040 | tf_op jit(solution)/shard_map/ppermute | solution.py:41
  228.5 50.7 %collective-permute-start.28 = (bf16[2,64,4224]{2,1,0:T(8,128)(2,1)S(1)}, bf16[2,64,4224]{2,1,0:T(8,128)(2,1)S(1)}, u32[]{:S(2)}, u32[]{:S(2)}) collective-permute-start(bf16[2,64,4224]{2,1,0:T(8,128)(2,1)S(1)} %collective-permute-done.22), channel_id=1, source_target_pairs={{0,1},{1,2},{2,3},{3,0},{4,5},{5,6},{6,7},{7,4},{8,9},{9,10},{10,1... | collective-permute-start | bytes 3244040 | tf_op jit(solution)/shard_map/ppermute | solution.py:41
  268.8 70.6 %collective-permute-start.32 = (bf16[4,64,2048]{2,1,0:T(8,128)(2,1)}, bf16[4,64,2048]{2,1,0:T(8,128)(2,1)}, u32[]{:S(2)}, u32[]{:S(2)}) collective-permute-start(bf16[4,64,2048]{2,1,0:T(8,128)(2,1)} %all-to-all-done.1), channel_id=1, source_target_pairs={{0,8},{8,0},{1,9},{9,1},{2,10},{10,2},{3,11},{11,3},{4,12},{12,4},... | collective-permute-start | bytes 3145736 | tf_op jit(solution)/shard_map/ppermute | solution.py:36
  274.1 60.6 %collective-permute-start.34 = (bf16[2,64,4224]{2,1,0:T(8,128)(2,1)}, bf16[2,64,4224]{2,1,0:T(8,128)(2,1)}, u32[]{:S(2)}, u32[]{:S(2)}) collective-permute-start(bf16[2,64,4224]{2,1,0:T(8,128)(2,1)} %collective-permute-done.25), channel_id=1, source_target_pairs={{0,16},{16,0},{1,17},{17,1},{2,18},{18,2},{3,19},{19,3},{4,20},{20... | collective-permute-start | bytes 3244040 | tf_op jit(solution)/shard_map/ppermute | solution.py:41
  279.1 55.6 %collective-permute-start.33 = (bf16[2,64,4224]{2,1,0:T(8,128)(2,1)}, bf16[2,64,4224]{2,1,0:T(8,128)(2,1)}, u32[]{:S(2)}, u32[]{:S(2)}) collective-permute-start(bf16[2,64,4224]{2,1,0:T(8,128)(2,1)} %collective-permute-done.25), channel_id=1, source_target_pairs={{0,1},{1,2},{2,3},{3,0},{4,5},{5,6},{6,7},{7,4},{8,9},{9,10},{10,1... | collective-permute-start | bytes 3244040 | tf_op jit(solution)/shard_map/ppermute | solution.py:41
  297.7 11.5 %collective-permute-start.44 = (f32[1,64]{1,0:T(1,128)S(1)}, f32[1,64]{1,0:T(1,128)S(1)}, u32[]{:S(2)}, u32[]{:S(2)}) collective-permute-start(f32[1,64]{1,0:T(1,128)S(1)} %bitcast.590), channel_id=1, source_target_pairs={{0,2},{1,3},{2,0},{3,1},{4,6},{5,7},{6,4},{7,5},{8,10},{9,11},{10,... | collective-permute-start | bytes 776 | tf_op jit(solution)/shard_map/ppermute | solution.py:41
  297.7 11.4 %collective-permute-start.43 = (f32[1,64]{1,0:T(1,128)S(1)}, f32[1,64]{1,0:T(1,128)S(1)}, u32[]{:S(2)}, u32[]{:S(2)}) collective-permute-start(f32[1,64]{1,0:T(1,128)S(1)} %bitcast.591), channel_id=1, source_target_pairs={{0,1},{1,2},{2,3},{3,0},{4,5},{5,6},{6,7},{7,4},{8,9},{9,10},{10,1... | collective-permute-start | bytes 776 | tf_op jit(solution)/shard_map/ppermute | solution.py:41
  309.2 50.6 %collective-permute-start.41 = (bf16[2,64,4224]{2,1,0:T(8,128)(2,1)}, bf16[2,64,4224]{2,1,0:T(8,128)(2,1)}, u32[]{:S(2)}, u32[]{:S(2)}) collective-permute-start(bf16[2,64,4224]{2,1,0:T(8,128)(2,1)} %copy-done.67), channel_id=1, source_target_pairs={{0,16},{16,0},{1,17},{17,1},{2,18},{18,2},{3,19},{19,3},{4,20},{20... | collective-permute-start | bytes 3244040 | tf_op jit(solution)/shard_map/ppermute | solution.py:41
  315.0 11.8 %collective-permute-start.47 = (f32[8,64]{1,0:T(8,128)S(1)}, f32[8,64]{1,0:T(8,128)S(1)}, u32[]{:S(2)}, u32[]{:S(2)}) collective-permute-start(f32[8,64]{1,0:T(8,128)S(1)} %bitcast.587), channel_id=1, source_target_pairs={{0,8},{8,0},{1,9},{9,1},{2,10},{10,2},{3,11},{11,3},{4,12},{12,4},... | collective-permute-start | bytes 6152 | tf_op jit(solution)/shard_map/ppermute | solution.py:36
  326.9 7.2 %collective-permute-start.48 = (f32[16,64]{1,0:T(8,128)S(1)}, f32[16,64]{1,0:T(8,128)S(1)}, u32[]{:S(2)}, u32[]{:S(2)}) collective-permute-start(f32[16,64]{1,0:T(8,128)S(1)} %fusion.88), channel_id=1, source_target_pairs={{0,16},{16,0},{1,17},{17,1},{2,18},{18,2},{3,19},{19,3},{4,20},{20... | collective-permute-start | bytes 12296 | tf_op jit(solution)/shard_map/ppermute | solution.py:41
  347.3 37.8 %collective-permute-start.42 = (bf16[2,64,4224]{2,1,0:T(8,128)(2,1)}, bf16[2,64,4224]{2,1,0:T(8,128)(2,1)S(1)}, u32[]{:S(2)}, u32[]{:S(2)}) collective-permute-start(bf16[2,64,4224]{2,1,0:T(8,128)(2,1)} %collective-permute-done.33), channel_id=1, source_target_pairs={{0,16},{16,0},{1,17},{17,1},{2,18},{18,2},{3,19},{19,3},{4,20},{20... | collective-permute-start | bytes 3244040 | tf_op jit(solution)/shard_map/ppermute | solution.py:41
  350.6 6.5 %collective-permute-start.35 = (bf16[256,2048]{1,0:T(8,128)(2,1)S(1)}, bf16[256,2048]{1,0:T(8,128)(2,1)S(1)}, u32[]{:S(2)}, u32[]{:S(2)}) collective-permute-start(bf16[256,2048]{1,0:T(8,128)(2,1)S(1)} %pad_maximum_fusion.6), channel_id=1, source_target_pairs={{0,4},{4,0},{1,5},{5,1},{2,6},{6,2},{3,7},{7,3},{8,12},{12,8},{9,1... | collective-permute-start | bytes 3145736 | tf_op jit(solution)/shard_map/ppermute | solution.py:36
  356.2 31.6 %collective-permute-start.40 = (bf16[256,2048]{1,0:T(8,128)(2,1)}, bf16[256,2048]{1,0:T(8,128)(2,1)S(1)}, u32[]{:S(2)}, u32[]{:S(2)}) collective-permute-start(bf16[256,2048]{1,0:T(8,128)(2,1)} %bitcast.103.g_ref), channel_id=1, source_target_pairs={{0,4},{4,0},{1,5},{5,1},{2,6},{6,2},{3,7},{7,3},{8,12},{12,8},{9,1... | collective-permute-start | bytes 3145736 | tf_op jit(solution)/shard_map/ppermute | solution.py:36
  359.4 25.7 %collective-permute-start.38 = (bf16[256,2048]{1,0:T(8,128)(2,1)}, bf16[256,2048]{1,0:T(8,128)(2,1)S(1)}, u32[]{:S(2)}, u32[]{:S(2)}) collective-permute-start(bf16[256,2048]{1,0:T(8,128)(2,1)} %multiply_convert_fusion.1.h_ref), channel_id=1, source_target_pairs={{0,8},{8,0},{1,9},{9,1},{2,10},{10,2},{3,11},{11,3},{4,12},{12,4},... | collective-permute-start | bytes 3145736 | tf_op jit(solution)/shard_map/ppermute | solution.py:36
  425.3 32.9 %collective-permute-start.51 = (bf16[256,2048]{1,0:T(8,128)(2,1)S(1)}, bf16[256,2048]{1,0:T(8,128)(2,1)}, u32[]{:S(2)}, u32[]{:S(2)}) collective-permute-start(bf16[256,2048]{1,0:T(8,128)(2,1)S(1)} %add_convert_fusion.3), channel_id=1, source_target_pairs={{0,8},{8,0},{1,9},{9,1},{2,10},{10,2},{3,11},{11,3},{4,12},{12,4},... | collective-permute-start | bytes 3145736 | tf_op jit(solution)/shard_map/ppermute | solution.py:36
  458.2 14.9 %collective-permute-start.52 = (bf16[256,2048]{1,0:T(8,128)(2,1)}, bf16[256,2048]{1,0:T(8,128)(2,1)}, u32[]{:S(2)}, u32[]{:S(2)}) collective-permute-start(bf16[256,2048]{1,0:T(8,128)(2,1)} %get-tuple-element.440), channel_id=1, source_target_pairs={{0,4},{4,0},{1,5},{5,1},{2,6},{6,2},{3,7},{7,3},{8,12},{12,8},{9,1... | collective-permute-start | bytes 3145736 | tf_op jit(solution)/shard_map/ppermute | solution.py:36
  472.6 9.0 %collective-permute-start.54 = (bf16[256,2048]{1,0:T(8,128)(2,1)}, bf16[256,2048]{1,0:T(8,128)(2,1)}, u32[]{:S(2)}, u32[]{:S(2)}) collective-permute-start(bf16[256,2048]{1,0:T(8,128)(2,1)} %get-tuple-element.446), channel_id=1, source_target_pairs={{0,4},{4,0},{1,5},{5,1},{2,6},{6,2},{3,7},{7,3},{8,12},{12,8},{9,1... | collective-permute-start | bytes 3145736 | tf_op jit(solution)/shard_map/ppermute | solution.py:36
  483.6 25.4 %collective-permute-start.55 = (bf16[256,2048]{1,0:T(8,128)(2,1)S(1)}, bf16[256,2048]{1,0:T(8,128)(2,1)S(1)}, u32[]{:S(2)}, u32[]{:S(2)}) collective-permute-start(bf16[256,2048]{1,0:T(8,128)(2,1)S(1)} %add_convert_fusion.1), channel_id=1, source_target_pairs={{0,8},{8,0},{1,9},{9,1},{2,10},{10,2},{3,11},{11,3},{4,12},{12,4},... | collective-permute-start | bytes 3145736 | tf_op jit(solution)/shard_map/ppermute | solution.py:36
  484.5 25.2 %collective-permute-start.56 = (f32[1,2048]{1,0:T(1,128)S(1)}, f32[1,2048]{1,0:T(1,128)S(1)}, u32[]{:S(2)}, u32[]{:S(2)}) collective-permute-start(f32[1,2048]{1,0:T(1,128)S(1)} %div.71.own_ref), channel_id=1, source_target_pairs={{0,4},{4,0},{1,5},{5,1},{2,6},{6,2},{3,7},{7,3},{8,12},{12,8},{9,1... | collective-permute-start | bytes 24584 | tf_op jit(solution)/shard_map/ppermute | solution.py:36
  509.1 18.9 %collective-permute-start.57 = (bf16[256,2048]{1,0:T(8,128)(2,1)S(1)}, bf16[256,2048]{1,0:T(8,128)(2,1)S(1)}, u32[]{:S(2)}, u32[]{:S(2)}) collective-permute-start(bf16[256,2048]{1,0:T(8,128)(2,1)S(1)} %copy-done.97), channel_id=1, source_target_pairs={{0,4},{4,0},{1,5},{5,1},{2,6},{6,2},{3,7},{7,3},{8,12},{12,8},{9,1... | collective-permute-start | bytes 3145736 | tf_op jit(solution)/shard_map/ppermute | solution.py:36
  525.6 27.4 %collective-permute-start.67 = (bf16[256,2048]{1,0:T(8,128)(2,1)}, bf16[256,2048]{1,0:T(8,128)(2,1)}, u32[]{:S(2)}, u32[]{:S(2)}) collective-permute-start(bf16[256,2048]{1,0:T(8,128)(2,1)} %slice.486), channel_id=1, source_target_pairs={{0,4},{4,0},{1,5},{5,1},{2,6},{6,2},{3,7},{7,3},{8,12},{12,8},{9,1... | collective-permute-start | bytes 3145736 | tf_op jit(solution)/shard_map/ppermute | solution.py:36
  533.6 11.7 %collective-permute-start.59 = (f32[1,2048]{1,0:T(1,128)}, f32[1,2048]{1,0:T(1,128)}, u32[]{:S(2)}, u32[]{:S(2)}) collective-permute-start(f32[1,2048]{1,0:T(1,128)} %add.678), channel_id=1, source_target_pairs={{0,8},{8,0},{1,9},{9,1},{2,10},{10,2},{3,11},{11,3},{4,12},{12,4},... | collective-permute-start | bytes 24584 | tf_op jit(solution)/shard_map/ppermute | solution.py:36
  540.9 30.7 %all-to-all-start.2 = ((bf16[4,64,2048]{2,1,0:T(8,128)(2,1)}), bf16[4,64,2048]{2,1,0:T(8,128)(2,1)}, u32[]{:S(2)}, u32[]{:S(2)}) async-start(bf16[4,64,2048]{2,1,0:T(8,128)(2,1)} %bitcast.524), calls=%async_computation.2 | async-start | bytes 2097152 | tf_op jit(solution)/shard_map/all_to_all | solution.py:1040
  555.9 19.2 %collective-permute-start.61 = (bf16[200,512]{1,0:T(8,128)(2,1)S(1)}, bf16[200,512]{1,0:T(8,128)(2,1)S(1)}, u32[]{:S(2)}, u32[]{:S(2)}) collective-permute-start(bf16[200,512]{1,0:T(8,128)(2,1)S(1)} %fusion.64), channel_id=1, source_target_pairs={{0,8},{8,0},{1,9},{9,1},{2,10},{10,2},{3,11},{11,3},{4,12},{12,4},... | collective-permute-start | bytes 614408 | tf_op jit(solution)/shard_map/ppermute | solution.py:36
  571.6 33.1 %all-to-all-start.3 = ((bf16[4,64,2048]{2,1,0:T(8,128)(2,1)}), bf16[4,64,2048]{2,1,0:T(8,128)(2,1)S(1)}, u32[]{:S(2)}, u32[]{:S(2)}) async-start(bf16[4,64,2048]{2,1,0:T(8,128)(2,1)} %bitcast.192), calls=%async_computation.3 | async-start | bytes 2097152 | tf_op jit(solution)/shard_map/all_to_all | solution.py:1040
  575.3 6.1 collective-permute-start.63
  581.5 16.5 %collective-permute-start.64 = (bf16[48,512]{1,0:T(8,128)(2,1)S(1)}, bf16[48,512]{1,0:T(8,128)(2,1)S(1)}, u32[]{:S(2)}, u32[]{:S(2)}) collective-permute-start(bf16[48,512]{1,0:T(8,128)(2,1)S(1)} %get-tuple-element.530), channel_id=1, source_target_pairs={{0,1},{1,2},{2,3},{3,0},{4,5},{5,6},{6,7},{7,4},{8,9},{9,10},{10,1... | collective-permute-start | bytes 147464 | tf_op jit(solution)/shard_map/ppermute | solution.py:41
  583.2 14.7 %collective-permute-start.66 = (bf16[48,512]{1,0:T(8,128)(2,1)S(1)}, bf16[48,512]{1,0:T(8,128)(2,1)S(1)}, u32[]{:S(2)}, u32[]{:S(2)}) collective-permute-start(bf16[48,512]{1,0:T(8,128)(2,1)S(1)} %get-tuple-element.531), channel_id=1, source_target_pairs={{0,3},{1,0},{2,1},{3,2},{4,7},{5,4},{6,5},{7,6},{8,11},{9,8},{10,9... | collective-permute-start | bytes 147464 | tf_op jit(solution)/shard_map/ppermute | solution.py:41
  585.4 19.3 %collective-permute-start.65 = (bf16[48,512]{1,0:T(8,128)(2,1)S(1)}, bf16[48,512]{1,0:T(8,128)(2,1)S(1)}, u32[]{:S(2)}, u32[]{:S(2)}) collective-permute-start(bf16[48,512]{1,0:T(8,128)(2,1)S(1)} %get-tuple-element.532), channel_id=1, source_target_pairs={{0,2},{1,3},{2,0},{3,1},{4,6},{5,7},{6,4},{7,5},{8,10},{9,11},{10,... | collective-permute-start | bytes 147464 | tf_op jit(solution)/shard_map/ppermute | solution.py:41
  587.3 33.0 %collective-permute-start.62 = (bf16[2,1,64,2048]{3,2,0,1:T(8,128)(2,1)S(1)}, bf16[2,1,64,2048]{3,2,0,1:T(8,128)(2,1)S(1)}, u32[]{:S(2)}, u32[]{:S(2)}) collective-permute-start(bf16[2,1,64,2048]{3,2,0,1:T(8,128)(2,1)S(1)} %dynamic-slice_bitcast_fusion.1), channel_id=1, source_target_pairs={{0,4},{4,0},{1,5},{5,1},{2,6},{6,2},{3,7},{7,3},{8,12},{12,8},{9,1... | collective-permute-start | bytes 1572872 | tf_op jit(solution)/shard_map/ppermute | solution.py:36
  604.7 7.6 %collective-permute-start.71 = (bf16[48,512]{1,0:T(8,128)(2,1)S(1)}, bf16[48,512]{1,0:T(8,128)(2,1)S(1)}, u32[]{:S(2)}, u32[]{:S(2)}) collective-permute-start(bf16[48,512]{1,0:T(8,128)(2,1)S(1)} %fusion.68), channel_id=1, source_target_pairs={{0,3},{1,0},{2,1},{3,2},{4,7},{5,4},{6,5},{7,6},{8,11},{9,8},{10,9... | collective-permute-start | bytes 147464 | tf_op jit(solution)/shard_map/ppermute | solution.py:41
  613.8 12.7 %collective-permute-start.68 = (bf16[2,1,64,2048]{3,2,0,1:T(8,128)(2,1)S(1)}, bf16[2,1,64,2048]{3,2,0,1:T(8,128)(2,1)S(1)}, u32[]{:S(2)}, u32[]{:S(2)}) collective-permute-start(bf16[2,1,64,2048]{3,2,0,1:T(8,128)(2,1)S(1)} %dynamic-slice_bitcast_fusion), channel_id=1, source_target_pairs={{0,4},{4,0},{1,5},{5,1},{2,6},{6,2},{3,7},{7,3},{8,12},{12,8},{9,1... | collective-permute-start | bytes 1572872 | tf_op jit(solution)/shard_map/ppermute | solution.py:36
  619.5 6.3 collective-permute-start.73
  623.7 10.4 %collective-permute-start.77 = (bf16[2,168,512]{2,1,0:T(8,128)(2,1)S(1)}, bf16[2,168,512]{2,1,0:T(8,128)(2,1)S(1)}, u32[]{:S(2)}, u32[]{:S(2)}) collective-permute-start(bf16[2,168,512]{2,1,0:T(8,128)(2,1)S(1)} %pad_maximum_fusion.18), channel_id=1, source_target_pairs={{0,4},{4,0},{1,5},{5,1},{2,6},{6,2},{3,7},{7,3},{8,12},{12,8},{9,1... | collective-permute-start | bytes 1032200 | tf_op jit(solution)/shard_map/ppermute | solution.py:36
  (123 other events, 1213.4 us)

commit v3 on v2

--- a/solution.py
+++ b/solution.py
@@ -71,7 +71,7 @@
 
 class Box:
     def __init__(self, array):
-        self.array = array
+        self.array = self.raw = array
 
 
 class Links:
@@ -81,12 +81,15 @@
         self.buffers = buffers
         self.rounds = []
         self.placed = 0
+        self.derived = []
 
     def run(self, queues):
         boxes = self.boxes
         while any(queues):
+            for name, sources, join_of in [e for e in self.derived if all(n in boxes for n in e[1])]:
+                boxes[name] = Box(join_of(*[boxes[n].array for n in sources]))
+            self.derived = [e for e in self.derived if e[0] not in boxes]
             ready = set(boxes)
-            self.place(len(self.rounds) - self.depth)
             self.rounds.append([])
             for queue in queues:
                 for place, (source, result, move) in enumerate(queue):
@@ -94,18 +97,21 @@
                         queue.pop(place)
                         self.send(boxes, source, result, move)
                         break
+            self.place(len(self.rounds) - self.depth)
 
     def place(self, until):
         while self.placed < until:
             for name, box in self.rounds[self.placed]:
                 for buffer in self.buffers.values():
-                    buffer.put(name, box.array)
+                    buffer.put(name, box.raw)
             self.placed += 1
 
     def send(self, boxes, source, result, move):
         box = boxes[source]
         if len(self.rounds) > self.depth:
             old = [b for name, b in self.rounds[-1 - self.depth] if b is not box and "_" not in name]
+            if len(self.rounds) > 4:
+                old += [b for name, b in self.rounds[-5] if b is not box and "_" in name]
             held = [b for b in self.buffers.values() if b.pending()]
             both = lax.optimization_barrier((box.array, [b.array for b in old], [b.array for b in held]))
             box.array = both[0]
@@ -248,6 +254,44 @@
         ),
         name=name,
     )(q, kv, kv, *extra, bias)
+
+
+def middle_back_kernel(
+    near_ref, pair_ref, far_ref, g_ref, middle_ref, t_ref, s_ref, n_ref, grad_ref, dt_ref, dm_ref
+):
+    second = near_ref[...].astype(F32) + pair_ref[...].astype(F32) + far_ref[...].astype(F32)
+    grad = g_ref[...].astype(F32) + rms_back(middle_ref[...], second)
+    grad_ref[...] = grad
+    dt_ref[...] = (grad * s_ref[...]).astype(BF)
+    part = jnp.sum(grad * t_ref[...], axis=0, keepdims=True) / n_ref[...]
+
+    @pl.when(pl.program_id(0) == 0)
+    def _():
+        dm_ref[...] = part
+
+    @pl.when(pl.program_id(0) > 0)
+    def _():
+        dm_ref[...] += part
+
+
+def middle_back(near, pair_part, far, g, middle, t, factor, norm):
+    rows, width = middle.shape
+    block = rows // 4
+    row = pl.BlockSpec((block, width), lambda i: (i, 0))
+    one = pl.BlockSpec((1, width), lambda i: (0, 0))
+    return pl.pallas_call(
+        middle_back_kernel,
+        grid=(rows // block,),
+        in_specs=[row] * 6 + [one] * 2,
+        out_specs=[row, row, one],
+        out_shape=[
+            jax.ShapeDtypeStruct((rows, width), F32),
+            jax.ShapeDtypeStruct((rows, width), BF),
+            jax.ShapeDtypeStruct((1, width), F32),
+        ],
+        cost_estimate=pl.CostEstimate(flops=20 * rows * width, bytes_accessed=24 * rows * width, transcendentals=rows),
+        name="middle_back",
+    )(near, pair_part, far, g, middle, t, factor, norm)
 
 
 def attend_back_turn_kernel(
@@ -721,10 +765,10 @@
     half = halve(pad_rows(shared, 16), "core", c)
     quarter = halve(pad_rows(jnp.concatenate([half, by_core], axis=0), 16), "xx", x)
     last = pad_rows(jnp.concatenate([quarter, by_quad], axis=0), 8 * unit)
+    last = spread(spread(last, "yy"), "seq").astype(BF)
     last, first_beside = lax.optimization_barrier((last, first_beside))
-    last = spread(spread(last, "yy"), "seq").astype(BF)
-    last, beside = lax.optimization_barrier((last, beside))
-    last = collect(collect(last, "seq"), "yy")
+    last, beside = lax.optimization_barrier((collect(last, "seq"), beside))
+    last = collect(last, "yy")
     joined = join(last[: quarter.shape[0]], "xx", x)
     everywhere = join(joined[: half.shape[0]], "core", c)
     mine = joined[half.shape[0] : half.shape[0] + by_core.shape[0]]
@@ -876,9 +920,33 @@
     feed_z = [(f"{side}{source}", f"{side}{step}", move) for source, step, move in order for side in sides]
     z_queue = attention_z[:2] + [("tokens", "tokens_moved", exchange), ("cotangent", "cotangent_moved", exchange)]
     z_queue += attention_z[2:] + feed_z
+    boxes["s0"] = Box((square_other + square_mine).sum(axis=0))
+    small_queue = [(f"s{step - 1}", f"s{step}", ring) for step in range(1, count)]
+
+    def by_seq(*pieces):
+        buffer = jnp.zeros((count, unit), F32)
+        for step, one in enumerate(pieces):
+            buffer = lax.dynamic_update_slice_in_dim(buffer, one, (z - step) % count, 0)
+        return buffer
+
+    def in_order(index):
+        return lambda mine, other: pair(mine, other, index).reshape(2 * mine.shape[0], unit)
+
+    def by_yy(*pieces):
+        buffer = jnp.zeros((ny,) + pieces[0].shape, F32)
+        for step, one in enumerate(pieces):
+            buffer = put(buffer, one, (y - step) % ny, 0)
+        return buffer
+
+    links.derived.append(("sz", [f"s{step}" for step in range(count)], by_seq))
+    small_queue.append(("sz", "szc", lambda a: swap(a, "core")))
+    links.derived.append(("sc", ["sz", "szc"], in_order(c)))
+    small_queue.append(("sc", "scx", cross_x))
+    links.derived.append(("sx", ["sc", "scx"], in_order(x)))
+    small_queue += moves_y("s", "x")
+    links.derived.append(("square", ["sx"] + [f"sxy{turn}" for turn in turns], by_yy))
     x_queue = [("a0", "a0x", cross_x)]
     y_queue = []
-    late_x = [("cotangent_moved", "cotangent_far", cross_x)]
     steps = [0] + [step for _, step, _ in order]
     feed_moves = [move for step in steps for side in sides for move in moves_y(side, step)]
     for place_of, step in enumerate(steps):
@@ -892,8 +960,7 @@
             del feed_moves[:1]
     y_queue += feed_moves
 
-    x_queue += late_x
-    links.run([z_queue, x_queue, y_queue])
+    links.run([z_queue, x_queue, y_queue, small_queue])
     links.place(len(links.rounds) - 2)
     while qkv_places:
         links.place(links.placed + 1)
@@ -901,9 +968,6 @@
     out_weight = buffers["out"].array.reshape(2, inside, inside)
     tokens_own = boxes["tokens_moved"].array.reshape(half, width)
     tokens_both = jnp.concatenate([tokens_own, swap(tokens_own, "core")], axis=0)
-    cotangent_own = boxes["cotangent_moved"].array.reshape(half, width)
-    cotangent_far = boxes["cotangent_far"].array.reshape(half, width)
-
     def positions_of(sub_place, core_place):
         source = jnp.arange(count, dtype=jnp.int32)[:, None] * local
         inner = sub_place * 2 * piece + core_place * piece + jnp.arange(piece, dtype=jnp.int32)[None]
@@ -951,13 +1015,11 @@
         return jnp.concatenate([own, swap(own, "core")], axis=0)
 
     out_rows = by_core(attention_down[3].T)[0].astype(BF)
-    contract_square = (square_other + square_mine).sum(axis=0)
-    qkv_p, contract_square = lax.optimization_barrier((qkv_p, contract_square))
-    contract_square = join(join(collect(contract_square, "seq"), "core", c), "xx", x)
-    contract_square = collect(contract_square, "yy").reshape(1, width)
-    mixed, cotangent_far, out_weight, feed_buffer.array = lax.optimization_barrier(
-        (mixed, cotangent_far, out_weight, feed_buffer.array)
-    )
+    contract_square = boxes["square"].array.reshape(1, width)
+    qkv_p, cotangent_own = lax.optimization_barrier((qkv_p, boxes["cotangent_moved"].array))
+    cotangent_own = cotangent_own.reshape(half, width)
+    cotangent_far = swap(cotangent_own, "xx")
+    mixed, cotangent_far, out_weight = lax.optimization_barrier((mixed, cotangent_far, out_weight))
     links.place(len(links.rounds))
     feed_weight = feed_buffer.array.reshape(width, 3 * quarter)
     out_square = jnp.sum(out_weight.astype(F32) ** 2, axis=1).reshape(1, width)
@@ -976,7 +1038,8 @@
     cross = jnp.stack(
         [cross[i * rank : (i + 1) * rank, i * width // 2 : (i + 1) * width // 2] for i in range(3)]
     )
-    second_far, cross, low = lax.optimization_barrier((second_far, cross, low))
+    core_up = by_core(attention_up[:3])[0]
+    second_far, cross, low, core_up = lax.optimization_barrier((second_far, cross, low, core_up))
 
     gate_up = jnp.stack([by_quarter(expand_up[i]) for i in range(2)])
     feed_downs = expand_down.transpose(0, 2, 1).reshape(2 * rank, width).astype(BF)
@@ -1004,11 +1067,11 @@
         feed_downs, gate_up, contract_rows, contract_ups,
     )[:7]
     back_near, back_sent, back_far = lax.optimization_barrier((back_near, back_sent, swap(back_far, "xx")))
-    second_grad = total(back_near, back_sent) + back_far.astype(F32)
-    middle_grad = grad_own + rms_back(middle, second_grad)
-
-    out_dm = jnp.sum(middle_grad * out_t, axis=0, keepdims=True) / out_norm
-    out_dt = core_join((middle_grad * out_scale).astype(BF))
+    middle_grad, out_dt_own, out_dm = middle_back(
+        back_near, swap(back_sent, "core"), back_far, cotangent_own, middle, out_t, out_scale, out_norm
+    )
+
+    out_dt = core_join(out_dt_own)
     mixed_grad = sum(nt(out_dt[:, i * inside : (i + 1) * inside], out_weight[i]) for i in range(2)).astype(BF)
     out_far, back_far = lax.optimization_barrier((total(out_far, out_sent).astype(BF), back_far))
     out_far = swap(out_far, "xx")
@@ -1035,7 +1098,6 @@
         qkv_dt, qkv_dm = attend_back_turn(
             heads, qkv_p, mixed_grad, bias, qkv_t, members(qkv_scale), members(1.0 / qkv_norm), cosine, sine
         )
-    core_up = by_core(attention_up[:3])[0]
     def restore_start(own):
         return lax.all_to_all(own.reshape(count, piece, width), "seq", 0, 0, tiled=True)
 
@@ -1075,8 +1137,9 @@
     shared = jnp.concatenate([flat(qkv_shared), flat(out_words), flat(feed_words)])
     cores = jnp.concatenate([flat(qkv_core), flat(dm_words), flat(out_core_words)])
     attention_shared, attention_cores, feed_quads, layer_moved, tokens_moved = reduce_all(
-        shared, cores, flat(feed_quad_words), layer_moved, restore_start(tokens_grad_own.astype(BF))
-    )
+        shared, cores, flat(feed_quad_words), layer_moved, tokens_grad_own.astype(BF)
+    )
+    tokens_moved = restore_start(tokens_moved)
     used = flat(qkv_shared).shape[0] + flat(out_words).shape[0]
     feed_shared = attention_shared[used:]
 

time: 647 us -> 608 us (0.940)
  local copies, waits for them, and re-layouts: 141 us -> 111 us
  starting transfers between devices: 85.2 us -> 76.5 us
    ppermute x45, waiting for transfers between devices: 50.6 us -> 117 us  [swap(): return lax.ppermute(a, name, [(0, 1), (1, 0)])]
    ppermute x33, waiting for transfers between devices: 98.9 us -> 47.8 us  [shift(): return lax.ppermute(a, name, [(i, (i + step) % size) for i in range(size)])]
    dynamic_update_slice x47, local copies, waits for them, and re-layouts: 83.2 us -> 70.4 us  [put(): lax.dynamic_update_slice(self.array, part, [jnp.int32(v) for v in start])]
    all_to_all x2, waiting for transfers between devices: 37.3 us -> 25.4 us  [body(): exchange = lambda a: lax.all_to_all(a, 'seq', 0, 0, tiled=True)]
    ppermute x33, starting transfers between devices: 47 us -> 35.6 us  [shift(): return lax.ppermute(a, name, [(i, (i + step) % size) for i in range(size)])]
    pallas_call x0 -> x1, Pallas kernels: none -> 6.61 us  [middle_back(): pl.pallas_call(middle_back_kernel, grid=(rows // block,), in_specs=[row]...]
    unnamed x220 -> x135, local copies, waits for them, and re-layouts: 20 us -> 13.6 us
  transfers between devices with their start and end apart: 82 -> 82, of which waited for: 29 -> 35; matrix products, arithmetic and copies ran while one was open for 30% -> 26% of each run, Pallas kernels for 15% -> 17%
where the time goes in v3:
time: 608 us; the launch traced here: 598 us
  waiting for transfers between devices  197 us (32%)
  Pallas kernels  135 us (22%)
  local copies, waits for them, and re-layouts  111 us (18%)
  starting transfers between devices  76.5 us (13%)
  other arithmetic  55.2 us (9%)
  matrix products  18.7 us (3%)
    ppermute x45, waiting for transfers between devices, swap(): return lax.ppermute(a, name, [(0, 1), (1, 0)])  117 us
    dynamic_update_slice x47, local copies, waits for them, and re-layouts, put(): lax.dynamic_update_slice(self.array, part, [jnp.int32(v) for v in start])  70.4 us
    pallas_call x2, Pallas kernels, feed_forward_back(): pl.pallas_call(functools.partial(feed_kernel, known), in_specs=[vmem] * 4...  61.5 us
    ppermute x33, waiting for transfers between devices, shift(): return lax.ppermute(a, name, [(i, (i + step) % size) for i in range(size)])  47.8 us
    ppermute x33, starting transfers between devices, shift(): return lax.ppermute(a, name, [(i, (i + step) % size) for i in range(size)])  35.6 us
    ppermute x45, starting transfers between devices, swap(): return lax.ppermute(a, name, [(0, 1), (1, 0)])  25.7 us
    all_to_all x2, waiting for transfers between devices, body(): exchange = lambda a: lax.all_to_all(a, 'seq', 0, 0, tiled=True)  25.4 us
    dot_general x7, matrix products, mm(): return lax.dot_general(a, b, (dims, ((), ())), preferred_element_type=F32)  16.6 us
  transfers between devices with their start and end apart: 82, of which 35 were waited for; matrix products, arithmetic and copies ran while one was open for 26% of the time, Pallas kernels for 17%

profile of v3, /device:TPU:0, one launch (start us, length us, event | category | flops | bytes accessed | tf_op | source)
XLA Modules:
  0.0 597.6 jit_solution(15508825479664145090)
XLA Ops:
  0.7 2.1 fusion.3
  3.4 4.9 dynamic-slice_reduce_fusion.1
  12.7 2.6 collective-permute-start.3
  24.3 3.9 feed_prepare.2
  28.3 4.0 feed_prepare.3
  59.7 16.6 %collective-permute-done.4 = bf16[2,64,4096]{2,1,0:T(8,128)(2,1)S(1)} collective-permute-done((bf16[2,64,4096]{2,1,0:T(8,128)(2,1)S(1)}, bf16[2,64,4096]{2,1,0:T(8,128)(2,1)S(1)}, u32[]{:S(2)}, u32[]{:S(2)}) %collective-permute-start.4) | collective-permute-done | bytes 1048608 | tf_op jit(solution)/shard_map/ppermute | solution.py:36
  79.7 3.5 all-to-all-start
  83.3 2.2 fusion.55
  88.9 2.1 fusion.53
  94.3 4.6 collective-permute-done.10
  104.2 2.1 fusion.52
  106.3 2.1 fusion.51
  108.3 2.1 fusion.50
  112.1 9.9 %collective-permute-done.16 = bf16[2,64,4224]{2,1,0:T(8,128)(2,1)} collective-permute-done((bf16[2,64,4224]{2,1,0:T(8,128)(2,1)}, bf16[2,64,4224]{2,1,0:T(8,128)(2,1)}, u32[]{:S(2)}, u32[]{:S(2)}) %collective-permute-start.16) | collective-permute-done | bytes 1081376 | tf_op jit(solution)/shard_map/ppermute | solution.py:36
  125.6 2.3 bitcast_dynamic-update-slice_fusion.13
  129.0 14.8 %collective-permute-done.19 = f32[8,64]{1,0:T(8,128)S(1)} collective-permute-done((f32[8,64]{1,0:T(8,128)S(1)}, f32[8,64]{1,0:T(8,128)S(1)}, u32[]{:S(2)}, u32[]{:S(2)}) %collective-permute-start.19) | collective-permute-done | bytes 2080 | tf_op jit(solution)/shard_map/ppermute | solution.py:36
  154.3 3.5 all-to-all-start.1
  157.8 12.4 %collective-permute-done.21 = bf16[2,64,4096]{2,1,0:T(8,128)(2,1)} collective-permute-done((bf16[2,64,4096]{2,1,0:T(8,128)(2,1)}, bf16[2,64,4096]{2,1,0:T(8,128)(2,1)}, u32[]{:S(2)}, u32[]{:S(2)}) %collective-permute-start.21) | collective-permute-done | bytes 1048608 | tf_op jit(solution)/shard_map/ppermute | solution.py:36
  174.9 2.1 fusion.47
  177.0 2.1 fusion.46
  182.4 2.3 bitcast_dynamic-update-slice_fusion.11
  184.7 8.0 %collective-permute-done.25 = bf16[2,64,4096]{2,1,0:T(8,128)(2,1)} collective-permute-done((bf16[2,64,4096]{2,1,0:T(8,128)(2,1)}, bf16[2,64,4096]{2,1,0:T(8,128)(2,1)}, u32[]{:S(2)}, u32[]{:S(2)}) %collective-permute-start.25) | collective-permute-done | bytes 1048608 | tf_op jit(solution)/shard_map/ppermute | solution.py:36
  192.7 25.4 %all-to-all-done.1 = bf16[4,64,2048]{2,1,0:T(8,128)(2,1)S(1)} async-done(((bf16[4,64,2048]{2,1,0:T(8,128)(2,1)}), bf16[4,64,2048]{2,1,0:T(8,128)(2,1)S(1)}, u32[]{:S(2)}, u32[]{:S(2)}) %all-to-all-start.1) | async-done | bytes 1048608 | tf_op jit(solution)/shard_map/all_to_all | solution.py:908
  218.6 2.1 fusion.45
  224.1 2.1 fusion.44
  227.5 2.1 fusion.43
  231.2 2.3 bitcast_dynamic-update-slice_fusion.10
  238.9 5.4 collective-permute-done.29
  247.2 2.4 bitcast_dynamic-update-slice_fusion.9
  249.6 2.4 bitcast_dynamic-update-slice_fusion.8
  253.4 12.5 %collective-permute-done.31 = bf16[2,64,4096]{2,1,0:T(8,128)(2,1)S(1)} collective-permute-done((bf16[2,64,4096]{2,1,0:T(8,128)(2,1)}, bf16[2,64,4096]{2,1,0:T(8,128)(2,1)S(1)}, u32[]{:S(2)}, u32[]{:S(2)}) %collective-permute-start.31) | collective-permute-done | bytes 1048608 | tf_op jit(solution)/shard_map/ppermute | solution.py:36
  266.9 4.6 copy-done.4
  271.5 13.4 %qkv_forward.1 = (bf16[512,3072]{1,0:T(8,128)(2,1)S(1)}, bf16[512,3072]{1,0:T(8,128)(2,1)S(1)}, f32[1,3072]{1,0:T(1,128)S(1)}, f32[48,3072]{1,0:T(8,128)S(1)}) custom-call(bf16[512,2048]{1,0:T(8,128)(2,1)S(1)} %fusion.1.h_ref, bf16[2048,3072]{1,0:T(8,128)(2,1)S(1)} %bitcast.557, bf16[48,2048]{1,0:T(8,128)(2,1)S(1)} %bitcast.559, f32[1,3072]{1,0:T(1,128)S(1)} %bitcast.571, ...), custom_call_target="tpu_custom_call" | custom-call | flops 6442450944 | bytes 22020096 | tf_op jit(solution)/shard_map/qkv_forward/pallas_call | solution.py:180
  287.0 8.7 %attend.1.u_ref = bf16[512,1024]{1,0:T(8,128)(2,1)S(1)} custom-call(bf16[512,3072]{1,0:T(8,128)(2,1)S(1)} %get-tuple-element.367.q_ref.k_ref.v_ref, bf16[512,3072]{1,0:T(8,128)(2,1)S(1)} %get-tuple-element.367.q_ref.k_ref.v_ref, bf16[512,3072]{1,0:T(8,128)(2,1)S(1)} %get-tuple-element.367.q_ref.k_ref.v_ref, f32[512,512]{1,0:T(8,128)S(1)} %and_select_fusion.bias_ref), custom_call_target="tpu_custom_call" | custom-call | flops 1073741824 | bytes 4194304 | tf_op jit(solution)/shard_map/attend/pallas_call | solution.py:244
  304.3 6.6 %collective-permute-done.33.g_ref = bf16[256,2048]{1,0:T(8,128)(2,1)} collective-permute-done((bf16[256,2048]{1,0:T(8,128)(2,1)S(1)}, bf16[256,2048]{1,0:T(8,128)(2,1)}, u32[]{:S(2)}, u32[]{:S(2)}) %collective-permute-start.33) | collective-permute-done | bytes 1048608 | tf_op jit(solution)/shard_map/ppermute | solution.py:36
  310.9 2.3 fusion.18
  313.2 2.3 fusion.28
  315.5 3.3 multiply_reduce_fusion
  318.8 2.3 fusion.31
  321.2 2.3 fusion.12
  336.1 11.2 %collective-permute-done.47 = bf16[2,64,4224]{2,1,0:T(8,128)(2,1)S(1)} collective-permute-done((bf16[2,64,4224]{2,1,0:T(8,128)(2,1)S(1)}, bf16[2,64,4224]{2,1,0:T(8,128)(2,1)S(1)}, u32[]{:S(2)}, u32[]{:S(2)}) %collective-permute-start.47) | collective-permute-done | bytes 1081376 | tf_op jit(solution)/shard_map/ppermute | solution.py:41
  348.4 9.8 %collective-permute-done.37.h_ref = bf16[256,2048]{1,0:T(8,128)(2,1)S(1)} collective-permute-done((bf16[256,2048]{1,0:T(8,128)(2,1)}, bf16[256,2048]{1,0:T(8,128)(2,1)S(1)}, u32[]{:S(2)}, u32[]{:S(2)}) %collective-permute-start.37) | collective-permute-done | bytes 1048608 | tf_op jit(solution)/shard_map/ppermute | solution.py:36
  358.2 10.2 %collective-permute-done.48 = bf16[2,64,4224]{2,1,0:T(8,128)(2,1)S(1)} collective-permute-done((bf16[2,64,4224]{2,1,0:T(8,128)(2,1)S(1)}, bf16[2,64,4224]{2,1,0:T(8,128)(2,1)S(1)}, u32[]{:S(2)}, u32[]{:S(2)}) %collective-permute-start.48) | collective-permute-done | bytes 1081376 | tf_op jit(solution)/shard_map/ppermute | solution.py:41
  370.5 31.0 %feed_forward_back.2 = (bf16[256,2048]{1,0:T(8,128)(2,1)}, bf16[256,2048]{1,0:T(8,128)(2,1)}, bf16[256,2048]{1,0:T(8,128)(2,1)}, bf16[256,2048]{1,0:T(8,128)(2,1...) custom-call(bf16[256,2048]{1,0:T(8,128)(2,1)} %copy-done.56, ...), custom_call_target="tpu_custom_call" | custom-call | flops 17716740096 | bytes 25690112 | tf_op jit(solution)/shard_map/feed_forward_back/pallas_call | solution.py:608
  402.1 2.3 collective-permute-done.49
  409.9 30.5 %feed_forward_back.3 = (bf16[256,2048]{1,0:T(8,128)(2,1)}, bf16[256,2048]{1,0:T(8,128)(2,1)}, bf16[256,2048]{1,0:T(8,128)(2,1)}, bf16[256,2048]{1,0:T(8,128)(2,1...) custom-call(bf16[256,2048]{1,0:T(8,128)(2,1)} %multiply_convert_fusi, ...), custom_call_target="tpu_custom_call" | custom-call | flops 17716740096 | bytes 25690112 | tf_op jit(solution)/shard_map/feed_forward_back/pallas_call | solution.py:608
  443.5 6.6 %middle_back.1 = (f32[256,2048]{1,0:T(8,128)}, bf16[256,2048]{1,0:T(8,128)(2,1)}, f32[1,2048]{1,0:T(1,128)}) custom-call(bf16[256,2048]{1,0:T(8,128)(2,1)} %get-tuple-element.402.near_ref, bf16[256,2048]{1,0:T(8,128)(2,1)} %collective-permute-done.52.pair_ref, bf16[256,2048]{1,0:T(8,128)(2,1)} %collective-permute-done.51.far_ref, ...), custom_call_target="tpu_custom_call" | custom-call | flops 10485760 | bytes 12582912 | tf_op jit(solution)/shard_map/middle_back/pallas_call | solution.py:282
  453.7 3.6 fusion.8
  457.3 2.9 add_convert_fusion.2.g_ref
  460.3 14.3 %attend_back_turn.1 = (bf16[3,512,1024]{2,1,0:T(8,128)(2,1)S(1)}, f32[3,1,1024]{2,1,0:T(1,128)S(1)}) custom-call(bf16[512,3072]{1,0:T(8,128)(2,1)} %copy-done.2, bf16[512,3072]{1,0:T(8,128)(2,1)} %copy-done.2, bf16[512,3072]{1,0:T(8,128)(2,1)} %copy-done.2, bf16[512,1024]{1,0:T(8,128)(2,1)S(1)} %add_convert_fusion.2.g_ref, ...), custom_call_target="tpu_custom_call" | custom-call | flops 2684354560 | bytes 10485760 | tf_op jit(solution)/shard_map/attend_back_turn/pallas_call | solution.py:318
  482.1 4.7 add_convert_fusion
  487.3 14.1 %qkv_back.1 = (bf16[512,2048]{1,0:T(8,128)(2,1)S(1)}, f32[4,48,512]{2,1,0:T(8,128)S(1)}, f32[2,48,512]{2,1,0:T(8,128)S(1)}) custom-call(bf16[3,512,1024]{2,1,0:T(8,128)(2,1)} %copy-done.29, bf16[2048,3072]{1,0:T(8,128)(2,1)} %bitcast.556, bf16[512,2048]{1,0:T(8,128)(2,1)S(1)} %fusion.1.h_ref, bf16[3,16,512]{2,1,0:T(8,128)(2,1)S(1)} %bitcast.573, ...), custom_call_target="tpu_custom_call" | custom-call | flops 6442450944 | bytes 12582912 | tf_op jit(solution)/shard_map/qkv_back/pallas_call | solution.py:392
  505.1 5.3 out_adapter.1
  510.5 3.6 feed_adapter.1
  515.2 4.4 all-to-all-start.2
  522.6 5.2 collective-permute-done.61
  528.9 4.8 collective-permute-done.62
  535.6 2.4 collective-permute-start.64
  543.0 6.2 %collective-permute-done.64 = bf16[48,512]{1,0:T(8,128)(2,1)S(1)} collective-permute-done((bf16[48,512]{1,0:T(8,128)(2,1)S(1)}, bf16[48,512]{1,0:T(8,128)(2,1)S(1)}, u32[]{:S(2)}, u32[]{:S(2)}) %collective-permute-start.64) | collective-permute-done | bytes 49184 | tf_op jit(solution)/shard_map/ppermute | solution.py:41
  553.2 2.1 collective-permute-done.67
  557.5 4.7 collective-permute-done.72
  563.5 3.8 all-to-all-start.3
  570.1 4.5 collective-permute-done.73
  587.0 6.7 %all-to-all-done.3 = bf16[4,64,2048]{2,1,0:T(8,128)(2,1)S(1)} async-done(((bf16[4,64,2048]{2,1,0:T(8,128)(2,1)}), bf16[4,64,2048]{2,1,0:T(8,128)(2,1)S(1)}, u32[]{:S(2)}, u32[]{:S(2)}) %all-to-all-start.3) | async-done | bytes 1048608 | tf_op jit(solution)/shard_map/all_to_all | solution.py:1102
  (503 shorter events, 187.0 us)
Async XLA Ops:
  12.7 41.9 %collective-permute-start.3 = (bf16[2,64,4096]{2,1,0:T(8,128)(2,1)S(1)}, bf16[2,64,4096]{2,1,0:T(8,128)(2,1)}, u32[]{:S(2)}, u32[]{:S(2)}) collective-permute-start(bf16[2,64,4096]{2,1,0:T(8,128)(2,1)S(1)} %maximum_maximum_fusion), channel_id=1, source_target_pairs={{0,1},{1,2},{2,3},{3,0},{4,5},{5,6},{6,7},{7,4},{8,9},{9,10},{10,1... | collective-permute-start | bytes 3145736 | tf_op jit(solution)/shard_map/ppermute | solution.py:41
  15.3 39.7 %collective-permute-start.5 = (bf16[2,64,4096]{2,1,0:T(8,128)(2,1)S(1)}, bf16[2,64,4096]{2,1,0:T(8,128)(2,1)}, u32[]{:S(2)}, u32[]{:S(2)}) collective-permute-start(bf16[2,64,4096]{2,1,0:T(8,128)(2,1)S(1)} %maximum_maximum_fusion), channel_id=1, source_target_pairs={{0,16},{16,0},{1,17},{17,1},{2,18},{18,2},{3,19},{19,3},{4,20},{20... | collective-permute-start | bytes 3145736 | tf_op jit(solution)/shard_map/ppermute | solution.py:41
  32.3 23.3 %collective-permute-start.1 = (bf16[2,64,4224]{2,1,0:T(8,128)(2,1)}, bf16[2,64,4224]{2,1,0:T(8,128)(2,1)}, u32[]{:S(2)}, u32[]{:S(2)}) collective-permute-start(bf16[2,64,4224]{2,1,0:T(8,128)(2,1)} %get-tuple-element.234), channel_id=1, source_target_pairs={{0,4},{4,0},{1,5},{5,1},{2,6},{6,2},{3,7},{7,3},{8,12},{12,8},{9,1... | collective-permute-start | bytes 3244040 | tf_op jit(solution)/shard_map/ppermute | solution.py:36
  33.0 17.3 %collective-permute-start.6 = (f32[1,64]{1,0:T(1,128)S(1)}, f32[1,64]{1,0:T(1,128)S(1)}, u32[]{:S(2)}, u32[]{:S(2)}) collective-permute-start(f32[1,64]{1,0:T(1,128)S(1)} %bitcast.650), channel_id=1, source_target_pairs={{0,1},{1,2},{2,3},{3,0},{4,5},{5,6},{6,7},{7,4},{8,9},{9,10},{10,1... | collective-permute-start | bytes 776 | tf_op jit(solution)/shard_map/ppermute | solution.py:41
  50.3 26.0 %collective-permute-start.4 = (bf16[2,64,4096]{2,1,0:T(8,128)(2,1)S(1)}, bf16[2,64,4096]{2,1,0:T(8,128)(2,1)S(1)}, u32[]{:S(2)}, u32[]{:S(2)}) collective-permute-start(bf16[2,64,4096]{2,1,0:T(8,128)(2,1)S(1)} %maximum_maximum_fusion), channel_id=1, source_target_pairs={{0,8},{8,0},{1,9},{9,1},{2,10},{10,2},{3,11},{11,3},{4,12},{12,4},... | collective-permute-start | bytes 3145736 | tf_op jit(solution)/shard_map/ppermute | solution.py:36
  51.8 25.7 %collective-permute-start.7 = (f32[1,64]{1,0:T(1,128)S(1)}, f32[1,64]{1,0:T(1,128)S(1)}, u32[]{:S(2)}, u32[]{:S(2)}) collective-permute-start(f32[1,64]{1,0:T(1,128)S(1)} %collective-permute-done.6), channel_id=1, source_target_pairs={{0,1},{1,2},{2,3},{3,0},{4,5},{5,6},{6,7},{7,4},{8,9},{9,10},{10,1... | collective-permute-start | bytes 776 | tf_op jit(solution)/shard_map/ppermute | solution.py:41
  54.5 44.3 %collective-permute-start.11 = (bf16[2,64,4096]{2,1,0:T(8,128)(2,1)}, bf16[2,64,4096]{2,1,0:T(8,128)(2,1)}, u32[]{:S(2)}, u32[]{:S(2)}) collective-permute-start(bf16[2,64,4096]{2,1,0:T(8,128)(2,1)} %collective-permute-done.3), channel_id=1, source_target_pairs={{0,16},{16,0},{1,17},{17,1},{2,18},{18,2},{3,19},{19,3},{4,20},{20... | collective-permute-start | bytes 3145736 | tf_op jit(solution)/shard_map/ppermute | solution.py:41
  55.0 43.8 %collective-permute-start.9 = (bf16[2,64,4096]{2,1,0:T(8,128)(2,1)}, bf16[2,64,4096]{2,1,0:T(8,128)(2,1)}, u32[]{:S(2)}, u32[]{:S(2)}) collective-permute-start(bf16[2,64,4096]{2,1,0:T(8,128)(2,1)} %collective-permute-done.3), channel_id=1, source_target_pairs={{0,1},{1,2},{2,3},{3,0},{4,5},{5,6},{6,7},{7,4},{8,9},{9,10},{10,1... | collective-permute-start | bytes 3145736 | tf_op jit(solution)/shard_map/ppermute | solution.py:41
  55.6 43.2 %collective-permute-start.10 = (bf16[2,64,4096]{2,1,0:T(8,128)(2,1)}, bf16[2,64,4096]{2,1,0:T(8,128)(2,1)}, u32[]{:S(2)}, u32[]{:S(2)}) collective-permute-start(bf16[2,64,4096]{2,1,0:T(8,128)(2,1)} %collective-permute-done.5), channel_id=1, source_target_pairs={{0,8},{8,0},{1,9},{9,1},{2,10},{10,2},{3,11},{11,3},{4,12},{12,4},... | collective-permute-start | bytes 3145736 | tf_op jit(solution)/shard_map/ppermute | solution.py:36
  77.6 15.1 %collective-permute-start.14 = (f32[1,64]{1,0:T(1,128)S(1)}, f32[1,64]{1,0:T(1,128)S(1)}, u32[]{:S(2)}, u32[]{:S(2)}) collective-permute-start(f32[1,64]{1,0:T(1,128)S(1)} %collective-permute-done.7), channel_id=1, source_target_pairs={{0,1},{1,2},{2,3},{3,0},{4,5},{5,6},{6,7},{7,4},{8,9},{9,10},{10,1... | collective-permute-start | bytes 776 | tf_op jit(solution)/shard_map/ppermute | solution.py:41
  79.2 32.9 %collective-permute-start.17 = (bf16[2,64,4224]{2,1,0:T(8,128)(2,1)}, bf16[2,64,4224]{2,1,0:T(8,128)(2,1)S(1)}, u32[]{:S(2)}, u32[]{:S(2)}) collective-permute-start(bf16[2,64,4224]{2,1,0:T(8,128)(2,1)} %pad_maximum_fusion.1), channel_id=1, source_target_pairs={{0,16},{16,0},{1,17},{17,1},{2,18},{18,2},{3,19},{19,3},{4,20},{20... | collective-permute-start | bytes 3244040 | tf_op jit(solution)/shard_map/ppermute | solution.py:41
  79.7 74.6 %all-to-all-start = ((bf16[4,64,2048]{2,1,0:T(8,128)(2,1)}), bf16[4,64,2048]{2,1,0:T(8,128)(2,1)S(1)}, u32[]{:S(2)}, u32[]{:S(2)}) async-start(bf16[4,64,2048]{2,1,0:T(8,128)(2,1)} %bitcast.15), calls=%async_computation | async-start | bytes 2097152 | tf_op jit(solution)/shard_map/all_to_all | solution.py:908
  92.7 29.4 %collective-permute-start.16 = (bf16[2,64,4224]{2,1,0:T(8,128)(2,1)}, bf16[2,64,4224]{2,1,0:T(8,128)(2,1)}, u32[]{:S(2)}, u32[]{:S(2)}) collective-permute-start(bf16[2,64,4224]{2,1,0:T(8,128)(2,1)} %pad_maximum_fusion.2), channel_id=1, source_target_pairs={{0,8},{8,0},{1,9},{9,1},{2,10},{10,2},{3,11},{11,3},{4,12},{12,4},... | collective-permute-start | bytes 3244040 | tf_op jit(solution)/shard_map/ppermute | solution.py:36
  98.9 46.4 %collective-permute-start.13 = (bf16[2,64,4096]{2,1,0:T(8,128)(2,1)}, bf16[2,64,4096]{2,1,0:T(8,128)(2,1)S(1)}, u32[]{:S(2)}, u32[]{:S(2)}) collective-permute-start(bf16[2,64,4096]{2,1,0:T(8,128)(2,1)} %collective-permute-done.9), channel_id=1, source_target_pairs={{0,16},{16,0},{1,17},{17,1},{2,18},{18,2},{3,19},{19,3},{4,20},{20... | collective-permute-start | bytes 3145736 | tf_op jit(solution)/shard_map/ppermute | solution.py:41
  99.4 12.7 %collective-permute-start.15 = (f32[4,64]{1,0:T(4,128)S(1)}, f32[4,64]{1,0:T(4,128)S(1)}, u32[]{:S(2)}, u32[]{:S(2)}) collective-permute-start(f32[4,64]{1,0:T(4,128)S(1)} %dynamic_update_slice.192), channel_id=1, source_target_pairs={{0,4},{4,0},{1,5},{5,1},{2,6},{6,2},{3,7},{7,3},{8,12},{12,8},{9,1... | collective-permute-start | bytes 3080 | tf_op jit(solution)/shard_map/ppermute | solution.py:36
  99.4 46.0 %collective-permute-start.12 = (bf16[2,64,4096]{2,1,0:T(8,128)(2,1)}, bf16[2,64,4096]{2,1,0:T(8,128)(2,1)S(1)}, u32[]{:S(2)}, u32[]{:S(2)}) collective-permute-start(bf16[2,64,4096]{2,1,0:T(8,128)(2,1)} %collective-permute-done.3), channel_id=1, source_target_pairs={{0,8},{8,0},{1,9},{9,1},{2,10},{10,2},{3,11},{11,3},{4,12},{12,4},... | collective-permute-start | bytes 3145736 | tf_op jit(solution)/shard_map/ppermute | solution.py:36
  122.1 48.1 %collective-permute-start.22 = (bf16[2,64,4224]{2,1,0:T(8,128)(2,1)}, bf16[2,64,4224]{2,1,0:T(8,128)(2,1)}, u32[]{:S(2)}, u32[]{:S(2)}) collective-permute-start(bf16[2,64,4224]{2,1,0:T(8,128)(2,1)} %collective-permute-done.16), channel_id=1, source_target_pairs={{0,16},{16,0},{1,17},{17,1},{2,18},{18,2},{3,19},{19,3},{4,20},{20... | collective-permute-start | bytes 3244040 | tf_op jit(solution)/shard_map/ppermute | solution.py:41
  122.5 25.6 %collective-permute-start.20 = (bf16[2,64,4096]{2,1,0:T(8,128)(2,1)}, bf16[2,64,4096]{2,1,0:T(8,128)(2,1)}, u32[]{:S(2)}, u32[]{:S(2)}) collective-permute-start(bf16[2,64,4096]{2,1,0:T(8,128)(2,1)} %collective-permute-done.9), channel_id=1, source_target_pairs={{0,1},{1,2},{2,3},{3,0},{4,5},{5,6},{6,7},{7,4},{8,9},{9,10},{10,1... | collective-permute-start | bytes 3145736 | tf_op jit(solution)/shard_map/ppermute | solution.py:41
  124.1 19.6 %collective-permute-start.19 = (f32[8,64]{1,0:T(8,128)S(1)}, f32[8,64]{1,0:T(8,128)S(1)}, u32[]{:S(2)}, u32[]{:S(2)}) collective-permute-start(f32[8,64]{1,0:T(8,128)S(1)} %bitcast.647), channel_id=1, source_target_pairs={{0,8},{8,0},{1,9},{9,1},{2,10},{10,2},{3,11},{11,3},{4,12},{12,4},... | collective-permute-start | bytes 6152 | tf_op jit(solution)/shard_map/ppermute | solution.py:36
  143.8 26.4 %collective-permute-start.21 = (bf16[2,64,4096]{2,1,0:T(8,128)(2,1)}, bf16[2,64,4096]{2,1,0:T(8,128)(2,1)}, u32[]{:S(2)}, u32[]{:S(2)}) collective-permute-start(bf16[2,64,4096]{2,1,0:T(8,128)(2,1)} %collective-permute-done.11), channel_id=1, source_target_pairs={{0,8},{8,0},{1,9},{9,1},{2,10},{10,2},{3,11},{11,3},{4,12},{12,4},... | collective-permute-start | bytes 3145736 | tf_op jit(solution)/shard_map/ppermute | solution.py:36
  145.4 29.1 %collective-permute-start.18 = (bf16[2,64,4224]{2,1,0:T(8,128)(2,1)}, bf16[2,64,4224]{2,1,0:T(8,128)(2,1)}, u32[]{:S(2)}, u32[]{:S(2)}) collective-permute-start(bf16[2,64,4224]{2,1,0:T(8,128)(2,1)} %pad_maximum_fusion.1), channel_id=1, source_target_pairs={{0,1},{1,2},{2,3},{3,0},{4,5},{5,6},{6,7},{7,4},{8,9},{9,10},{10,1... | collective-permute-start | bytes 3244040 | tf_op jit(solution)/shard_map/ppermute | solution.py:41
  147.0 45.7 %collective-permute-start.25 = (bf16[2,64,4096]{2,1,0:T(8,128)(2,1)}, bf16[2,64,4096]{2,1,0:T(8,128)(2,1)}, u32[]{:S(2)}, u32[]{:S(2)}) collective-permute-start(bf16[2,64,4096]{2,1,0:T(8,128)(2,1)} %collective-permute-done.9), channel_id=1, source_target_pairs={{0,8},{8,0},{1,9},{9,1},{2,10},{10,2},{3,11},{11,3},{4,12},{12,4},... | collective-permute-start | bytes 3145736 | tf_op jit(solution)/shard_map/ppermute | solution.py:36
  153.1 65.0 %collective-permute-start.26 = (bf16[2,64,4096]{2,1,0:T(8,128)(2,1)}, bf16[2,64,4096]{2,1,0:T(8,128)(2,1)}, u32[]{:S(2)}, u32[]{:S(2)}) collective-permute-start(bf16[2,64,4096]{2,1,0:T(8,128)(2,1)} %collective-permute-done.20), channel_id=1, source_target_pairs={{0,16},{16,0},{1,17},{17,1},{2,18},{18,2},{3,19},{19,3},{4,20},{20... | collective-permute-start | bytes 3145736 | tf_op jit(solution)/shard_map/ppermute | solution.py:41
  154.3 63.8 %all-to-all-start.1 = ((bf16[4,64,2048]{2,1,0:T(8,128)(2,1)}), bf16[4,64,2048]{2,1,0:T(8,128)(2,1)S(1)}, u32[]{:S(2)}, u32[]{:S(2)}) async-start(bf16[4,64,2048]{2,1,0:T(8,128)(2,1)} %bitcast.583), calls=%async_computation.1 | async-start | bytes 2097152 | tf_op jit(solution)/shard_map/all_to_all | solution.py:908
  170.2 47.9 %collective-permute-start.24 = (bf16[2,64,4224]{2,1,0:T(8,128)(2,1)}, bf16[2,64,4224]{2,1,0:T(8,128)(2,1)}, u32[]{:S(2)}, u32[]{:S(2)}) collective-permute-start(bf16[2,64,4224]{2,1,0:T(8,128)(2,1)} %collective-permute-done.16), channel_id=1, source_target_pairs={{0,1},{1,2},{2,3},{3,0},{4,5},{5,6},{6,7},{7,4},{8,9},{9,10},{10,1... | collective-permute-start | bytes 3244040 | tf_op jit(solution)/shard_map/ppermute | solution.py:41
  171.8 54.4 %collective-permute-start.28 = (bf16[2,64,4096]{2,1,0:T(8,128)(2,1)}, bf16[2,64,4096]{2,1,0:T(8,128)(2,1)}, u32[]{:S(2)}, u32[]{:S(2)}) collective-permute-start(bf16[2,64,4096]{2,1,0:T(8,128)(2,1)} %copy-done.41), channel_id=1, source_target_pairs={{0,8},{8,0},{1,9},{9,1},{2,10},{10,2},{3,11},{11,3},{4,12},{12,4},... | collective-permute-start | bytes 3145736 | tf_op jit(solution)/shard_map/ppermute | solution.py:36
  174.5 63.5 %collective-permute-start.30 = (bf16[2,64,4224]{2,1,0:T(8,128)(2,1)}, bf16[2,64,4224]{2,1,0:T(8,128)(2,1)}, u32[]{:S(2)}, u32[]{:S(2)}) collective-permute-start(bf16[2,64,4224]{2,1,0:T(8,128)(2,1)} %collective-permute-done.18), channel_id=1, source_target_pairs={{0,16},{16,0},{1,17},{17,1},{2,18},{18,2},{3,19},{19,3},{4,20},{20... | collective-permute-start | bytes 3244040 | tf_op jit(solution)/shard_map/ppermute | solution.py:41
  192.7 40.8 %collective-permute-start.23 = (bf16[256,2048]{1,0:T(8,128)(2,1)S(1)}, bf16[256,2048]{1,0:T(8,128)(2,1)}, u32[]{:S(2)}, u32[]{:S(2)}) collective-permute-start(bf16[256,2048]{1,0:T(8,128)(2,1)S(1)} %bitcast.575), channel_id=1, source_target_pairs={{0,4},{4,0},{1,5},{5,1},{2,6},{6,2},{3,7},{7,3},{8,12},{12,8},{9,1... | collective-permute-start | bytes 3145736 | tf_op jit(solution)/shard_map/ppermute | solution.py:36
  218.0 28.7 %collective-permute-start.41 = (bf16[2,64,4224]{2,1,0:T(8,128)(2,1)}, bf16[2,64,4224]{2,1,0:T(8,128)(2,1)S(1)}, u32[]{:S(2)}, u32[]{:S(2)}) collective-permute-start(bf16[2,64,4224]{2,1,0:T(8,128)(2,1)} %collective-permute-done.18), channel_id=1, source_target_pairs={{0,1},{1,2},{2,3},{3,0},{4,5},{5,6},{6,7},{7,4},{8,9},{9,10},{10,1... | collective-permute-start | bytes 3244040 | tf_op jit(solution)/shard_map/ppermute | solution.py:41
  218.1 26.3 %collective-permute-start.29 = (bf16[2,64,4096]{2,1,0:T(8,128)(2,1)}, bf16[2,64,4096]{2,1,0:T(8,128)(2,1)S(1)}, u32[]{:S(2)}, u32[]{:S(2)}) collective-permute-start(bf16[2,64,4096]{2,1,0:T(8,128)(2,1)} %collective-permute-done.20), channel_id=1, source_target_pairs={{0,8},{8,0},{1,9},{9,1},{2,10},{10,2},{3,11},{11,3},{4,12},{12,4},... | collective-permute-start | bytes 3145736 | tf_op jit(solution)/shard_map/ppermute | solution.py:36
  226.2 27.0 %collective-permute-start.42 = (bf16[2,64,4224]{2,1,0:T(8,128)(2,1)}, bf16[2,64,4224]{2,1,0:T(8,128)(2,1)S(1)}, u32[]{:S(2)}, u32[]{:S(2)}) collective-permute-start(bf16[2,64,4224]{2,1,0:T(8,128)(2,1)} %collective-permute-done.24), channel_id=1, source_target_pairs={{0,16},{16,0},{1,17},{17,1},{2,18},{18,2},{3,19},{19,3},{4,20},{20... | collective-permute-start | bytes 3244040 | tf_op jit(solution)/shard_map/ppermute | solution.py:41
  238.0 59.3 %collective-permute-start.40 = (bf16[2,64,4224]{2,1,0:T(8,128)(2,1)}, bf16[2,64,4224]{2,1,0:T(8,128)(2,1)S(1)}, u32[]{:S(2)}, u32[]{:S(2)}) collective-permute-start(bf16[2,64,4224]{2,1,0:T(8,128)(2,1)} %collective-permute-done.24), channel_id=1, source_target_pairs={{0,1},{1,2},{2,3},{3,0},{4,5},{5,6},{6,7},{7,4},{8,9},{9,10},{10,1... | collective-permute-start | bytes 3244040 | tf_op jit(solution)/shard_map/ppermute | solution.py:41
  238.2 27.7 %collective-permute-start.31 = (bf16[2,64,4096]{2,1,0:T(8,128)(2,1)}, bf16[2,64,4096]{2,1,0:T(8,128)(2,1)S(1)}, u32[]{:S(2)}, u32[]{:S(2)}) collective-permute-start(bf16[2,64,4096]{2,1,0:T(8,128)(2,1)} %collective-permute-done.26), channel_id=1, source_target_pairs={{0,8},{8,0},{1,9},{9,1},{2,10},{10,2},{3,11},{11,3},{4,12},{12,4},... | collective-permute-start | bytes 3145736 | tf_op jit(solution)/shard_map/ppermute | solution.py:36
  246.8 54.0 %collective-permute-start.43 = (bf16[2,64,4224]{2,1,0:T(8,128)(2,1)S(1)}, bf16[2,64,4224]{2,1,0:T(8,128)(2,1)S(1)}, u32[]{:S(2)}, u32[]{:S(2)}) collective-permute-start(bf16[2,64,4224]{2,1,0:T(8,128)(2,1)S(1)} %collective-permute-done.41), channel_id=1, source_target_pairs={{0,16},{16,0},{1,17},{17,1},{2,18},{18,2},{3,19},{19,3},{4,20},{20... | collective-permute-start | bytes 3244040 | tf_op jit(solution)/shard_map/ppermute | solution.py:41
  253.2 48.0 %collective-permute-start.45 = (bf16[2,64,4224]{2,1,0:T(8,128)(2,1)S(1)}, bf16[2,64,4224]{2,1,0:T(8,128)(2,1)S(1)}, u32[]{:S(2)}, u32[]{:S(2)}) collective-permute-start(bf16[2,64,4224]{2,1,0:T(8,128)(2,1)S(1)} %collective-permute-done.41), channel_id=1, source_target_pairs={{0,1},{1,2},{2,3},{3,0},{4,5},{5,6},{6,7},{7,4},{8,9},{9,10},{10,1... | collective-permute-start | bytes 3244040 | tf_op jit(solution)/shard_map/ppermute | solution.py:41
  286.5 24.3 %collective-permute-start.33 = (bf16[256,2048]{1,0:T(8,128)(2,1)S(1)}, bf16[256,2048]{1,0:T(8,128)(2,1)}, u32[]{:S(2)}, u32[]{:S(2)}) collective-permute-start(bf16[256,2048]{1,0:T(8,128)(2,1)S(1)} %bitcast.580), channel_id=1, source_target_pairs={{0,8},{8,0},{1,9},{9,1},{2,10},{10,2},{3,11},{11,3},{4,12},{12,4},... | collective-permute-start | bytes 3145736 | tf_op jit(solution)/shard_map/ppermute | solution.py:36
  297.3 28.4 %collective-permute-start.46 = (bf16[2,64,4224]{2,1,0:T(8,128)(2,1)S(1)}, bf16[2,64,4224]{2,1,0:T(8,128)(2,1)S(1)}, u32[]{:S(2)}, u32[]{:S(2)}) collective-permute-start(bf16[2,64,4224]{2,1,0:T(8,128)(2,1)S(1)} %collective-permute-done.40), channel_id=1, source_target_pairs={{0,16},{16,0},{1,17},{17,1},{2,18},{18,2},{3,19},{19,3},{4,20},{20... | collective-permute-start | bytes 3244040 | tf_op jit(solution)/shard_map/ppermute | solution.py:41
  300.8 26.6 %collective-permute-start.44 = (bf16[2,64,4224]{2,1,0:T(8,128)(2,1)S(1)}, bf16[2,64,4224]{2,1,0:T(8,128)(2,1)S(1)}, u32[]{:S(2)}, u32[]{:S(2)}) collective-permute-start(bf16[2,64,4224]{2,1,0:T(8,128)(2,1)S(1)} %collective-permute-done.40), channel_id=1, source_target_pairs={{0,1},{1,2},{2,3},{3,0},{4,5},{5,6},{6,7},{7,4},{8,9},{9,10},{10,1... | collective-permute-start | bytes 3244040 | tf_op jit(solution)/shard_map/ppermute | solution.py:41
  301.2 46.1 %collective-permute-start.47 = (bf16[2,64,4224]{2,1,0:T(8,128)(2,1)S(1)}, bf16[2,64,4224]{2,1,0:T(8,128)(2,1)S(1)}, u32[]{:S(2)}, u32[]{:S(2)}) collective-permute-start(bf16[2,64,4224]{2,1,0:T(8,128)(2,1)S(1)} %collective-permute-done.45), channel_id=1, source_target_pairs={{0,16},{16,0},{1,17},{17,1},{2,18},{18,2},{3,19},{19,3},{4,20},{20... | collective-permute-start | bytes 3244040 | tf_op jit(solution)/shard_map/ppermute | solution.py:41
  323.7 7.8 %collective-permute-start.34 = (bf16[256,2048]{1,0:T(8,128)(2,1)S(1)}, bf16[256,2048]{1,0:T(8,128)(2,1)S(1)}, u32[]{:S(2)}, u32[]{:S(2)}) collective-permute-start(bf16[256,2048]{1,0:T(8,128)(2,1)S(1)} %pad_maximum_fusion.5), channel_id=1, source_target_pairs={{0,4},{4,0},{1,5},{5,1},{2,6},{6,2},{3,7},{7,3},{8,12},{12,8},{9,1... | collective-permute-start | bytes 3145736 | tf_op jit(solution)/shard_map/ppermute | solution.py:36
  324.2 46.2 %collective-permute-start.39 = (bf16[256,2048]{1,0:T(8,128)(2,1)}, bf16[256,2048]{1,0:T(8,128)(2,1)}, u32[]{:S(2)}, u32[]{:S(2)}) collective-permute-start(bf16[256,2048]{1,0:T(8,128)(2,1)} %collective-permute-done.33.g_ref), channel_id=1, source_target_pairs={{0,4},{4,0},{1,5},{5,1},{2,6},{6,2},{3,7},{7,3},{8,12},{12,8},{9,1... | collective-permute-start | bytes 3145736 | tf_op jit(solution)/shard_map/ppermute | solution.py:36
  327.4 41.0 %collective-permute-start.48 = (bf16[2,64,4224]{2,1,0:T(8,128)(2,1)S(1)}, bf16[2,64,4224]{2,1,0:T(8,128)(2,1)S(1)}, u32[]{:S(2)}, u32[]{:S(2)}) collective-permute-start(bf16[2,64,4224]{2,1,0:T(8,128)(2,1)S(1)} %collective-permute-done.44), channel_id=1, source_target_pairs={{0,16},{16,0},{1,17},{17,1},{2,18},{18,2},{3,19},{19,3},{4,20},{20... | collective-permute-start | bytes 3244040 | tf_op jit(solution)/shard_map/ppermute | solution.py:41
  334.7 23.5 %collective-permute-start.37 = (bf16[256,2048]{1,0:T(8,128)(2,1)}, bf16[256,2048]{1,0:T(8,128)(2,1)S(1)}, u32[]{:S(2)}, u32[]{:S(2)}) collective-permute-start(bf16[256,2048]{1,0:T(8,128)(2,1)} %multiply_convert_fusion.h_ref), channel_id=1, source_target_pairs={{0,8},{8,0},{1,9},{9,1},{2,10},{10,2},{3,11},{11,3},{4,12},{12,4},... | collective-permute-start | bytes 3145736 | tf_op jit(solution)/shard_map/ppermute | solution.py:36
  358.2 11.2 %collective-permute-start.38 = (bf16[256,2048]{1,0:T(8,128)(2,1)S(1)}, bf16[256,2048]{1,0:T(8,128)(2,1)S(1)}, u32[]{:S(2)}, u32[]{:S(2)}) collective-permute-start(bf16[256,2048]{1,0:T(8,128)(2,1)S(1)} %collective-permute-done.37.h_ref), channel_id=1, source_target_pairs={{0,4},{4,0},{1,5},{5,1},{2,6},{6,2},{3,7},{7,3},{8,12},{12,8},{9,1... | collective-permute-start | bytes 3145736 | tf_op jit(solution)/shard_map/ppermute | solution.py:36
  401.5 5.9 collective-permute-start.36
  402.0 6.9 %collective-permute-start.50 = (bf16[256,2048]{1,0:T(8,128)(2,1)S(1)}, bf16[256,2048]{1,0:T(8,128)(2,1)S(1)}, u32[]{:S(2)}, u32[]{:S(2)}) collective-permute-start(bf16[256,2048]{1,0:T(8,128)(2,1)S(1)} %bitcast.581), channel_id=1, source_target_pairs={{0,4},{4,0},{1,5},{5,1},{2,6},{6,2},{3,7},{7,3},{8,12},{12,8},{9,1... | collective-permute-start | bytes 3145736 | tf_op jit(solution)/shard_map/ppermute | solution.py:36
  407.4 33.1 %collective-permute-start.51 = (bf16[256,2048]{1,0:T(8,128)(2,1)S(1)}, bf16[256,2048]{1,0:T(8,128)(2,1)}, u32[]{:S(2)}, u32[]{:S(2)}) collective-permute-start(bf16[256,2048]{1,0:T(8,128)(2,1)S(1)} %add_convert_fusion.3), channel_id=1, source_target_pairs={{0,8},{8,0},{1,9},{9,1},{2,10},{10,2},{3,11},{11,3},{4,12},{12,4},... | collective-permute-start | bytes 3145736 | tf_op jit(solution)/shard_map/ppermute | solution.py:36
  440.6 9.8 %collective-permute-start.54 = (bf16[256,2048]{1,0:T(8,128)(2,1)}, bf16[256,2048]{1,0:T(8,128)(2,1)}, u32[]{:S(2)}, u32[]{:S(2)}) collective-permute-start(bf16[256,2048]{1,0:T(8,128)(2,1)} %get-tuple-element.410), channel_id=1, source_target_pairs={{0,4},{4,0},{1,5},{5,1},{2,6},{6,2},{3,7},{7,3},{8,12},{12,8},{9,1... | collective-permute-start | bytes 3145736 | tf_op jit(solution)/shard_map/ppermute | solution.py:36
  452.4 25.6 %collective-permute-start.55 = (bf16[256,2048]{1,0:T(8,128)(2,1)S(1)}, bf16[256,2048]{1,0:T(8,128)(2,1)}, u32[]{:S(2)}, u32[]{:S(2)}) collective-permute-start(bf16[256,2048]{1,0:T(8,128)(2,1)S(1)} %add_convert_fusion.1), channel_id=1, source_target_pairs={{0,8},{8,0},{1,9},{9,1},{2,10},{10,2},{3,11},{11,3},{4,12},{12,4},... | collective-permute-start | bytes 3145736 | tf_op jit(solution)/shard_map/ppermute | solution.py:36
  486.8 17.1 %collective-permute-start.58 = (f32[1,2048]{1,0:T(1,128)S(1)}, f32[1,2048]{1,0:T(1,128)S(1)}, u32[]{:S(2)}, u32[]{:S(2)}) collective-permute-start(f32[1,2048]{1,0:T(1,128)S(1)} %div.65.cdm_ref), channel_id=1, source_target_pairs={{0,4},{4,0},{1,5},{5,1},{2,6},{6,2},{3,7},{7,3},{8,12},{12,8},{9,1... | collective-permute-start | bytes 24584 | tf_op jit(solution)/shard_map/ppermute | solution.py:36
  503.8 18.3 %collective-permute-start.70 = (bf16[256,2048]{1,0:T(8,128)(2,1)}, bf16[256,2048]{1,0:T(8,128)(2,1)S(1)}, u32[]{:S(2)}, u32[]{:S(2)}) collective-permute-start(bf16[256,2048]{1,0:T(8,128)(2,1)} %slice.486), channel_id=1, source_target_pairs={{0,4},{4,0},{1,5},{5,1},{2,6},{6,2},{3,7},{7,3},{8,12},{12,8},{9,1... | collective-permute-start | bytes 3145736 | tf_op jit(solution)/shard_map/ppermute | solution.py:36
  504.0 6.5 %collective-permute-start.59 = (f32[1,2048]{1,0:T(1,128)S(1)}, f32[1,2048]{1,0:T(1,128)S(1)}, u32[]{:S(2)}, u32[]{:S(2)}) collective-permute-start(f32[1,2048]{1,0:T(1,128)S(1)} %add.663), channel_id=1, source_target_pairs={{0,8},{8,0},{1,9},{9,1},{2,10},{10,2},{3,11},{11,3},{4,12},{12,4},... | collective-permute-start | bytes 24584 | tf_op jit(solution)/shard_map/ppermute | solution.py:36
  515.2 34.0 %all-to-all-start.2 = ((bf16[4,64,2048]{2,1,0:T(8,128)(2,1)}), bf16[4,64,2048]{2,1,0:T(8,128)(2,1)S(1)}, u32[]{:S(2)}, u32[]{:S(2)}) async-start(bf16[4,64,2048]{2,1,0:T(8,128)(2,1)} %bitcast.182), calls=%async_computation.2 | async-start | bytes 2097152 | tf_op jit(solution)/shard_map/all_to_all | solution.py:1102
  521.0 6.8 %collective-permute-start.61 = (bf16[200,512]{1,0:T(8,128)(2,1)S(1)}, bf16[200,512]{1,0:T(8,128)(2,1)S(1)}, u32[]{:S(2)}, u32[]{:S(2)}) collective-permute-start(bf16[200,512]{1,0:T(8,128)(2,1)S(1)} %fusion.91), channel_id=1, source_target_pairs={{0,8},{8,0},{1,9},{9,1},{2,10},{10,2},{3,11},{11,3},{4,12},{12,4},... | collective-permute-start | bytes 614408 | tf_op jit(solution)/shard_map/ppermute | solution.py:36
  533.8 9.2 %collective-permute-start.63 = (bf16[48,512]{1,0:T(8,128)(2,1)S(1)}, bf16[48,512]{1,0:T(8,128)(2,1)S(1)}, u32[]{:S(2)}, u32[]{:S(2)}) collective-permute-start(bf16[48,512]{1,0:T(8,128)(2,1)S(1)} %get-tuple-element.495), channel_id=1, source_target_pairs={{0,1},{1,2},{2,3},{3,0},{4,5},{5,6},{6,7},{7,4},{8,9},{9,10},{10,1... | collective-permute-start | bytes 147464 | tf_op jit(solution)/shard_map/ppermute | solution.py:41
  535.6 13.6 %collective-permute-start.64 = (bf16[48,512]{1,0:T(8,128)(2,1)S(1)}, bf16[48,512]{1,0:T(8,128)(2,1)S(1)}, u32[]{:S(2)}, u32[]{:S(2)}) collective-permute-start(bf16[48,512]{1,0:T(8,128)(2,1)S(1)} %get-tuple-element.497), channel_id=1, source_target_pairs={{0,2},{1,3},{2,0},{3,1},{4,6},{5,7},{6,4},{7,5},{8,10},{9,11},{10,... | collective-permute-start | bytes 147464 | tf_op jit(solution)/shard_map/ppermute | solution.py:41
  538.0 11.3 %collective-permute-start.65 = (bf16[48,512]{1,0:T(8,128)(2,1)S(1)}, bf16[48,512]{1,0:T(8,128)(2,1)S(1)}, u32[]{:S(2)}, u32[]{:S(2)}) collective-permute-start(bf16[48,512]{1,0:T(8,128)(2,1)S(1)} %get-tuple-element.496), channel_id=1, source_target_pairs={{0,3},{1,0},{2,1},{3,2},{4,7},{5,4},{6,5},{7,6},{8,11},{9,8},{10,9... | collective-permute-start | bytes 147464 | tf_op jit(solution)/shard_map/ppermute | solution.py:41
  549.3 6.0 collective-permute-start.67
  550.4 6.0 collective-permute-start.68
  562.2 6.1 %collective-permute-start.76 = (bf16[168,512]{1,0:T(8,128)(2,1)S(1)}, bf16[168,512]{1,0:T(8,128)(2,1)}, u32[]{:S(2)}, u32[]{:S(2)}) collective-permute-start(bf16[168,512]{1,0:T(8,128)(2,1)S(1)} %slice.607), channel_id=1, source_target_pairs={{0,8},{8,0},{1,9},{9,1},{2,10},{10,2},{3,11},{11,3},{4,12},{12,4},... | collective-permute-start | bytes 516104 | tf_op jit(solution)/shard_map/ppermute | solution.py:36
  563.4 12.6 %collective-permute-start.66 = (bf16[2,1,64,2048]{3,2,0,1:T(8,128)(2,1)S(1)}, bf16[2,1,64,2048]{3,2,0,1:T(8,128)(2,1)}, u32[]{:S(2)}, u32[]{:S(2)}) collective-permute-start(bf16[2,1,64,2048]{3,2,0,1:T(8,128)(2,1)S(1)} %dynamic-slice_bitcast_fusion.1), channel_id=1, source_target_pairs={{0,4},{4,0},{1,5},{5,1},{2,6},{6,2},{3,7},{7,3},{8,12},{12,8},{9,1... | collective-permute-start | bytes 1572872 | tf_op jit(solution)/shard_map/ppermute | solution.py:36
  563.5 30.2 %all-to-all-start.3 = ((bf16[4,64,2048]{2,1,0:T(8,128)(2,1)}), bf16[4,64,2048]{2,1,0:T(8,128)(2,1)S(1)}, u32[]{:S(2)}, u32[]{:S(2)}) async-start(bf16[4,64,2048]{2,1,0:T(8,128)(2,1)} %bitcast.194), calls=%async_computation.3 | async-start | bytes 2097152 | tf_op jit(solution)/shard_map/all_to_all | solution.py:1102
  567.3 7.3 %collective-permute-start.73 = (bf16[200,512]{1,0:T(8,128)(2,1)S(1)}, bf16[200,512]{1,0:T(8,128)(2,1)S(1)}, u32[]{:S(2)}, u32[]{:S(2)}) collective-permute-start(bf16[200,512]{1,0:T(8,128)(2,1)S(1)} %slice.578), channel_id=1, source_target_pairs={{0,8},{8,0},{1,9},{9,1},{2,10},{10,2},{3,11},{11,3},{4,12},{12,4},... | collective-permute-start | bytes 614408 | tf_op jit(solution)/shard_map/ppermute | solution.py:36
  570.1 15.0 %collective-permute-start.77 = (bf16[2,168,512]{2,1,0:T(8,128)(2,1)}, bf16[2,168,512]{2,1,0:T(8,128)(2,1)}, u32[]{:S(2)}, u32[]{:S(2)}) collective-permute-start(bf16[2,168,512]{2,1,0:T(8,128)(2,1)} %pad_maximum_fusion.17), channel_id=1, source_target_pairs={{0,4},{4,0},{1,5},{5,1},{2,6},{6,2},{3,7},{7,3},{8,12},{12,8},{9,1... | collective-permute-start | bytes 1032200 | tf_op jit(solution)/shard_map/ppermute | solution.py:36
  (81 other events, 612.2 us)

commit v4 on v3

--- a/solution.py
+++ b/solution.py
@@ -110,8 +110,8 @@
         box = boxes[source]
         if len(self.rounds) > self.depth:
             old = [b for name, b in self.rounds[-1 - self.depth] if b is not box and "_" not in name]
-            if len(self.rounds) > 4:
-                old += [b for name, b in self.rounds[-5] if b is not box and "_" in name]
+            if len(self.rounds) > 6:
+                old += [b for name, b in self.rounds[-7] if b is not box and "_" in name]
             held = [b for b in self.buffers.values() if b.pending()]
             both = lax.optimization_barrier((box.array, [b.array for b in old], [b.array for b in held]))
             box.array = both[0]
@@ -860,8 +860,7 @@
         "a0": Box(attention_piece),
         "m0": Box(feed_near),
         "feed": Box(feed_far),
-        "tokens": Box(relayout_start(tokens)),
-        "cotangent": Box(relayout_start(cotangent)),
+        "rows": Box(jnp.concatenate([relayout_start(tokens), relayout_start(cotangent)], axis=1)),
     }
     inside = width // 2
 
@@ -918,8 +917,7 @@
         order.append((step - 1, step, ring))
     attention_z = [(f"a{source}", f"a{step}", move) for source, step, move in order]
     feed_z = [(f"{side}{source}", f"{side}{step}", move) for source, step, move in order for side in sides]
-    z_queue = attention_z[:2] + [("tokens", "tokens_moved", exchange), ("cotangent", "cotangent_moved", exchange)]
-    z_queue += attention_z[2:] + feed_z
+    z_queue = attention_z[:2] + [("rows", "rows_moved", exchange)] + attention_z[2:] + feed_z
     boxes["s0"] = Box((square_other + square_mine).sum(axis=0))
     small_queue = [(f"s{step - 1}", f"s{step}", ring) for step in range(1, count)]
 
@@ -966,7 +964,8 @@
         links.place(links.placed + 1)
     qkv_weight = buffers["qkv"].array.reshape(width, 3 * inside)
     out_weight = buffers["out"].array.reshape(2, inside, inside)
-    tokens_own = boxes["tokens_moved"].array.reshape(half, width)
+    rows_moved = boxes["rows_moved"].array
+    tokens_own = rows_moved[:, :piece].reshape(half, width)
     tokens_both = jnp.concatenate([tokens_own, swap(tokens_own, "core")], axis=0)
     def positions_of(sub_place, core_place):
         source = jnp.arange(count, dtype=jnp.int32)[:, None] * local
@@ -1016,7 +1015,7 @@
 
     out_rows = by_core(attention_down[3].T)[0].astype(BF)
     contract_square = boxes["square"].array.reshape(1, width)
-    qkv_p, cotangent_own = lax.optimization_barrier((qkv_p, boxes["cotangent_moved"].array))
+    qkv_p, cotangent_own = lax.optimization_barrier((qkv_p, rows_moved[:, piece:]))
     cotangent_own = cotangent_own.reshape(half, width)
     cotangent_far = swap(cotangent_own, "xx")
     mixed, cotangent_far, out_weight = lax.optimization_barrier((mixed, cotangent_far, out_weight))

time: 608 us -> 605 us (level)
  waiting for transfers between devices: 197 us -> 189 us
    ppermute x33, waiting for transfers between devices: 47.8 us -> 38 us  [shift(): return lax.ppermute(a, name, [(i, (i + step) % size) for i in range(size)])]
    all_to_all x2 -> x1, waiting for transfers between devices: 25.4 us -> 33.3 us  [body(): exchange = lambda a: lax.all_to_all(a, 'seq', 0, 0, tiled=True)]
    ppermute x45, waiting for transfers between devices: 117 us -> 111 us  [swap(): return lax.ppermute(a, name, [(0, 1), (1, 0)])]
    unnamed x135 -> x137, local copies, waits for them, and re-layouts: 13.6 us -> 14.1 us
  transfers between devices with their start and end apart: 82 -> 81, of which waited for: 35 -> 29; matrix products, arithmetic and copies ran while one was open for 26% -> 27% of each run, Pallas kernels for 17% -> 18%
where the time goes in v4:
time: 605 us; the launch traced here: 595 us
  waiting for transfers between devices  189 us (31%)
  Pallas kernels  136 us (22%)
  local copies, waits for them, and re-layouts  116 us (19%)
  starting transfers between devices  80.4 us (13%)
  other arithmetic  51.4 us (8%)
  matrix products  18.7 us (3%)
    ppermute x45, waiting for transfers between devices, swap(): return lax.ppermute(a, name, [(0, 1), (1, 0)])  111 us
    dynamic_update_slice x47, local copies, waits for them, and re-layouts, put(): lax.dynamic_update_slice(self.array, part, [jnp.int32(v) for v in start])  74.1 us
    pallas_call x2, Pallas kernels, feed_forward_back(): pl.pallas_call(functools.partial(feed_kernel, known), in_specs=[vmem] * 4...  61.7 us
    ppermute x33, starting transfers between devices, shift(): return lax.ppermute(a, name, [(i, (i + step) % size) for i in range(size)])  40.9 us
    ppermute x33, waiting for transfers between devices, shift(): return lax.ppermute(a, name, [(i, (i + step) % size) for i in range(size)])  38 us
    all_to_all x1, waiting for transfers between devices, body(): exchange = lambda a: lax.all_to_all(a, 'seq', 0, 0, tiled=True)  33.3 us
    ppermute x45, starting transfers between devices, swap(): return lax.ppermute(a, name, [(0, 1), (1, 0)])  27 us
    dot_general x7, matrix products, mm(): return lax.dot_general(a, b, (dims, ((), ())), preferred_element_type=F32)  16.6 us
  transfers between devices with their start and end apart: 81, of which 29 were waited for; matrix products, arithmetic and copies ran while one was open for 27% of the time, Pallas kernels for 18%

profile of v4, /device:TPU:0, one launch (start us, length us, event | category | flops | bytes accessed | tf_op | source)
XLA Modules:
  0.0 594.6 jit_solution(18370656466713335403)
XLA Ops:
  0.7 2.1 fusion.3
  3.4 4.9 dynamic-slice_reduce_fusion.1
  12.7 2.6 collective-permute-start.6
  24.3 3.9 feed_prepare.2
  28.2 4.0 feed_prepare.3
  58.9 15.8 %collective-permute-done.7 = bf16[2,64,4096]{2,1,0:T(8,128)(2,1)S(1)} collective-permute-done((bf16[2,64,4096]{2,1,0:T(8,128)(2,1)S(1)}, bf16[2,64,4096]{2,1,0:T(8,128)(2,1)S(1)}, u32[]{:S(2)}, u32[]{:S(2)}) %collective-permute-start.7) | collective-permute-done | bytes 1048608 | tf_op jit(solution)/shard_map/ppermute | solution.py:36
  78.2 3.6 all-to-all-start
  81.8 2.2 fusion.55
  92.8 4.5 collective-permute-done.11
  102.8 2.1 fusion.52
  107.0 2.1 fusion.50
  112.3 8.2 %collective-permute-done.14 = bf16[2,64,4224]{2,1,0:T(8,128)(2,1)} collective-permute-done((bf16[2,64,4224]{2,1,0:T(8,128)(2,1)}, bf16[2,64,4224]{2,1,0:T(8,128)(2,1)}, u32[]{:S(2)}, u32[]{:S(2)}) %collective-permute-start.14) | collective-permute-done | bytes 1081376 | tf_op jit(solution)/shard_map/ppermute | solution.py:36
  122.6 2.3 bitcast_dynamic-update-slice_fusion.13
  124.8 2.3 bitcast_dynamic-update-slice_fusion.12
  127.1 15.1 %collective-permute-done.16 = f32[8,64]{1,0:T(8,128)S(1)} collective-permute-done((f32[8,64]{1,0:T(8,128)S(1)}, f32[8,64]{1,0:T(8,128)S(1)}, u32[]{:S(2)}, u32[]{:S(2)}) %collective-permute-start.16) | collective-permute-done | bytes 2080 | tf_op jit(solution)/shard_map/ppermute | solution.py:36
  149.1 2.1 fusion.49
  154.7 15.8 %collective-permute-done.23 = f32[16,64]{1,0:T(8,128)S(1)} collective-permute-done((f32[16,64]{1,0:T(8,128)S(1)}, f32[16,64]{1,0:T(8,128)S(1)}, u32[]{:S(2)}, u32[]{:S(2)}) %collective-permute-start.23) | collective-permute-done | bytes 4128 | tf_op jit(solution)/shard_map/ppermute | solution.py:41
  170.5 2.1 collective-permute-start.20
  174.8 2.5 collective-permute-start.27
  178.9 2.3 bitcast_dynamic-update-slice_fusion.11
  182.9 2.1 fusion.46
  185.0 2.3 bitcast_dynamic-update-slice_fusion.10
  188.0 11.6 %collective-permute-done.21 = bf16[2,64,4096]{2,1,0:T(8,128)(2,1)S(1)} collective-permute-done((bf16[2,64,4096]{2,1,0:T(8,128)(2,1)}, bf16[2,64,4096]{2,1,0:T(8,128)(2,1)S(1)}, u32[]{:S(2)}, u32[]{:S(2)}) %collective-permute-start.21) | collective-permute-done | bytes 1048608 | tf_op jit(solution)/shard_map/ppermute | solution.py:36
  199.6 2.5 collective-permute-start.41
  204.7 2.4 bitcast_dynamic-update-slice_fusion.9
  207.8 2.1 fusion.44
  211.6 7.4 %collective-permute-done.28 = bf16[2,64,4096]{2,1,0:T(8,128)(2,1)S(1)} collective-permute-done((bf16[2,64,4096]{2,1,0:T(8,128)(2,1)S(1)}, bf16[2,64,4096]{2,1,0:T(8,128)(2,1)S(1)}, u32[]{:S(2)}, u32[]{:S(2)}) %collective-permute-start.28) | collective-permute-done | bytes 1048608 | tf_op jit(solution)/shard_map/ppermute | solution.py:36
  222.1 33.3 %all-to-all-done = bf16[4,128,2048]{2,1,0:T(8,128)(2,1)S(1)} async-done(((bf16[4,128,2048]{2,1,0:T(8,128)(2,1)}), bf16[4,128,2048]{2,1,0:T(8,128)(2,1)S(1)}, u32[]{:S(2)}, u32[]{:S(2)}) %all-to-all-start) | async-done | bytes 2097184 | tf_op jit(solution)/shard_map/all_to_all | solution.py:907
  255.5 2.9 bitcast_dynamic-update-slice_fusion.8
  258.4 2.3 bitcast_dynamic-update-slice_fusion.7
  264.3 2.1 fusion.42
  266.5 2.4 bitcast_dynamic-update-slice_fusion.6
  268.9 2.3 bitcast_dynamic-update-slice_fusion.5
  273.6 2.5 collective-permute-done.32
  277.1 4.6 copy-done.4
  281.7 13.4 %qkv_forward.1 = (bf16[512,3072]{1,0:T(8,128)(2,1)S(1)}, bf16[512,3072]{1,0:T(8,128)(2,1)S(1)}, f32[1,3072]{1,0:T(1,128)S(1)}, f32[48,3072]{1,0:T(8,128)S(1)}) custom-call(bf16[512,2048]{1,0:T(8,128)(2,1)S(1)} %fusion.1.h_ref, bf16[2048,3072]{1,0:T(8,128)(2,1)S(1)} %bitcast.557, bf16[48,2048]{1,0:T(8,128)(2,1)S(1)} %bitcast.558, f32[1,3072]{1,0:T(1,128)S(1)} %bitcast.571, ...), custom_call_target="tpu_custom_call" | custom-call | flops 6442450944 | bytes 22020096 | tf_op jit(solution)/shard_map/qkv_forward/pallas_call | solution.py:180
  298.2 8.9 %attend.1.u_ref = bf16[512,1024]{1,0:T(8,128)(2,1)S(1)} custom-call(bf16[512,3072]{1,0:T(8,128)(2,1)S(1)} %get-tuple-element.365.q_ref.k_ref.v_ref, bf16[512,3072]{1,0:T(8,128)(2,1)S(1)} %get-tuple-element.365.q_ref.k_ref.v_ref, bf16[512,3072]{1,0:T(8,128)(2,1)S(1)} %get-tuple-element.365.q_ref.k_ref.v_ref, f32[512,512]{1,0:T(8,128)S(1)} %and_select_fusion.bias_ref), custom_call_target="tpu_custom_call" | custom-call | flops 1073741824 | bytes 4194304 | tf_op jit(solution)/shard_map/attend/pallas_call | solution.py:244
  315.9 3.7 collective-permute-done.34.g_ref
  319.6 2.3 fusion.28
  321.9 2.3 fusion.31
  324.3 3.3 multiply_reduce_fusion
  328.3 2.3 fusion.18
  330.6 2.3 fusion.12
  339.3 24.1 %collective-permute-done.38.h_ref = bf16[256,2048]{1,0:T(8,128)(2,1)S(1)} collective-permute-done((bf16[256,2048]{1,0:T(8,128)(2,1)}, bf16[256,2048]{1,0:T(8,128)(2,1)S(1)}, u32[]{:S(2)}, u32[]{:S(2)}) %collective-permute-start.38) | collective-permute-done | bytes 1048608 | tf_op jit(solution)/shard_map/ppermute | solution.py:36
  367.1 31.2 %feed_forward_back.2 = (bf16[256,2048]{1,0:T(8,128)(2,1)}, bf16[256,2048]{1,0:T(8,128)(2,1)}, bf16[256,2048]{1,0:T(8,128)(2,1)}, bf16[256,2048]{1,0:T(8,128)(2,1...) custom-call(bf16[256,2048]{1,0:T(8,128)(2,1)} %copy-done.57, ...), custom_call_target="tpu_custom_call" | custom-call | flops 17716740096 | bytes 25690112 | tf_op jit(solution)/shard_map/feed_forward_back/pallas_call | solution.py:608
  399.0 2.2 collective-permute-done.49
  406.2 30.5 %feed_forward_back.3 = (bf16[256,2048]{1,0:T(8,128)(2,1)}, bf16[256,2048]{1,0:T(8,128)(2,1)}, bf16[256,2048]{1,0:T(8,128)(2,1)}, bf16[256,2048]{1,0:T(8,128)(2,1...) custom-call(bf16[256,2048]{1,0:T(8,128)(2,1)} %multiply_convert_fusi, ...), custom_call_target="tpu_custom_call" | custom-call | flops 17716740096 | bytes 25690112 | tf_op jit(solution)/shard_map/feed_forward_back/pallas_call | solution.py:608
  439.8 6.3 %middle_back.1 = (f32[256,2048]{1,0:T(8,128)}, bf16[256,2048]{1,0:T(8,128)(2,1)}, f32[1,2048]{1,0:T(1,128)}) custom-call(bf16[256,2048]{1,0:T(8,128)(2,1)} %get-tuple-element.398.near_ref, bf16[256,2048]{1,0:T(8,128)(2,1)} %collective-permute-done.52.pair_ref, bf16[256,2048]{1,0:T(8,128)(2,1)} %collective-permute-done.51.far_ref, ...), custom_call_target="tpu_custom_call" | custom-call | flops 10485760 | bytes 12582912 | tf_op jit(solution)/shard_map/middle_back/pallas_call | solution.py:282
  449.7 3.6 fusion.8
  453.4 2.9 add_convert_fusion.2.g_ref
  456.3 14.3 %attend_back_turn.1 = (bf16[3,512,1024]{2,1,0:T(8,128)(2,1)S(1)}, f32[3,1,1024]{2,1,0:T(1,128)S(1)}) custom-call(bf16[512,3072]{1,0:T(8,128)(2,1)} %copy-done.2, bf16[512,3072]{1,0:T(8,128)(2,1)} %copy-done.2, bf16[512,3072]{1,0:T(8,128)(2,1)} %copy-done.2, bf16[512,1024]{1,0:T(8,128)(2,1)S(1)} %add_convert_fusion.2.g_ref, ...), custom_call_target="tpu_custom_call" | custom-call | flops 2684354560 | bytes 10485760 | tf_op jit(solution)/shard_map/attend_back_turn/pallas_call | solution.py:318
  478.0 4.7 add_convert_fusion
  483.2 14.2 %qkv_back.1 = (bf16[512,2048]{1,0:T(8,128)(2,1)S(1)}, f32[4,48,512]{2,1,0:T(8,128)S(1)}, f32[2,48,512]{2,1,0:T(8,128)S(1)}) custom-call(bf16[3,512,1024]{2,1,0:T(8,128)(2,1)} %copy-done.29, bf16[2048,3072]{1,0:T(8,128)(2,1)} %bitcast.556, bf16[512,2048]{1,0:T(8,128)(2,1)S(1)} %fusion.1.h_ref, bf16[3,16,512]{2,1,0:T(8,128)(2,1)S(1)} %bitcast.573, ...), custom_call_target="tpu_custom_call" | custom-call | flops 6442450944 | bytes 12582912 | tf_op jit(solution)/shard_map/qkv_back/pallas_call | solution.py:392
  501.2 5.3 out_adapter.1
  506.6 3.6 feed_adapter.1
  511.3 5.1 all-to-all-start.1
  519.3 5.3 collective-permute-done.61
  525.1 5.4 collective-permute-done.62
  532.3 2.4 collective-permute-start.64
  539.8 6.2 %collective-permute-done.64 = bf16[48,512]{1,0:T(8,128)(2,1)S(1)} collective-permute-done((bf16[48,512]{1,0:T(8,128)(2,1)S(1)}, bf16[48,512]{1,0:T(8,128)(2,1)S(1)}, u32[]{:S(2)}, u32[]{:S(2)}) %collective-permute-start.64) | collective-permute-done | bytes 49184 | tf_op jit(solution)/shard_map/ppermute | solution.py:41
  553.6 5.3 collective-permute-done.72
  560.1 3.8 all-to-all-start.2
  566.8 4.4 collective-permute-done.73
  583.7 6.7 %all-to-all-done.2 = bf16[4,64,2048]{2,1,0:T(8,128)(2,1)S(1)} async-done(((bf16[4,64,2048]{2,1,0:T(8,128)(2,1)}), bf16[4,64,2048]{2,1,0:T(8,128)(2,1)S(1)}, u32[]{:S(2)}, u32[]{:S(2)}) %all-to-all-start.2) | async-done | bytes 1048608 | tf_op jit(solution)/shard_map/all_to_all | solution.py:1101
  (505 shorter events, 181.5 us)
Async XLA Ops:
  12.7 41.0 %collective-permute-start.6 = (bf16[2,64,4096]{2,1,0:T(8,128)(2,1)S(1)}, bf16[2,64,4096]{2,1,0:T(8,128)(2,1)}, u32[]{:S(2)}, u32[]{:S(2)}) collective-permute-start(bf16[2,64,4096]{2,1,0:T(8,128)(2,1)S(1)} %maximum_maximum_fusion), channel_id=1, source_target_pairs={{0,1},{1,2},{2,3},{3,0},{4,5},{5,6},{6,7},{7,4},{8,9},{9,10},{10,1... | collective-permute-start | bytes 3145736 | tf_op jit(solution)/shard_map/ppermute | solution.py:41
  15.3 38.7 %collective-permute-start.8 = (bf16[2,64,4096]{2,1,0:T(8,128)(2,1)S(1)}, bf16[2,64,4096]{2,1,0:T(8,128)(2,1)}, u32[]{:S(2)}, u32[]{:S(2)}) collective-permute-start(bf16[2,64,4096]{2,1,0:T(8,128)(2,1)S(1)} %maximum_maximum_fusion), channel_id=1, source_target_pairs={{0,16},{16,0},{1,17},{17,1},{2,18},{18,2},{3,19},{19,3},{4,20},{20... | collective-permute-start | bytes 3145736 | tf_op jit(solution)/shard_map/ppermute | solution.py:41
  28.2 26.5 %collective-permute-start.3 = (bf16[2,64,4224]{2,1,0:T(8,128)(2,1)}, bf16[2,64,4224]{2,1,0:T(8,128)(2,1)}, u32[]{:S(2)}, u32[]{:S(2)}) collective-permute-start(bf16[2,64,4224]{2,1,0:T(8,128)(2,1)} %get-tuple-element.235), channel_id=1, source_target_pairs={{0,4},{4,0},{1,5},{5,1},{2,6},{6,2},{3,7},{7,3},{8,12},{12,8},{9,1... | collective-permute-start | bytes 3244040 | tf_op jit(solution)/shard_map/ppermute | solution.py:36
  36.9 11.8 %collective-permute-start.1 = (f32[1,64]{1,0:T(1,128)S(1)}, f32[1,64]{1,0:T(1,128)S(1)}, u32[]{:S(2)}, u32[]{:S(2)}) collective-permute-start(f32[1,64]{1,0:T(1,128)S(1)} %bitcast.651), channel_id=1, source_target_pairs={{0,1},{1,2},{2,3},{3,0},{4,5},{5,6},{6,7},{7,4},{8,9},{9,10},{10,1... | collective-permute-start | bytes 776 | tf_op jit(solution)/shard_map/ppermute | solution.py:41
  48.7 26.1 %collective-permute-start.7 = (bf16[2,64,4096]{2,1,0:T(8,128)(2,1)S(1)}, bf16[2,64,4096]{2,1,0:T(8,128)(2,1)S(1)}, u32[]{:S(2)}, u32[]{:S(2)}) collective-permute-start(bf16[2,64,4096]{2,1,0:T(8,128)(2,1)S(1)} %maximum_maximum_fusion), channel_id=1, source_target_pairs={{0,8},{8,0},{1,9},{9,1},{2,10},{10,2},{3,11},{11,3},{4,12},{12,4},... | collective-permute-start | bytes 3145736 | tf_op jit(solution)/shard_map/ppermute | solution.py:36
  50.3 25.8 %collective-permute-start.2 = (f32[1,64]{1,0:T(1,128)S(1)}, f32[1,64]{1,0:T(1,128)S(1)}, u32[]{:S(2)}, u32[]{:S(2)}) collective-permute-start(f32[1,64]{1,0:T(1,128)S(1)} %collective-permute-done.1), channel_id=1, source_target_pairs={{0,1},{1,2},{2,3},{3,0},{4,5},{5,6},{6,7},{7,4},{8,9},{9,10},{10,1... | collective-permute-start | bytes 776 | tf_op jit(solution)/shard_map/ppermute | solution.py:41
  53.7 39.1 %collective-permute-start.10 = (bf16[2,64,4096]{2,1,0:T(8,128)(2,1)}, bf16[2,64,4096]{2,1,0:T(8,128)(2,1)}, u32[]{:S(2)}, u32[]{:S(2)}) collective-permute-start(bf16[2,64,4096]{2,1,0:T(8,128)(2,1)} %collective-permute-done.6), channel_id=1, source_target_pairs={{0,1},{1,2},{2,3},{3,0},{4,5},{5,6},{6,7},{7,4},{8,9},{9,10},{10,1... | collective-permute-start | bytes 3145736 | tf_op jit(solution)/shard_map/ppermute | solution.py:41
  54.0 43.4 %collective-permute-start.12 = (bf16[2,64,4096]{2,1,0:T(8,128)(2,1)}, bf16[2,64,4096]{2,1,0:T(8,128)(2,1)}, u32[]{:S(2)}, u32[]{:S(2)}) collective-permute-start(bf16[2,64,4096]{2,1,0:T(8,128)(2,1)} %collective-permute-done.6), channel_id=1, source_target_pairs={{0,16},{16,0},{1,17},{17,1},{2,18},{18,2},{3,19},{19,3},{4,20},{20... | collective-permute-start | bytes 3145736 | tf_op jit(solution)/shard_map/ppermute | solution.py:41
  54.8 42.6 %collective-permute-start.11 = (bf16[2,64,4096]{2,1,0:T(8,128)(2,1)}, bf16[2,64,4096]{2,1,0:T(8,128)(2,1)}, u32[]{:S(2)}, u32[]{:S(2)}) collective-permute-start(bf16[2,64,4096]{2,1,0:T(8,128)(2,1)} %collective-permute-done.8), channel_id=1, source_target_pairs={{0,8},{8,0},{1,9},{9,1},{2,10},{10,2},{3,11},{11,3},{4,12},{12,4},... | collective-permute-start | bytes 3145736 | tf_op jit(solution)/shard_map/ppermute | solution.py:36
  76.1 15.1 %collective-permute-start.9 = (f32[1,64]{1,0:T(1,128)S(1)}, f32[1,64]{1,0:T(1,128)S(1)}, u32[]{:S(2)}, u32[]{:S(2)}) collective-permute-start(f32[1,64]{1,0:T(1,128)S(1)} %collective-permute-done.2), channel_id=1, source_target_pairs={{0,1},{1,2},{2,3},{3,0},{4,5},{5,6},{6,7},{7,4},{8,9},{9,10},{10,1... | collective-permute-start | bytes 776 | tf_op jit(solution)/shard_map/ppermute | solution.py:41
  77.7 34.6 %collective-permute-start.15 = (bf16[2,64,4224]{2,1,0:T(8,128)(2,1)}, bf16[2,64,4224]{2,1,0:T(8,128)(2,1)}, u32[]{:S(2)}, u32[]{:S(2)}) collective-permute-start(bf16[2,64,4224]{2,1,0:T(8,128)(2,1)} %pad_maximum_fusion.2), channel_id=1, source_target_pairs={{0,16},{16,0},{1,17},{17,1},{2,18},{18,2},{3,19},{19,3},{4,20},{20... | collective-permute-start | bytes 3244040 | tf_op jit(solution)/shard_map/ppermute | solution.py:41
  78.2 177.2 %all-to-all-start = ((bf16[4,128,2048]{2,1,0:T(8,128)(2,1)}), bf16[4,128,2048]{2,1,0:T(8,128)(2,1)S(1)}, u32[]{:S(2)}, u32[]{:S(2)}) async-start(bf16[4,128,2048]{2,1,0:T(8,128)(2,1)} %pad_maximum_fusion), calls=%async_computation | async-start | bytes 4194304 | tf_op jit(solution)/shard_map/all_to_all | solution.py:907
  91.2 29.3 %collective-permute-start.14 = (bf16[2,64,4224]{2,1,0:T(8,128)(2,1)}, bf16[2,64,4224]{2,1,0:T(8,128)(2,1)}, u32[]{:S(2)}, u32[]{:S(2)}) collective-permute-start(bf16[2,64,4224]{2,1,0:T(8,128)(2,1)} %pad_maximum_fusion.3), channel_id=1, source_target_pairs={{0,8},{8,0},{1,9},{9,1},{2,10},{10,2},{3,11},{11,3},{4,12},{12,4},... | collective-permute-start | bytes 3244040 | tf_op jit(solution)/shard_map/ppermute | solution.py:36
  97.4 48.1 %collective-permute-start.17 = (bf16[2,64,4096]{2,1,0:T(8,128)(2,1)}, bf16[2,64,4096]{2,1,0:T(8,128)(2,1)}, u32[]{:S(2)}, u32[]{:S(2)}) collective-permute-start(bf16[2,64,4096]{2,1,0:T(8,128)(2,1)} %collective-permute-done.10), channel_id=1, source_target_pairs={{0,1},{1,2},{2,3},{3,0},{4,5},{5,6},{6,7},{7,4},{8,9},{9,10},{10,1... | collective-permute-start | bytes 3145736 | tf_op jit(solution)/shard_map/ppermute | solution.py:41
  98.9 44.9 %collective-permute-start.19 = (bf16[2,64,4096]{2,1,0:T(8,128)(2,1)}, bf16[2,64,4096]{2,1,0:T(8,128)(2,1)S(1)}, u32[]{:S(2)}, u32[]{:S(2)}) collective-permute-start(bf16[2,64,4096]{2,1,0:T(8,128)(2,1)} %collective-permute-done.10), channel_id=1, source_target_pairs={{0,16},{16,0},{1,17},{17,1},{2,18},{18,2},{3,19},{19,3},{4,20},{20... | collective-permute-start | bytes 3145736 | tf_op jit(solution)/shard_map/ppermute | solution.py:41
  99.4 11.3 %collective-permute-start.13 = (f32[4,64]{1,0:T(4,128)S(1)}, f32[4,64]{1,0:T(4,128)S(1)}, u32[]{:S(2)}, u32[]{:S(2)}) collective-permute-start(f32[4,64]{1,0:T(4,128)S(1)} %dynamic_update_slice.186), channel_id=1, source_target_pairs={{0,4},{4,0},{1,5},{5,1},{2,6},{6,2},{3,7},{7,3},{8,12},{12,8},{9,1... | collective-permute-start | bytes 3080 | tf_op jit(solution)/shard_map/ppermute | solution.py:36
  110.7 34.7 %collective-permute-start.18 = (bf16[2,64,4096]{2,1,0:T(8,128)(2,1)}, bf16[2,64,4096]{2,1,0:T(8,128)(2,1)S(1)}, u32[]{:S(2)}, u32[]{:S(2)}) collective-permute-start(bf16[2,64,4096]{2,1,0:T(8,128)(2,1)} %collective-permute-done.6), channel_id=1, source_target_pairs={{0,8},{8,0},{1,9},{9,1},{2,10},{10,2},{3,11},{11,3},{4,12},{12,4},... | collective-permute-start | bytes 3145736 | tf_op jit(solution)/shard_map/ppermute | solution.py:36
  120.5 54.2 %collective-permute-start.26 = (bf16[2,64,4224]{2,1,0:T(8,128)(2,1)}, bf16[2,64,4224]{2,1,0:T(8,128)(2,1)}, u32[]{:S(2)}, u32[]{:S(2)}) collective-permute-start(bf16[2,64,4224]{2,1,0:T(8,128)(2,1)} %collective-permute-done.14), channel_id=1, source_target_pairs={{0,16},{16,0},{1,17},{17,1},{2,18},{18,2},{3,19},{19,3},{4,20},{20... | collective-permute-start | bytes 3244040 | tf_op jit(solution)/shard_map/ppermute | solution.py:41
  121.0 21.2 %collective-permute-start.16 = (f32[8,64]{1,0:T(8,128)S(1)}, f32[8,64]{1,0:T(8,128)S(1)}, u32[]{:S(2)}, u32[]{:S(2)}) collective-permute-start(f32[8,64]{1,0:T(8,128)S(1)} %bitcast.648), channel_id=1, source_target_pairs={{0,8},{8,0},{1,9},{9,1},{2,10},{10,2},{3,11},{11,3},{4,12},{12,4},... | collective-permute-start | bytes 6152 | tf_op jit(solution)/shard_map/ppermute | solution.py:36
  142.2 32.5 %collective-permute-start.24 = (bf16[2,64,4224]{2,1,0:T(8,128)(2,1)}, bf16[2,64,4224]{2,1,0:T(8,128)(2,1)}, u32[]{:S(2)}, u32[]{:S(2)}) collective-permute-start(bf16[2,64,4224]{2,1,0:T(8,128)(2,1)} %pad_maximum_fusion.2), channel_id=1, source_target_pairs={{0,1},{1,2},{2,3},{3,0},{4,5},{5,6},{6,7},{7,4},{8,9},{9,10},{10,1... | collective-permute-start | bytes 3244040 | tf_op jit(solution)/shard_map/ppermute | solution.py:41
  143.9 29.4 %collective-permute-start.25 = (bf16[2,64,4096]{2,1,0:T(8,128)(2,1)}, bf16[2,64,4096]{2,1,0:T(8,128)(2,1)}, u32[]{:S(2)}, u32[]{:S(2)}) collective-permute-start(bf16[2,64,4096]{2,1,0:T(8,128)(2,1)} %collective-permute-done.12), channel_id=1, source_target_pairs={{0,8},{8,0},{1,9},{9,1},{2,10},{10,2},{3,11},{11,3},{4,12},{12,4},... | collective-permute-start | bytes 3145736 | tf_op jit(solution)/shard_map/ppermute | solution.py:36
  145.5 41.9 %collective-permute-start.22 = (bf16[2,64,4096]{2,1,0:T(8,128)(2,1)}, bf16[2,64,4096]{2,1,0:T(8,128)(2,1)}, u32[]{:S(2)}, u32[]{:S(2)}) collective-permute-start(bf16[2,64,4096]{2,1,0:T(8,128)(2,1)} %collective-permute-done.17), channel_id=1, source_target_pairs={{0,16},{16,0},{1,17},{17,1},{2,18},{18,2},{3,19},{19,3},{4,20},{20... | collective-permute-start | bytes 3145736 | tf_op jit(solution)/shard_map/ppermute | solution.py:41
  145.9 24.6 %collective-permute-start.23 = (f32[16,64]{1,0:T(8,128)S(1)}, f32[16,64]{1,0:T(8,128)S(1)}, u32[]{:S(2)}, u32[]{:S(2)}) collective-permute-start(f32[16,64]{1,0:T(8,128)S(1)} %maximum_bitcast_fusion.1), channel_id=1, source_target_pairs={{0,16},{16,0},{1,17},{17,1},{2,18},{18,2},{3,19},{19,3},{4,20},{20... | collective-permute-start | bytes 12296 | tf_op jit(solution)/shard_map/ppermute | solution.py:41
  170.5 29.1 %collective-permute-start.20 = (bf16[2,64,4224]{2,1,0:T(8,128)(2,1)}, bf16[2,64,4224]{2,1,0:T(8,128)(2,1)}, u32[]{:S(2)}, u32[]{:S(2)}) collective-permute-start(bf16[2,64,4224]{2,1,0:T(8,128)(2,1)} %collective-permute-done.14), channel_id=1, source_target_pairs={{0,1},{1,2},{2,3},{3,0},{4,5},{5,6},{6,7},{7,4},{8,9},{9,10},{10,1... | collective-permute-start | bytes 3244040 | tf_op jit(solution)/shard_map/ppermute | solution.py:41
  173.3 26.3 %collective-permute-start.21 = (bf16[2,64,4096]{2,1,0:T(8,128)(2,1)}, bf16[2,64,4096]{2,1,0:T(8,128)(2,1)S(1)}, u32[]{:S(2)}, u32[]{:S(2)}) collective-permute-start(bf16[2,64,4096]{2,1,0:T(8,128)(2,1)} %collective-permute-done.10), channel_id=1, source_target_pairs={{0,8},{8,0},{1,9},{9,1},{2,10},{10,2},{3,11},{11,3},{4,12},{12,4},... | collective-permute-start | bytes 3145736 | tf_op jit(solution)/shard_map/ppermute | solution.py:36
  174.8 80.6 %collective-permute-start.27 = (bf16[2,64,4224]{2,1,0:T(8,128)(2,1)}, bf16[2,64,4224]{2,1,0:T(8,128)(2,1)}, u32[]{:S(2)}, u32[]{:S(2)}) collective-permute-start(bf16[2,64,4224]{2,1,0:T(8,128)(2,1)} %collective-permute-done.24), channel_id=1, source_target_pairs={{0,1},{1,2},{2,3},{3,0},{4,5},{5,6},{6,7},{7,4},{8,9},{9,10},{10,1... | collective-permute-start | bytes 3244040 | tf_op jit(solution)/shard_map/ppermute | solution.py:41
  177.2 78.1 %collective-permute-start.29 = (bf16[2,64,4224]{2,1,0:T(8,128)(2,1)}, bf16[2,64,4224]{2,1,0:T(8,128)(2,1)}, u32[]{:S(2)}, u32[]{:S(2)}) collective-permute-start(bf16[2,64,4224]{2,1,0:T(8,128)(2,1)} %collective-permute-done.24), channel_id=1, source_target_pairs={{0,16},{16,0},{1,17},{17,1},{2,18},{18,2},{3,19},{19,3},{4,20},{20... | collective-permute-start | bytes 3244040 | tf_op jit(solution)/shard_map/ppermute | solution.py:41
  187.3 31.7 %collective-permute-start.28 = (bf16[2,64,4096]{2,1,0:T(8,128)(2,1)S(1)}, bf16[2,64,4096]{2,1,0:T(8,128)(2,1)S(1)}, u32[]{:S(2)}, u32[]{:S(2)}) collective-permute-start(bf16[2,64,4096]{2,1,0:T(8,128)(2,1)S(1)} %copy-done.41), channel_id=1, source_target_pairs={{0,8},{8,0},{1,9},{9,1},{2,10},{10,2},{3,11},{11,3},{4,12},{12,4},... | collective-permute-start | bytes 3145736 | tf_op jit(solution)/shard_map/ppermute | solution.py:36
  199.6 66.8 %collective-permute-start.41 = (bf16[2,64,4224]{2,1,0:T(8,128)(2,1)}, bf16[2,64,4224]{2,1,0:T(8,128)(2,1)}, u32[]{:S(2)}, u32[]{:S(2)}) collective-permute-start(bf16[2,64,4224]{2,1,0:T(8,128)(2,1)} %collective-permute-done.20), channel_id=1, source_target_pairs={{0,1},{1,2},{2,3},{3,0},{4,5},{5,6},{6,7},{7,4},{8,9},{9,10},{10,1... | collective-permute-start | bytes 3244040 | tf_op jit(solution)/shard_map/ppermute | solution.py:41
  202.1 64.3 %collective-permute-start.42 = (bf16[2,64,4224]{2,1,0:T(8,128)(2,1)}, bf16[2,64,4224]{2,1,0:T(8,128)(2,1)}, u32[]{:S(2)}, u32[]{:S(2)}) collective-permute-start(bf16[2,64,4224]{2,1,0:T(8,128)(2,1)} %collective-permute-done.20), channel_id=1, source_target_pairs={{0,16},{16,0},{1,17},{17,1},{2,18},{18,2},{3,19},{19,3},{4,20},{20... | collective-permute-start | bytes 3244040 | tf_op jit(solution)/shard_map/ppermute | solution.py:41
  219.0 42.0 %collective-permute-start.31 = (bf16[2,64,4096]{2,1,0:T(8,128)(2,1)}, bf16[2,64,4096]{2,1,0:T(8,128)(2,1)}, u32[]{:S(2)}, u32[]{:S(2)}) collective-permute-start(bf16[2,64,4096]{2,1,0:T(8,128)(2,1)} %collective-permute-done.17), channel_id=1, source_target_pairs={{0,8},{8,0},{1,9},{9,1},{2,10},{10,2},{3,11},{11,3},{4,12},{12,4},... | collective-permute-start | bytes 3145736 | tf_op jit(solution)/shard_map/ppermute | solution.py:36
  255.4 54.1 %collective-permute-start.45 = (bf16[2,64,4224]{2,1,0:T(8,128)(2,1)}, bf16[2,64,4224]{2,1,0:T(8,128)(2,1)S(1)}, u32[]{:S(2)}, u32[]{:S(2)}) collective-permute-start(bf16[2,64,4224]{2,1,0:T(8,128)(2,1)} %collective-permute-done.27), channel_id=1, source_target_pairs={{0,1},{1,2},{2,3},{3,0},{4,5},{5,6},{6,7},{7,4},{8,9},{9,10},{10,1... | collective-permute-start | bytes 3244040 | tf_op jit(solution)/shard_map/ppermute | solution.py:41
  255.4 54.1 %collective-permute-start.46 = (bf16[2,64,4224]{2,1,0:T(8,128)(2,1)}, bf16[2,64,4224]{2,1,0:T(8,128)(2,1)S(1)}, u32[]{:S(2)}, u32[]{:S(2)}) collective-permute-start(bf16[2,64,4224]{2,1,0:T(8,128)(2,1)} %collective-permute-done.27), channel_id=1, source_target_pairs={{0,16},{16,0},{1,17},{17,1},{2,18},{18,2},{3,19},{19,3},{4,20},{20... | collective-permute-start | bytes 3244040 | tf_op jit(solution)/shard_map/ppermute | solution.py:41
  261.0 15.1 %collective-permute-start.32 = (bf16[2,64,4096]{2,1,0:T(8,128)(2,1)}, bf16[2,64,4096]{2,1,0:T(8,128)(2,1)S(1)}, u32[]{:S(2)}, u32[]{:S(2)}) collective-permute-start(bf16[2,64,4096]{2,1,0:T(8,128)(2,1)} %collective-permute-done.22), channel_id=1, source_target_pairs={{0,8},{8,0},{1,9},{9,1},{2,10},{10,2},{3,11},{11,3},{4,12},{12,4},... | collective-permute-start | bytes 3145736 | tf_op jit(solution)/shard_map/ppermute | solution.py:36
  266.4 46.9 %collective-permute-start.43 = (bf16[2,64,4224]{2,1,0:T(8,128)(2,1)}, bf16[2,64,4224]{2,1,0:T(8,128)(2,1)S(1)}, u32[]{:S(2)}, u32[]{:S(2)}) collective-permute-start(bf16[2,64,4224]{2,1,0:T(8,128)(2,1)} %collective-permute-done.41), channel_id=1, source_target_pairs={{0,1},{1,2},{2,3},{3,0},{4,5},{5,6},{6,7},{7,4},{8,9},{9,10},{10,1... | collective-permute-start | bytes 3244040 | tf_op jit(solution)/shard_map/ppermute | solution.py:41
  271.2 42.2 %collective-permute-start.44 = (bf16[2,64,4224]{2,1,0:T(8,128)(2,1)}, bf16[2,64,4224]{2,1,0:T(8,128)(2,1)S(1)}, u32[]{:S(2)}, u32[]{:S(2)}) collective-permute-start(bf16[2,64,4224]{2,1,0:T(8,128)(2,1)} %collective-permute-done.41), channel_id=1, source_target_pairs={{0,16},{16,0},{1,17},{17,1},{2,18},{18,2},{3,19},{19,3},{4,20},{20... | collective-permute-start | bytes 3244040 | tf_op jit(solution)/shard_map/ppermute | solution.py:41
  296.8 22.9 %collective-permute-start.34 = (bf16[256,2048]{1,0:T(8,128)(2,1)S(1)}, bf16[256,2048]{1,0:T(8,128)(2,1)}, u32[]{:S(2)}, u32[]{:S(2)}) collective-permute-start(bf16[256,2048]{1,0:T(8,128)(2,1)S(1)} %bitcast.578), channel_id=1, source_target_pairs={{0,8},{8,0},{1,9},{9,1},{2,10},{10,2},{3,11},{11,3},{4,12},{12,4},... | collective-permute-start | bytes 3145736 | tf_op jit(solution)/shard_map/ppermute | solution.py:36
  309.5 28.7 %collective-permute-start.47 = (bf16[2,64,4224]{2,1,0:T(8,128)(2,1)S(1)}, bf16[2,64,4224]{2,1,0:T(8,128)(2,1)S(1)}, u32[]{:S(2)}, u32[]{:S(2)}) collective-permute-start(bf16[2,64,4224]{2,1,0:T(8,128)(2,1)S(1)} %collective-permute-done.45), channel_id=1, source_target_pairs={{0,16},{16,0},{1,17},{17,1},{2,18},{18,2},{3,19},{19,3},{4,20},{20... | collective-permute-start | bytes 3244040 | tf_op jit(solution)/shard_map/ppermute | solution.py:41
  313.3 50.1 %collective-permute-start.48 = (bf16[2,64,4224]{2,1,0:T(8,128)(2,1)S(1)}, bf16[2,64,4224]{2,1,0:T(8,128)(2,1)S(1)}, u32[]{:S(2)}, u32[]{:S(2)}) collective-permute-start(bf16[2,64,4224]{2,1,0:T(8,128)(2,1)S(1)} %collective-permute-done.43), channel_id=1, source_target_pairs={{0,16},{16,0},{1,17},{17,1},{2,18},{18,2},{3,19},{19,3},{4,20},{20... | collective-permute-start | bytes 3244040 | tf_op jit(solution)/shard_map/ppermute | solution.py:41
  327.6 6.8 %collective-permute-start.35 = (bf16[256,2048]{1,0:T(8,128)(2,1)S(1)}, bf16[256,2048]{1,0:T(8,128)(2,1)S(1)}, u32[]{:S(2)}, u32[]{:S(2)}) collective-permute-start(bf16[256,2048]{1,0:T(8,128)(2,1)S(1)} %pad_maximum_fusion.6), channel_id=1, source_target_pairs={{0,4},{4,0},{1,5},{5,1},{2,6},{6,2},{3,7},{7,3},{8,12},{12,8},{9,1... | collective-permute-start | bytes 3145736 | tf_op jit(solution)/shard_map/ppermute | solution.py:36
  332.9 34.1 %collective-permute-start.40 = (bf16[256,2048]{1,0:T(8,128)(2,1)}, bf16[256,2048]{1,0:T(8,128)(2,1)}, u32[]{:S(2)}, u32[]{:S(2)}) collective-permute-start(bf16[256,2048]{1,0:T(8,128)(2,1)} %collective-permute-done.34.g_ref), channel_id=1, source_target_pairs={{0,4},{4,0},{1,5},{5,1},{2,6},{6,2},{3,7},{7,3},{8,12},{12,8},{9,1... | collective-permute-start | bytes 3145736 | tf_op jit(solution)/shard_map/ppermute | solution.py:36
  337.6 25.8 %collective-permute-start.38 = (bf16[256,2048]{1,0:T(8,128)(2,1)}, bf16[256,2048]{1,0:T(8,128)(2,1)S(1)}, u32[]{:S(2)}, u32[]{:S(2)}) collective-permute-start(bf16[256,2048]{1,0:T(8,128)(2,1)} %multiply_convert_fusion.h_ref), channel_id=1, source_target_pairs={{0,8},{8,0},{1,9},{9,1},{2,10},{10,2},{3,11},{11,3},{4,12},{12,4},... | collective-permute-start | bytes 3145736 | tf_op jit(solution)/shard_map/ppermute | solution.py:36
  398.5 5.7 collective-permute-start.37
  398.8 5.9 collective-permute-start.50
  404.2 32.5 %collective-permute-start.51 = (bf16[256,2048]{1,0:T(8,128)(2,1)S(1)}, bf16[256,2048]{1,0:T(8,128)(2,1)}, u32[]{:S(2)}, u32[]{:S(2)}) collective-permute-start(bf16[256,2048]{1,0:T(8,128)(2,1)S(1)} %add_convert_fusion.3), channel_id=1, source_target_pairs={{0,8},{8,0},{1,9},{9,1},{2,10},{10,2},{3,11},{11,3},{4,12},{12,4},... | collective-permute-start | bytes 3145736 | tf_op jit(solution)/shard_map/ppermute | solution.py:36
  436.9 9.4 %collective-permute-start.54 = (bf16[256,2048]{1,0:T(8,128)(2,1)}, bf16[256,2048]{1,0:T(8,128)(2,1)}, u32[]{:S(2)}, u32[]{:S(2)}) collective-permute-start(bf16[256,2048]{1,0:T(8,128)(2,1)} %get-tuple-element.406), channel_id=1, source_target_pairs={{0,4},{4,0},{1,5},{5,1},{2,6},{6,2},{3,7},{7,3},{8,12},{12,8},{9,1... | collective-permute-start | bytes 3145736 | tf_op jit(solution)/shard_map/ppermute | solution.py:36
  448.3 25.5 %collective-permute-start.55 = (bf16[256,2048]{1,0:T(8,128)(2,1)S(1)}, bf16[256,2048]{1,0:T(8,128)(2,1)}, u32[]{:S(2)}, u32[]{:S(2)}) collective-permute-start(bf16[256,2048]{1,0:T(8,128)(2,1)S(1)} %add_convert_fusion.1), channel_id=1, source_target_pairs={{0,8},{8,0},{1,9},{9,1},{2,10},{10,2},{3,11},{11,3},{4,12},{12,4},... | collective-permute-start | bytes 3145736 | tf_op jit(solution)/shard_map/ppermute | solution.py:36
  482.8 17.2 %collective-permute-start.58 = (f32[1,2048]{1,0:T(1,128)S(1)}, f32[1,2048]{1,0:T(1,128)S(1)}, u32[]{:S(2)}, u32[]{:S(2)}) collective-permute-start(f32[1,2048]{1,0:T(1,128)S(1)} %div.65.cdm_ref), channel_id=1, source_target_pairs={{0,4},{4,0},{1,5},{5,1},{2,6},{6,2},{3,7},{7,3},{8,12},{12,8},{9,1... | collective-permute-start | bytes 24584 | tf_op jit(solution)/shard_map/ppermute | solution.py:36
  499.8 19.0 %collective-permute-start.70 = (bf16[256,2048]{1,0:T(8,128)(2,1)}, bf16[256,2048]{1,0:T(8,128)(2,1)S(1)}, u32[]{:S(2)}, u32[]{:S(2)}) collective-permute-start(bf16[256,2048]{1,0:T(8,128)(2,1)} %slice.494), channel_id=1, source_target_pairs={{0,4},{4,0},{1,5},{5,1},{2,6},{6,2},{3,7},{7,3},{8,12},{12,8},{9,1... | collective-permute-start | bytes 3145736 | tf_op jit(solution)/shard_map/ppermute | solution.py:36
  499.9 6.5 %collective-permute-start.59 = (f32[1,2048]{1,0:T(1,128)S(1)}, f32[1,2048]{1,0:T(1,128)S(1)}, u32[]{:S(2)}, u32[]{:S(2)}) collective-permute-start(f32[1,2048]{1,0:T(1,128)S(1)} %add.663), channel_id=1, source_target_pairs={{0,8},{8,0},{1,9},{9,1},{2,10},{10,2},{3,11},{11,3},{4,12},{12,4},... | collective-permute-start | bytes 24584 | tf_op jit(solution)/shard_map/ppermute | solution.py:36
  510.3 6.0 %collective-permute-start.60 = (bf16[256,512]{1,0:T(8,128)(2,1)S(1)}, bf16[256,512]{1,0:T(8,128)(2,1)S(1)}, u32[]{:S(2)}, u32[]{:S(2)}) collective-permute-start(bf16[256,512]{1,0:T(8,128)(2,1)S(1)} %fusion.74), channel_id=1, source_target_pairs={{0,4},{4,0},{1,5},{5,1},{2,6},{6,2},{3,7},{7,3},{8,12},{12,8},{9,1... | collective-permute-start | bytes 786440 | tf_op jit(solution)/shard_map/ppermute | solution.py:36
  511.3 34.7 %all-to-all-start.1 = ((bf16[4,64,2048]{2,1,0:T(8,128)(2,1)}), bf16[4,64,2048]{2,1,0:T(8,128)(2,1)S(1)}, u32[]{:S(2)}, u32[]{:S(2)}) async-start(bf16[4,64,2048]{2,1,0:T(8,128)(2,1)} %bitcast.182), calls=%async_computation.1 | async-start | bytes 2097152 | tf_op jit(solution)/shard_map/all_to_all | solution.py:1101
  517.7 6.8 %collective-permute-start.61 = (bf16[200,512]{1,0:T(8,128)(2,1)S(1)}, bf16[200,512]{1,0:T(8,128)(2,1)S(1)}, u32[]{:S(2)}, u32[]{:S(2)}) collective-permute-start(bf16[200,512]{1,0:T(8,128)(2,1)S(1)} %fusion.91), channel_id=1, source_target_pairs={{0,8},{8,0},{1,9},{9,1},{2,10},{10,2},{3,11},{11,3},{4,12},{12,4},... | collective-permute-start | bytes 614408 | tf_op jit(solution)/shard_map/ppermute | solution.py:36
  524.7 5.8 collective-permute-start.62
  530.6 9.2 %collective-permute-start.63 = (bf16[48,512]{1,0:T(8,128)(2,1)S(1)}, bf16[48,512]{1,0:T(8,128)(2,1)S(1)}, u32[]{:S(2)}, u32[]{:S(2)}) collective-permute-start(bf16[48,512]{1,0:T(8,128)(2,1)S(1)} %get-tuple-element.493), channel_id=1, source_target_pairs={{0,1},{1,2},{2,3},{3,0},{4,5},{5,6},{6,7},{7,4},{8,9},{9,10},{10,1... | collective-permute-start | bytes 147464 | tf_op jit(solution)/shard_map/ppermute | solution.py:41
  532.3 13.6 %collective-permute-start.64 = (bf16[48,512]{1,0:T(8,128)(2,1)S(1)}, bf16[48,512]{1,0:T(8,128)(2,1)S(1)}, u32[]{:S(2)}, u32[]{:S(2)}) collective-permute-start(bf16[48,512]{1,0:T(8,128)(2,1)S(1)} %get-tuple-element.495), channel_id=1, source_target_pairs={{0,2},{1,3},{2,0},{3,1},{4,6},{5,7},{6,4},{7,5},{8,10},{9,11},{10,... | collective-permute-start | bytes 147464 | tf_op jit(solution)/shard_map/ppermute | solution.py:41
  534.7 11.3 %collective-permute-start.65 = (bf16[48,512]{1,0:T(8,128)(2,1)S(1)}, bf16[48,512]{1,0:T(8,128)(2,1)S(1)}, u32[]{:S(2)}, u32[]{:S(2)}) collective-permute-start(bf16[48,512]{1,0:T(8,128)(2,1)S(1)} %get-tuple-element.494), channel_id=1, source_target_pairs={{0,3},{1,0},{2,1},{3,2},{4,7},{5,4},{6,5},{7,6},{8,11},{9,8},{10,9... | collective-permute-start | bytes 147464 | tf_op jit(solution)/shard_map/ppermute | solution.py:41
  546.0 6.0 %collective-permute-start.67 = (bf16[48,512]{1,0:T(8,128)(2,1)S(1)}, bf16[48,512]{1,0:T(8,128)(2,1)S(1)}, u32[]{:S(2)}, u32[]{:S(2)}) collective-permute-start(bf16[48,512]{1,0:T(8,128)(2,1)S(1)} %fusion.95), channel_id=1, source_target_pairs={{0,1},{1,2},{2,3},{3,0},{4,5},{5,6},{6,7},{7,4},{8,9},{9,10},{10,1... | collective-permute-start | bytes 147464 | tf_op jit(solution)/shard_map/ppermute | solution.py:41
  547.2 6.0 %collective-permute-start.68 = (bf16[48,512]{1,0:T(8,128)(2,1)S(1)}, bf16[48,512]{1,0:T(8,128)(2,1)S(1)}, u32[]{:S(2)}, u32[]{:S(2)}) collective-permute-start(bf16[48,512]{1,0:T(8,128)(2,1)S(1)} %fusion.95), channel_id=1, source_target_pairs={{0,2},{1,3},{2,0},{3,1},{4,6},{5,7},{6,4},{7,5},{8,10},{9,11},{10,... | collective-permute-start | bytes 147464 | tf_op jit(solution)/shard_map/ppermute | solution.py:41
  559.0 6.1 %collective-permute-start.76 = (bf16[168,512]{1,0:T(8,128)(2,1)S(1)}, bf16[168,512]{1,0:T(8,128)(2,1)}, u32[]{:S(2)}, u32[]{:S(2)}) collective-permute-start(bf16[168,512]{1,0:T(8,128)(2,1)S(1)} %slice.615), channel_id=1, source_target_pairs={{0,8},{8,0},{1,9},{9,1},{2,10},{10,2},{3,11},{11,3},{4,12},{12,4},... | collective-permute-start | bytes 516104 | tf_op jit(solution)/shard_map/ppermute | solution.py:36
  560.0 12.6 %collective-permute-start.66 = (bf16[2,1,64,2048]{3,2,0,1:T(8,128)(2,1)S(1)}, bf16[2,1,64,2048]{3,2,0,1:T(8,128)(2,1)}, u32[]{:S(2)}, u32[]{:S(2)}) collective-permute-start(bf16[2,1,64,2048]{3,2,0,1:T(8,128)(2,1)S(1)} %dynamic-slice_bitcast_fusion.1), channel_id=1, source_target_pairs={{0,4},{4,0},{1,5},{5,1},{2,6},{6,2},{3,7},{7,3},{8,12},{12,8},{9,1... | collective-permute-start | bytes 1572872 | tf_op jit(solution)/shard_map/ppermute | solution.py:36
  560.1 30.2 %all-to-all-start.2 = ((bf16[4,64,2048]{2,1,0:T(8,128)(2,1)}), bf16[4,64,2048]{2,1,0:T(8,128)(2,1)S(1)}, u32[]{:S(2)}, u32[]{:S(2)}) async-start(bf16[4,64,2048]{2,1,0:T(8,128)(2,1)} %bitcast.194), calls=%async_computation.2 | async-start | bytes 2097152 | tf_op jit(solution)/shard_map/all_to_all | solution.py:1101
  564.0 7.3 %collective-permute-start.73 = (bf16[200,512]{1,0:T(8,128)(2,1)S(1)}, bf16[200,512]{1,0:T(8,128)(2,1)S(1)}, u32[]{:S(2)}, u32[]{:S(2)}) collective-permute-start(bf16[200,512]{1,0:T(8,128)(2,1)S(1)} %slice.586), channel_id=1, source_target_pairs={{0,8},{8,0},{1,9},{9,1},{2,10},{10,2},{3,11},{11,3},{4,12},{12,4},... | collective-permute-start | bytes 614408 | tf_op jit(solution)/shard_map/ppermute | solution.py:36
  566.8 14.9 %collective-permute-start.77 = (bf16[2,168,512]{2,1,0:T(8,128)(2,1)}, bf16[2,168,512]{2,1,0:T(8,128)(2,1)}, u32[]{:S(2)}, u32[]{:S(2)}) collective-permute-start(bf16[2,168,512]{2,1,0:T(8,128)(2,1)} %pad_maximum_fusion.18), channel_id=1, source_target_pairs={{0,4},{4,0},{1,5},{5,1},{2,6},{6,2},{3,7},{7,3},{8,12},{12,8},{9,1... | collective-permute-start | bytes 1032200 | tf_op jit(solution)/shard_map/ppermute | solution.py:36
  (81 other events, 706.4 us)
